TPU v7x, 32 devices: a whole 2x2x4 slice. The times are simulated.
32 devices in a mesh: gx: 8 (over z, y), gy: 4 (over x, core).
Axes of the slice: x: 2, y: 2, z: 4, core: 2. Of those that a mesh axis runs over, the one named last changes fastest.
Arguments:
- positions: float32 [3, 8, 4, 4, 256], P(None, 'gx', 'gy'), as said below
- counts: int32 [8, 4, 4], P('gx', 'gy'), may hold values from 128 to 256, as said below
- targets: float32 [3, 8, 4, 4, 256], P(None, 'gx', 'gy')
- landmark_index: int32 [8, 4, 4], replicated, may hold values from 0 to 1023, as said below
- coarse_matrix: float32 [128, 128], P('gy', 'gx'), as said below
Outputs:
- solution: float32 [3, 8, 4, 4, 256], P(None, 'gx', 'gy')
- residual: float32 [3, 8, 4, 4, 256], P(None, 'gx', 'gy')
Inputs may be any that keep to these rules, and one draw needn't show every extreme that they name: `counts`: some cell holds all 256 points live. `landmark_index`: the 4 entries of a column name different live points of that column. `positions`: each point lies inside its cell: x in [i, i + 1), y in [j, j + 1), z in [layer, layer + 1). `coarse_matrix`: gram is symmetric positive definite.
All inputs are finite; a program needn't handle non-finite values.
Results may differ from a plain program's by a relative error of at most 0.0003.
Values sent between devices are 32-bit elements; how exact they have to be, the bound alone decides.
No kernel may reach another device: no remote copies, remote signals or barrier semaphores. Data moves between devices by JAX's collectives and lax.ppermute only.
A program may use at most 64 MiB of HBM per device.

v0:
```python
import jax
import jax.numpy as jnp
from jax import lax
from jax.sharding import PartitionSpec as P

ITERS = 2


RIDGE_WEIGHT = 2.0
HIGHEST_PRECISION = lax.Precision.HIGHEST


def with_halo(x, sides, width):
    for axis, dim in sides:
        peers, length = (lax.axis_size(axis), x.shape[dim])
        up = [(i, (i + 1) % peers) for i in range(peers - 1)]
        down = [(j, i) for i, j in up]
        last = lax.slice_in_dim(x, length - width, length, axis=dim)
        leading = lax.slice_in_dim(x, 0, width, axis=dim)
        before = lax.ppermute(last, axis, up)
        after = lax.ppermute(leading, axis, down)
        x = jnp.concatenate([before, x, after], axis=dim)
    return x


def wendland(points_a, points_b):
    square_sum = jnp.zeros((points_a.shape[1], points_b.shape[1]), jnp.float32)
    for coord in range(3):
        offset = points_a[coord][:, None] - points_b[coord][None, :]
        square_sum = square_sum + offset * offset
    distance = jnp.sqrt(square_sum)
    remain = jnp.maximum(1.0 - distance, 0.0)
    remain = remain * remain
    return remain * remain * (4.0 * distance + 1.0)


def cell_rim(field):
    return with_halo(field, (("gx", 1), ("gy", 2)), 1)


def inner_sums(left, right):
    return jnp.sum(left * right, axis=(1, 2, 3, 4))


def per_component(values):
    return values[:, None, None, None, None]


def global_inner(values):
    return lax.psum(values, ("gx", "gy"))


def local(positions, counts, targets, landmark_index, coarse_matrix):
    components = targets.shape[0]
    layer_count = positions.shape[3]
    slot_count = positions.shape[4]
    owned_count = landmark_index.shape[2]
    column_points = layer_count * slot_count
    slot_ids = jnp.arange(slot_count, dtype=jnp.int32)
    live_mask = (slot_ids[None, None, None, :] < counts[:, :, :, None]).astype(jnp.float32)
    live_flat = live_mask.reshape(1, column_points)
    rhs_field = live_mask[None] * targets
    ext_pos = cell_rim(positions)
    ext_cloud = ext_pos.reshape(3, 9 * column_points)
    own_points = positions.reshape(3, column_points)
    row_index = lax.axis_index("gx")
    col_index = lax.axis_index("gy")
    three_ids = jnp.arange(3, dtype=jnp.int32)
    near_rows = jnp.clip(row_index + three_ids - 1, 0, lax.axis_size("gx") - 1)
    near_cols = jnp.clip(col_index + three_ids - 1, 0, lax.axis_size("gy") - 1)
    near_index = landmark_index[near_rows[:, None], near_cols[None, :], :]
    ext_flat = ext_pos.reshape(3, 3, 3, column_points)
    near_pos = jnp.take_along_axis(ext_flat, near_index[None], axis=3)
    landmark_pos = near_pos[:, 1, 1, :]
    spread_kernel = wendland(own_points, near_pos.reshape(3, 9 * owned_count))

    def coarse_solve(terms):
        row_terms = lax.all_gather(terms, "gy", axis=0, tiled=True)
        return lax.psum_scatter(
            jnp.dot(coarse_matrix, row_terms, precision=HIGHEST_PRECISION),
            "gx",
            scatter_dimension=0,
            tiled=True,
        )

    def landmark_sums(vector):
        gather_kernel = wendland(landmark_pos, ext_cloud)
        ext_vec = cell_rim(vector).reshape(components, 9 * column_points)
        return jnp.einsum("kn,qn->kq", gather_kernel, ext_vec, precision=HIGHEST_PRECISION)

    def precondition(vector):
        terms = landmark_sums(vector)
        coarse = coarse_solve(terms)
        near_coarse = with_halo(
            coarse.reshape(1, 1, owned_count, components), (("gx", 0), ("gy", 1)), 1
        )
        near_coarse = near_coarse.reshape(9 * owned_count, components)
        spread = jnp.einsum("nm,mq->qn", spread_kernel, near_coarse, precision=HIGHEST_PRECISION)
        return vector / RIDGE_WEIGHT + (live_flat * spread).reshape(vector.shape)

    solution = jnp.zeros_like(rhs_field)
    residual = rhs_field
    search = precondition(residual)
    gamma = global_inner(inner_sums(residual, search))
    direction = search
    for iteration in range(ITERS):
        operator_ext_vec = cell_rim(direction)
        layer_out = []
        for layer in range(layer_count):
            low_layer = max(layer - 1, 0)
            high_layer = min(layer + 2, layer_count)
            near_points = ext_pos[:, :, :, low_layer:high_layer, :].reshape(3, -1)
            near_values = operator_ext_vec[:, :, :, low_layer:high_layer, :].reshape(components, -1)
            kern = wendland(positions[:, 0, 0, layer, :], near_points)
            layer_out.append(
                jnp.einsum("bn,qn->qb", kern, near_values, precision=HIGHEST_PRECISION)
            )
        product = jnp.stack(layer_out, axis=1).reshape(direction.shape)
        image = live_mask[None] * product + RIDGE_WEIGHT * direction
        alpha = gamma / global_inner(inner_sums(direction, image))
        solution = solution + per_component(alpha) * direction
        residual = residual - per_component(alpha) * image
        if iteration + 1 < ITERS:
            search = precondition(residual)
            gamma_new = global_inner(inner_sums(residual, search))
            direction = search + per_component(gamma_new / gamma) * direction
            gamma = gamma_new
    return (solution, residual)


def solution(mesh):
    return jax.shard_map(
        local,
        mesh=mesh,
        in_specs=(
            P(None, "gx", "gy", None, None),
            P("gx", "gy", None),
            P(None, "gx", "gy", None, None),
            P(),
            P("gy", "gx"),
        ),
        out_specs=(P(None, "gx", "gy", None, None), P(None, "gx", "gy", None, None)),
        check_vma=False,
    )
```

profile of v0, /device:TPU:0, one launch (start us, length us, event | category | flops | bytes accessed | tf_op | source)
XLA Modules:
  0.0 359.1 jit_solution(12400177089312174159)
XLA Ops:
  2.1 4.9 %collective-permute-start.4 = (f32[3,1,1,4,256]{4,0,3,2,1:T(4,128)S(1)}, f32[3,1,1,4,256]{4,0,3,2,1:T(4,128)S(1)}, u32[]{:S(2)}, u32[]{:S(2)}) collective-permute-start(f32[3,1,1,4,256]{4,0,3,2,1:T(4,128)S(1)} %copy_multiply_fusion), channel_id=1, source_target_pairs={{0,4},{4,8},{8,12},{12,16},{16,20},{20,24},{24,28},{1,5},{5,9},{9,... | collective-permute-start | bytes 36872 | tf_op jit(solution)/shard_map/ppermute | solution.py:20
  7.0 1.3 collective-permute-start.5
  8.3 4.5 %collective-permute-start = (f32[3,1,1,4,256]{4,3,2,1,0:T(4,128)}, f32[3,1,1,4,256]{4,3,2,1,0:T(4,128)S(1)}, u32[]{:S(2)}, u32[]{:S(2)}) collective-permute-start(f32[3,1,1,4,256]{4,3,2,1,0:T(4,128)} %param.5), channel_id=1, source_target_pairs={{0,4},{4,8},{8,12},{12,16},{16,20},{20,24},{24,28},{1,5},{5,9},{9,... | collective-permute-start | bytes 36872 | tf_op jit(solution)/shard_map/ppermute | solution.py:20
  12.9 1.3 collective-permute-start.1
  22.8 1.3 collective-permute-start.3
  24.1 4.8 %collective-permute-start.6 = (f32[3,3,1,4,256]{4,0,3,2,1:T(4,128)S(1)}, f32[3,3,1,4,256]{4,0,3,2,1:T(4,128)S(1)}, u32[]{:S(2)}, u32[]{:S(2)}) collective-permute-start(f32[3,3,1,4,256]{4,0,3,2,1:T(4,128)S(1)} %pad_maximum_fusion.5), channel_id=1, source_target_pairs={{0,1},{1,2},{2,3},{4,5},{5,6},{6,7},{8,9},{9,10},{10,11},{12,13},{... | collective-permute-start | bytes 110600 | tf_op jit(solution)/shard_map/ppermute | solution.py:20
  28.9 1.3 collective-permute-start.7
  30.2 2.9 copy.71
  33.1 2.4 gather_fusion.1
  36.8 7.2 %all-gather = f32[4,4,3]{2,1,0:T(4,128)S(1)} all-gather(f32[1,4,3]{2,1,0:T(4,128)S(1)} %convolution_bitcast_fusion.3), channel_id=1, replica_groups=mesh['gx'=8,'gy'=4] {'gy'}, dimensions={0}, use_global_device_ids=true | all-gather | bytes 240 | tf_op jit(solution)/shard_map/all_gather | solution.py:78
  44.2 22.8 %all-reduce = f32[32,3]{0,1:T(4,128)S(1)} all-reduce(f32[32,3]{0,1:T(4,128)S(1)} %convolution_bitcast_fusion.2), channel_id=2, replica_groups=mesh['gx'=8,'gy'=4] {'gx'}, use_global_device_ids=true, to_apply=%region_0.1.clone | all-reduce | flops 96 | bytes 768
  67.1 1.5 collective-permute-start.8
  68.6 1.3 collective-permute-start.9
  70.1 4.0 %collective-permute-done.9 = f32[1,1,4,3]{3,2,1,0:T(4,128)S(1)} collective-permute-done((f32[1,1,4,3]{3,2,1,0:T(4,128)S(1)}, f32[1,1,4,3]{3,2,1,0:T(4,128)S(1)}, u32[]{:S(2)}, u32[]{:S(2)}) %collective-permute-start.9) | collective-permute-done | bytes 80 | tf_op jit(solution)/shard_map/ppermute | solution.py:21
  75.4 1.3 collective-permute-start.11
  76.8 3.9 %collective-permute-done.11 = f32[3,1,4,3]{3,2,1,0:T(4,128)S(1)} collective-permute-done((f32[3,1,4,3]{3,2,1,0:T(4,128)S(1)}, f32[3,1,4,3]{3,2,1,0:T(4,128)S(1)}, u32[]{:S(2)}, u32[]{:S(2)}) %collective-permute-start.11) | collective-permute-done | bytes 176 | tf_op jit(solution)/shard_map/ppermute | solution.py:21
  81.1 3.4 collective-permute-start.12
  84.6 1.3 collective-permute-start.13
  86.0 4.2 %collective-permute-done.13 = f32[3,1,1,4,256]{4,0,3,2,1:T(4,128)S(1)} collective-permute-done((f32[3,1,1,4,256]{4,0,3,2,1:T(4,128)S(1)}, f32[3,1,1,4,256]{4,0,3,2,1:T(4,128)S(1)}, u32[]{:S(2)}, u32[]{:S(2)}) %collective-permute-start.13) | collective-permute-done | bytes 12320 | tf_op jit(solution)/shard_map/ppermute | solution.py:21
  90.2 2.9 collective-permute-start.14
  93.1 1.6 collective-permute-start.15
  95.0 2.2 collective-permute-done.15
  97.3 6.4 %fusion.82 = f32[3,1,1,1,256]{4,0,3,2,1:T(4,128)S(1)} fusion(f32[3,4608]{1,0:T(4,128)S(1)} %bitcast.137, f32[4608]{0:T(1024)S(1)} %sub.492, f32[256]{0:T(256)S(1)} %bitcast.187, f32[4608]{0:T(1024)S(1)} %sub.241, f32[256]{0:T(256)S(1)} %bitcast.189, f32[4608]{0:T(1024)S(1)} %sub.236, f32[256]{0:T(256)S(1)} %bitcast.185), kind=kOutput, calls=%fused_computation.90 | convolution fusion | flops 60162048 | bytes 116736 | tf_op jit(solution)/shard_map/bn,qn->qb/dot_general | solution.py:116
  103.8 10.1 %fusion.86 = f32[3,1,1,1,256]{4,0,3,2,1:T(4,128)S(1)} fusion(f32[3,6912]{1,0:T(4,128)S(1)} %bitcast.133, f32[6912]{0:T(1024)S(1)} %sub.508, f32[256]{0:T(256)S(1)} %bitcast.179, f32[6912]{0:T(1024)S(1)} %sub.503, f32[256]{0:T(256)S(1)} %bitcast.181, f32[6912]{0:T(1024)S(1)} %sub.498, f32[256]{0:T(256)S(1)} %bitcast.183), kind=kOutput, calls=%fused_computation.94 | convolution fusion | flops 90243072 | bytes 172032 | tf_op jit(solution)/shard_map/bn,qn->qb/dot_general | solution.py:116
  113.9 9.8 %fusion.84 = f32[3,1,1,1,256]{4,0,3,2,1:T(4,128)S(1)} fusion(f32[3,6912]{1,0:T(4,128)S(1)} %bitcast.132, f32[6912]{0:T(1024)S(1)} %sub.524, f32[256]{0:T(256)S(1)} %bitcast.173, f32[6912]{0:T(1024)S(1)} %sub.519, f32[256]{0:T(256)S(1)} %bitcast.175, f32[6912]{0:T(1024)S(1)} %sub.514, f32[256]{0:T(256)S(1)} %bitcast.177), kind=kOutput, calls=%fused_computation.92 | convolution fusion | flops 90243072 | bytes 172032 | tf_op jit(solution)/shard_map/bn,qn->qb/dot_general | solution.py:116
  123.6 6.5 %fusion.80 = f32[3,1,1,1,256]{4,0,3,2,1:T(4,128)S(1)} fusion(f32[3,4608]{1,0:T(4,128)S(1)} %bitcast.135, f32[4608]{0:T(1024)S(1)} %sub.540, f32[256]{0:T(256)S(1)} %bitcast.169, f32[4608]{0:T(1024)S(1)} %sub.535, f32[256]{0:T(256)S(1)} %bitcast.171, f32[4608]{0:T(1024)S(1)} %sub.530, f32[256]{0:T(256)S(1)} %bitcast.167), kind=kOutput, calls=%fused_computation.88 | convolution fusion | flops 60162048 | bytes 116736 | tf_op jit(solution)/shard_map/bn,qn->qb/dot_general | solution.py:116
  130.3 39.7 %all-reduce.2 = (f32[3]{0:T(128)S(1)}, f32[3]{0:T(128)S(1)}) all-reduce(f32[3]{0:T(128)S(1)} %get-tuple-element.11, f32[3]{0:T(128)S(1)} %get-tuple-element.10), channel_id=1, replica_groups=mesh['gx'=8,'gy'=4] {'gx','gy'}, use_global_device_ids=true, to_apply=%region_2.3 | all-reduce | flops 6 | bytes 48 | tf_op jit(solution)/shard_map/psum | solution.py:50
  170.1 4.2 %collective-permute-start.16 = (f32[3,1,1,4,256]{4,0,3,2,1:T(4,128)S(1)}, f32[3,1,1,4,256]{4,0,3,2,1:T(4,128)S(1)}, u32[]{:S(2)}, u32[]{:S(2)}) collective-permute-start(f32[3,1,1,4,256]{4,0,3,2,1:T(4,128)S(1)} %multiply_subtract_fusion.1), channel_id=1, source_target_pairs={{0,4},{4,8},{8,12},{12,16},{16,20},{20,24},{24,28},{1,5},{5,9},{9,... | collective-permute-start | bytes 36872 | tf_op jit(solution)/shard_map/ppermute | solution.py:20
  174.3 1.3 collective-permute-start.17
  175.7 4.2 %collective-permute-done.17 = f32[3,1,1,4,256]{4,0,3,2,1:T(4,128)S(1)} collective-permute-done((f32[3,1,1,4,256]{4,0,3,2,1:T(4,128)S(1)}, f32[3,1,1,4,256]{4,0,3,2,1:T(4,128)S(1)}, u32[]{:S(2)}, u32[]{:S(2)}) %collective-permute-start.17) | collective-permute-done | bytes 12320 | tf_op jit(solution)/shard_map/ppermute | solution.py:21
  179.9 1.3 collective-permute-start.18
  181.2 1.3 collective-permute-start.19
  182.5 3.1 collective-permute-done.19
  186.6 6.7 %all-gather.1 = f32[4,4,3]{2,1,0:T(4,128)S(1)} all-gather(f32[1,4,3]{2,1,0:T(4,128)S(1)} %convolution_bitcast_fusion.1), channel_id=1, replica_groups=mesh['gx'=8,'gy'=4] {'gy'}, dimensions={0}, use_global_device_ids=true | all-gather | bytes 240 | tf_op jit(solution)/shard_map/all_gather | solution.py:78
  193.4 20.0 %all-reduce.1 = f32[32,3]{0,1:T(4,128)S(1)} all-reduce(f32[32,3]{0,1:T(4,128)S(1)} %convolution_bitcast_fusion), channel_id=3, replica_groups=mesh['gx'=8,'gy'=4] {'gx'}, use_global_device_ids=true, to_apply=%region_5.6.clone | all-reduce | flops 96 | bytes 768
  216.2 4.2 %collective-permute-done.21 = f32[1,1,4,3]{3,2,1,0:T(4,128)S(1)} collective-permute-done((f32[1,1,4,3]{3,2,1,0:T(4,128)S(1)}, f32[1,1,4,3]{3,2,1,0:T(4,128)S(1)}, u32[]{:S(2)}, u32[]{:S(2)}) %collective-permute-start.21) | collective-permute-done | bytes 80 | tf_op jit(solution)/shard_map/ppermute | solution.py:21
  223.0 3.3 collective-permute-done.23
  226.8 39.5 %psum.30 = f32[3]{0:T(128)S(1)} all-reduce(f32[3]{0:T(128)S(1)} %multiply_reduce_fusion.1), channel_id=1, replica_groups=mesh['gx'=8,'gy'=4] {'gx','gy'}, use_global_device_ids=true, to_apply=%region_7.8 | all-reduce | flops 3 | bytes 24 | tf_op jit(solution)/shard_map/psum | solution.py:50
  266.5 4.2 %collective-permute-start.24 = (f32[3,1,1,4,256]{4,0,3,2,1:T(4,128)S(1)}, f32[3,1,1,4,256]{4,0,3,2,1:T(4,128)S(1)}, u32[]{:S(2)}, u32[]{:S(2)}) collective-permute-start(f32[3,1,1,4,256]{4,0,3,2,1:T(4,128)S(1)} %multiply_add_fusion.1), channel_id=1, source_target_pairs={{0,4},{4,8},{8,12},{12,16},{16,20},{20,24},{24,28},{1,5},{5,9},{9,... | collective-permute-start | bytes 36872 | tf_op jit(solution)/shard_map/ppermute | solution.py:20
  270.6 1.3 collective-permute-start.25
  272.1 4.2 %collective-permute-done.25 = f32[3,1,1,4,256]{4,0,3,2,1:T(4,128)S(1)} collective-permute-done((f32[3,1,1,4,256]{4,0,3,2,1:T(4,128)S(1)}, f32[3,1,1,4,256]{4,0,3,2,1:T(4,128)S(1)}, u32[]{:S(2)}, u32[]{:S(2)}) %collective-permute-start.25) | collective-permute-done | bytes 12320 | tf_op jit(solution)/shard_map/ppermute | solution.py:21
  277.6 1.5 collective-permute-start.27
  279.1 3.6 collective-permute-done.27
  282.8 6.4 %fusion.83 = f32[3,1,1,1,256]{4,0,3,2,1:T(4,128)S(1)} fusion(f32[3,4608]{1,0:T(4,128)S(1)} %bitcast.136, f32[4608]{0:T(1024)S(1)} %sub.492, f32[256]{0:T(256)S(1)} %bitcast.188, f32[4608]{0:T(1024)S(1)} %sub.241, f32[256]{0:T(256)S(1)} %bitcast.190, f32[4608]{0:T(1024)S(1)} %sub.236, f32[256]{0:T(256)S(1)} %bitcast.186), kind=kOutput, calls=%fused_computation.91 | convolution fusion | flops 60162048 | bytes 116736 | tf_op jit(solution)/shard_map/bn,qn->qb/dot_general | solution.py:116
  289.2 10.0 %fusion.87 = f32[3,1,1,1,256]{4,0,3,2,1:T(4,128)S(1)} fusion(f32[3,6912]{1,0:T(4,128)S(1)} %bitcast.131, f32[6912]{0:T(1024)S(1)} %sub.508, f32[256]{0:T(256)S(1)} %bitcast.180, f32[6912]{0:T(1024)S(1)} %sub.503, f32[256]{0:T(256)S(1)} %bitcast.182, f32[6912]{0:T(1024)S(1)} %sub.498, f32[256]{0:T(256)S(1)} %bitcast.184), kind=kOutput, calls=%fused_computation.95 | convolution fusion | flops 90243072 | bytes 172032 | tf_op jit(solution)/shard_map/bn,qn->qb/dot_general | solution.py:116
  299.2 9.8 %fusion.85 = f32[3,1,1,1,256]{4,0,3,2,1:T(4,128)S(1)} fusion(f32[3,6912]{1,0:T(4,128)S(1)} %bitcast.130, f32[6912]{0:T(1024)S(1)} %sub.524, f32[256]{0:T(256)S(1)} %bitcast.174, f32[6912]{0:T(1024)S(1)} %sub.519, f32[256]{0:T(256)S(1)} %bitcast.176, f32[6912]{0:T(1024)S(1)} %sub.514, f32[256]{0:T(256)S(1)} %bitcast.178), kind=kOutput, calls=%fused_computation.93 | convolution fusion | flops 90243072 | bytes 172032 | tf_op jit(solution)/shard_map/bn,qn->qb/dot_general | solution.py:116
  309.0 6.5 %fusion.81 = f32[3,1,1,1,256]{4,0,3,2,1:T(4,128)S(1)} fusion(f32[3,4608]{1,0:T(4,128)S(1)} %bitcast.134, f32[4608]{0:T(1024)S(1)} %sub.540, f32[256]{0:T(256)S(1)} %bitcast.170, f32[4608]{0:T(1024)S(1)} %sub.535, f32[256]{0:T(256)S(1)} %bitcast.172, f32[4608]{0:T(1024)S(1)} %sub.530, f32[256]{0:T(256)S(1)} %bitcast.168), kind=kOutput, calls=%fused_computation.89 | convolution fusion | flops 60162048 | bytes 116736 | tf_op jit(solution)/shard_map/bn,qn->qb/dot_general | solution.py:116
  315.6 42.0 %psum.31 = f32[3]{0:T(128)S(1)} all-reduce(f32[3]{0:T(128)S(1)} %multiply_reduce_fusion), channel_id=1, replica_groups=mesh['gx'=8,'gy'=4] {'gx','gy'}, use_global_device_ids=true, to_apply=%region_9.10 | all-reduce | flops 3 | bytes 24 | tf_op jit(solution)/shard_map/psum | solution.py:50
  (124 shorter events, 23.7 us)
Async XLA Ops:
  0.6 43.3 %copy-start = (f32[32,16]{0,1:T(8,128)S(1)}, f32[32,16]{0,1:T(8,128)}, u32[]{:S(2)}) copy-start(f32[32,16]{0,1:T(8,128)} %param.9) | copy-start | bytes 6148
  0.6 80.5 %copy-start.1 = (f32[3,1,1,4,256]{4,3,2,1,0:T(4,128)S(1)}, f32[3,1,1,4,256]{4,3,2,1,0:T(4,128)}, u32[]{:S(2)}) copy-start(f32[3,1,1,4,256]{4,3,2,1,0:T(4,128)} %param.7) | copy-start | bytes 36868
  2.1 22.0 %collective-permute-start.4 = (f32[3,1,1,4,256]{4,0,3,2,1:T(4,128)S(1)}, f32[3,1,1,4,256]{4,0,3,2,1:T(4,128)S(1)}, u32[]{:S(2)}, u32[]{:S(2)}) collective-permute-start(f32[3,1,1,4,256]{4,0,3,2,1:T(4,128)S(1)} %copy_multiply_fusion), channel_id=1, source_target_pairs={{0,4},{4,8},{8,12},{12,16},{16,20},{20,24},{24,28},{1,5},{5,9},{9,... | collective-permute-start | bytes 36872 | tf_op jit(solution)/shard_map/ppermute | solution.py:20
  7.0 17.1 %collective-permute-start.5 = (f32[3,1,1,4,256]{4,0,3,2,1:T(4,128)S(1)}, f32[3,1,1,4,256]{4,0,3,2,1:T(4,128)S(1)}, u32[]{:S(2)}, u32[]{:S(2)}) collective-permute-start(f32[3,1,1,4,256]{4,0,3,2,1:T(4,128)S(1)} %copy_multiply_fusion), channel_id=1, source_target_pairs={{4,0},{8,4},{12,8},{16,12},{20,16},{24,20},{28,24},{5,1},{9,5},{13... | collective-permute-start | bytes 36872 | tf_op jit(solution)/shard_map/ppermute | solution.py:21
  8.3 12.4 %collective-permute-start = (f32[3,1,1,4,256]{4,3,2,1,0:T(4,128)}, f32[3,1,1,4,256]{4,3,2,1,0:T(4,128)S(1)}, u32[]{:S(2)}, u32[]{:S(2)}) collective-permute-start(f32[3,1,1,4,256]{4,3,2,1,0:T(4,128)} %param.5), channel_id=1, source_target_pairs={{0,4},{4,8},{8,12},{12,16},{16,20},{20,24},{24,28},{1,5},{5,9},{9,... | collective-permute-start | bytes 36872 | tf_op jit(solution)/shard_map/ppermute | solution.py:20
  12.9 8.6 %collective-permute-start.1 = (f32[3,1,1,4,256]{4,3,2,1,0:T(4,128)}, f32[3,1,1,4,256]{4,3,2,1,0:T(4,128)S(1)}, u32[]{:S(2)}, u32[]{:S(2)}) collective-permute-start(f32[3,1,1,4,256]{4,3,2,1,0:T(4,128)} %param.5), channel_id=1, source_target_pairs={{4,0},{8,4},{12,8},{16,12},{20,16},{24,20},{28,24},{5,1},{9,5},{13... | collective-permute-start | bytes 36872 | tf_op jit(solution)/shard_map/ppermute | solution.py:21
  21.5 8.7 %collective-permute-start.2 = (f32[3,3,1,4,256]{4,3,2,1,0:T(4,128)S(1)}, f32[3,3,1,4,256]{4,3,2,1,0:T(4,128)S(1)}, u32[]{:S(2)}, u32[]{:S(2)}) collective-permute-start(f32[3,3,1,4,256]{4,3,2,1,0:T(4,128)S(1)} %constant_dynamic-update-slice_fusion), channel_id=1, source_target_pairs={{0,1},{1,2},{2,3},{4,5},{5,6},{6,7},{8,9},{9,10},{10,11},{12,13},{... | collective-permute-start | bytes 110600 | tf_op jit(solution)/shard_map/ppermute | solution.py:20
  22.8 7.4 %collective-permute-start.3 = (f32[3,3,1,4,256]{4,3,2,1,0:T(4,128)S(1)}, f32[3,3,1,4,256]{4,3,2,1,0:T(4,128)S(1)}, u32[]{:S(2)}, u32[]{:S(2)}) collective-permute-start(f32[3,3,1,4,256]{4,3,2,1,0:T(4,128)S(1)} %constant_dynamic-update-slice_fusion), channel_id=1, source_target_pairs={{1,0},{2,1},{3,2},{5,4},{6,5},{7,6},{9,8},{10,9},{11,10},{13,12},{... | collective-permute-start | bytes 110600 | tf_op jit(solution)/shard_map/ppermute | solution.py:21
  24.1 11.8 %collective-permute-start.6 = (f32[3,3,1,4,256]{4,0,3,2,1:T(4,128)S(1)}, f32[3,3,1,4,256]{4,0,3,2,1:T(4,128)S(1)}, u32[]{:S(2)}, u32[]{:S(2)}) collective-permute-start(f32[3,3,1,4,256]{4,0,3,2,1:T(4,128)S(1)} %pad_maximum_fusion.5), channel_id=1, source_target_pairs={{0,1},{1,2},{2,3},{4,5},{5,6},{6,7},{8,9},{9,10},{10,11},{12,13},{... | collective-permute-start | bytes 110600 | tf_op jit(solution)/shard_map/ppermute | solution.py:20
  28.9 7.0 %collective-permute-start.7 = (f32[3,3,1,4,256]{4,0,3,2,1:T(4,128)S(1)}, f32[3,3,1,4,256]{4,0,3,2,1:T(4,128)S(1)}, u32[]{:S(2)}, u32[]{:S(2)}) collective-permute-start(f32[3,3,1,4,256]{4,0,3,2,1:T(4,128)S(1)} %pad_maximum_fusion.5), channel_id=1, source_target_pairs={{1,0},{2,1},{3,2},{5,4},{6,5},{7,6},{9,8},{10,9},{11,10},{13,12},{... | collective-permute-start | bytes 110600 | tf_op jit(solution)/shard_map/ppermute | solution.py:21
  67.1 3.0 collective-permute-start.8
  68.6 5.5 %collective-permute-start.9 = (f32[1,1,4,3]{3,2,1,0:T(4,128)S(1)}, f32[1,1,4,3]{3,2,1,0:T(4,128)S(1)}, u32[]{:S(2)}, u32[]{:S(2)}) collective-permute-start(f32[1,1,4,3]{3,2,1,0:T(4,128)S(1)} %bitcast.149), channel_id=1, source_target_pairs={{4,0},{8,4},{12,8},{16,12},{20,16},{24,20},{28,24},{5,1},{9,5},{13... | collective-permute-start | bytes 152 | tf_op jit(solution)/shard_map/ppermute | solution.py:21
  74.1 2.7 collective-permute-start.10
  75.4 5.3 %collective-permute-start.11 = (f32[3,1,4,3]{3,2,1,0:T(4,128)S(1)}, f32[3,1,4,3]{3,2,1,0:T(4,128)S(1)}, u32[]{:S(2)}, u32[]{:S(2)}) collective-permute-start(f32[3,1,4,3]{3,2,1,0:T(4,128)S(1)} %pad_maximum_fusion.11), channel_id=1, source_target_pairs={{1,0},{2,1},{3,2},{5,4},{6,5},{7,6},{9,8},{10,9},{11,10},{13,12},{... | collective-permute-start | bytes 440 | tf_op jit(solution)/shard_map/ppermute | solution.py:21
  81.1 4.9 %collective-permute-start.12 = (f32[3,1,1,4,256]{4,0,3,2,1:T(4,128)S(1)}, f32[3,1,1,4,256]{4,0,3,2,1:T(4,128)S(1)}, u32[]{:S(2)}, u32[]{:S(2)}) collective-permute-start(f32[3,1,1,4,256]{4,0,3,2,1:T(4,128)S(1)} %multiply_add_fusion.3), channel_id=1, source_target_pairs={{0,4},{4,8},{8,12},{12,16},{16,20},{20,24},{24,28},{1,5},{5,9},{9,... | collective-permute-start | bytes 36872 | tf_op jit(solution)/shard_map/ppermute | solution.py:20
  84.6 5.6 %collective-permute-start.13 = (f32[3,1,1,4,256]{4,0,3,2,1:T(4,128)S(1)}, f32[3,1,1,4,256]{4,0,3,2,1:T(4,128)S(1)}, u32[]{:S(2)}, u32[]{:S(2)}) collective-permute-start(f32[3,1,1,4,256]{4,0,3,2,1:T(4,128)S(1)} %multiply_add_fusion.3), channel_id=1, source_target_pairs={{4,0},{8,4},{12,8},{16,12},{20,16},{24,20},{28,24},{5,1},{9,5},{13... | collective-permute-start | bytes 36872 | tf_op jit(solution)/shard_map/ppermute | solution.py:21
  90.2 4.8 %collective-permute-start.14 = (f32[3,3,1,4,256]{4,0,3,2,1:T(4,128)S(1)}, f32[3,3,1,4,256]{4,0,3,2,1:T(4,128)S(1)}, u32[]{:S(2)}, u32[]{:S(2)}) collective-permute-start(f32[3,3,1,4,256]{4,0,3,2,1:T(4,128)S(1)} %pad_maximum_fusion.6), channel_id=1, source_target_pairs={{0,1},{1,2},{2,3},{4,5},{5,6},{6,7},{8,9},{9,10},{10,11},{12,13},{... | collective-permute-start | bytes 110600 | tf_op jit(solution)/shard_map/ppermute | solution.py:20
  93.1 4.1 %collective-permute-start.15 = (f32[3,3,1,4,256]{4,0,3,2,1:T(4,128)S(1)}, f32[3,3,1,4,256]{4,0,3,2,1:T(4,128)S(1)}, u32[]{:S(2)}, u32[]{:S(2)}) collective-permute-start(f32[3,3,1,4,256]{4,0,3,2,1:T(4,128)S(1)} %pad_maximum_fusion.6), channel_id=1, source_target_pairs={{1,0},{2,1},{3,2},{5,4},{6,5},{7,6},{9,8},{10,9},{11,10},{13,12},{... | collective-permute-start | bytes 110600 | tf_op jit(solution)/shard_map/ppermute | solution.py:21
  170.1 5.6 %collective-permute-start.16 = (f32[3,1,1,4,256]{4,0,3,2,1:T(4,128)S(1)}, f32[3,1,1,4,256]{4,0,3,2,1:T(4,128)S(1)}, u32[]{:S(2)}, u32[]{:S(2)}) collective-permute-start(f32[3,1,1,4,256]{4,0,3,2,1:T(4,128)S(1)} %multiply_subtract_fusion.1), channel_id=1, source_target_pairs={{0,4},{4,8},{8,12},{12,16},{16,20},{20,24},{24,28},{1,5},{5,9},{9,... | collective-permute-start | bytes 36872 | tf_op jit(solution)/shard_map/ppermute | solution.py:20
  174.3 5.6 %collective-permute-start.17 = (f32[3,1,1,4,256]{4,0,3,2,1:T(4,128)S(1)}, f32[3,1,1,4,256]{4,0,3,2,1:T(4,128)S(1)}, u32[]{:S(2)}, u32[]{:S(2)}) collective-permute-start(f32[3,1,1,4,256]{4,0,3,2,1:T(4,128)S(1)} %multiply_subtract_fusion.1), channel_id=1, source_target_pairs={{4,0},{8,4},{12,8},{16,12},{20,16},{24,20},{28,24},{5,1},{9,5},{13... | collective-permute-start | bytes 36872 | tf_op jit(solution)/shard_map/ppermute | solution.py:21
  179.9 2.6 collective-permute-start.18
  181.2 4.5 %collective-permute-start.19 = (f32[3,3,1,4,256]{4,0,3,2,1:T(4,128)S(1)}, f32[3,3,1,4,256]{4,0,3,2,1:T(4,128)S(1)}, u32[]{:S(2)}, u32[]{:S(2)}) collective-permute-start(f32[3,3,1,4,256]{4,0,3,2,1:T(4,128)S(1)} %pad_maximum_fusion.7), channel_id=1, source_target_pairs={{1,0},{2,1},{3,2},{5,4},{6,5},{7,6},{9,8},{10,9},{11,10},{13,12},{... | collective-permute-start | bytes 110600 | tf_op jit(solution)/shard_map/ppermute | solution.py:21
  213.6 2.6 collective-permute-start.20
  214.9 5.5 %collective-permute-start.21 = (f32[1,1,4,3]{3,2,1,0:T(4,128)S(1)}, f32[1,1,4,3]{3,2,1,0:T(4,128)S(1)}, u32[]{:S(2)}, u32[]{:S(2)}) collective-permute-start(f32[1,1,4,3]{3,2,1,0:T(4,128)S(1)} %bitcast.153), channel_id=1, source_target_pairs={{4,0},{8,4},{12,8},{16,12},{20,16},{24,20},{28,24},{5,1},{9,5},{13... | collective-permute-start | bytes 152 | tf_op jit(solution)/shard_map/ppermute | solution.py:21
  220.4 2.6 collective-permute-start.22
  221.7 4.6 %collective-permute-start.23 = (f32[3,1,4,3]{3,2,1,0:T(4,128)S(1)}, f32[3,1,4,3]{3,2,1,0:T(4,128)S(1)}, u32[]{:S(2)}, u32[]{:S(2)}) collective-permute-start(f32[3,1,4,3]{3,2,1,0:T(4,128)S(1)} %pad_maximum_fusion.12), channel_id=1, source_target_pairs={{1,0},{2,1},{3,2},{5,4},{6,5},{7,6},{9,8},{10,9},{11,10},{13,12},{... | collective-permute-start | bytes 440 | tf_op jit(solution)/shard_map/ppermute | solution.py:21
  266.5 5.6 %collective-permute-start.24 = (f32[3,1,1,4,256]{4,0,3,2,1:T(4,128)S(1)}, f32[3,1,1,4,256]{4,0,3,2,1:T(4,128)S(1)}, u32[]{:S(2)}, u32[]{:S(2)}) collective-permute-start(f32[3,1,1,4,256]{4,0,3,2,1:T(4,128)S(1)} %multiply_add_fusion.1), channel_id=1, source_target_pairs={{0,4},{4,8},{8,12},{12,16},{16,20},{20,24},{24,28},{1,5},{5,9},{9,... | collective-permute-start | bytes 36872 | tf_op jit(solution)/shard_map/ppermute | solution.py:20
  270.6 5.6 %collective-permute-start.25 = (f32[3,1,1,4,256]{4,0,3,2,1:T(4,128)S(1)}, f32[3,1,1,4,256]{4,0,3,2,1:T(4,128)S(1)}, u32[]{:S(2)}, u32[]{:S(2)}) collective-permute-start(f32[3,1,1,4,256]{4,0,3,2,1:T(4,128)S(1)} %multiply_add_fusion.1), channel_id=1, source_target_pairs={{4,0},{8,4},{12,8},{16,12},{20,16},{24,20},{28,24},{5,1},{9,5},{13... | collective-permute-start | bytes 36872 | tf_op jit(solution)/shard_map/ppermute | solution.py:21
  276.3 2.8 collective-permute-start.26
  277.6 5.1 %collective-permute-start.27 = (f32[3,3,1,4,256]{4,0,3,2,1:T(4,128)S(1)}, f32[3,3,1,4,256]{4,0,3,2,1:T(4,128)S(1)}, u32[]{:S(2)}, u32[]{:S(2)}) collective-permute-start(f32[3,3,1,4,256]{4,0,3,2,1:T(4,128)S(1)} %pad_maximum_fusion.8), channel_id=1, source_target_pairs={{1,0},{2,1},{3,2},{5,4},{6,5},{7,6},{9,8},{10,9},{11,10},{13,12},{... | collective-permute-start | bytes 110600 | tf_op jit(solution)/shard_map/ppermute | solution.py:21
where the time goes:
time: 364 us; the launch traced here: 359 us
  blocking collectives  178 us (49%)
  matrix products  68.3 us (19%)
  starting transfers between devices  56.6 us (16%)
  waiting for transfers between devices  37.2 us (10%)
  local copies, waits for them, and re-layouts  14.3 us (4%)
    psum x3, blocking collectives, global_inner(): return lax.psum(values, ('gx', 'gy'))  121 us
    dot_general x8, matrix products, local(): jnp.einsum('bn,qn->qb', kern, near_values, precision=HIGHEST_PRECISION)  65.5 us
    unnamed x2, blocking collectives  42.8 us
    ppermute x14, starting transfers between devices, with_halo(): before = lax.ppermute(last, axis, up)  38 us
    ppermute x14, waiting for transfers between devices, with_halo(): after = lax.ppermute(leading, axis, down)  36.9 us
    ppermute x14, starting transfers between devices, with_halo(): after = lax.ppermute(leading, axis, down)  18.6 us
    all_gather x2, blocking collectives, coarse_solve(): row_terms = lax.all_gather(terms, 'gy', axis=0, tiled=True)  13.8 us
  transfers between devices with their start and end apart: 28, of which 13 were waited for; matrix products, arithmetic and copies ran while one was open for 4% of the time, Pallas kernels for 0%

commit v1 on v0

--- a/solution.py
+++ b/solution.py
@@ -1,6 +1,10 @@
+import functools
+
 import jax
 import jax.numpy as jnp
 from jax import lax
+from jax.experimental import pallas as pl
+from jax.experimental.pallas import tpu as pltpu
 from jax.sharding import PartitionSpec as P
 
 ITERS = 2
@@ -8,6 +12,13 @@
 
 RIDGE_WEIGHT = 2.0
 HIGHEST_PRECISION = lax.Precision.HIGHEST
+
+F32 = jnp.float32
+BF16 = jnp.bfloat16
+LANES = 128
+FAR = 4096.0
+KERN_SCALE = 256.0
+VMEM_BYTES = 34 * 2**20
 
 
 def with_halo(x, sides, width):
@@ -50,7 +61,7 @@
     return lax.psum(values, ("gx", "gy"))
 
 
-def local(positions, counts, targets, landmark_index, coarse_matrix):
+def local_plain(positions, counts, targets, landmark_index, coarse_matrix):
     components = targets.shape[0]
     layer_count = positions.shape[3]
     slot_count = positions.shape[4]
@@ -128,6 +139,457 @@
     return (solution, residual)
 
 
+def row_ids(lanes):
+    return lax.broadcasted_iota(jnp.int32, (8, lanes), 0)
+
+
+def lane_ids(rows, lanes):
+    return lax.broadcasted_iota(jnp.int32, (rows, lanes), 1)
+
+
+def split_three(values):
+    high = values.astype(BF16).astype(F32)
+    rest = values - high
+    middle = rest.astype(BF16).astype(F32)
+    low = (rest - middle).astype(BF16).astype(F32)
+    return high, middle, low
+
+
+def centred(column, centre):
+    row = row_ids(column.shape[1])
+    shift = jnp.where(row == 0, centre[0], jnp.where(row == 1, centre[1], centre[2]))
+    xyz = jnp.where(row < 3, column - shift, 0.0)
+    norm = 16.0 * jnp.sum(xyz * xyz, axis=0, keepdims=True)
+    return row, xyz, norm + (1.0 - column[6:7, :]) * FAR
+
+
+def near_features(column, centre):
+    row, xyz, norm = centred(column, centre)
+    high, middle, low = split_three(
+        jnp.where(row == 3, norm, jnp.where(row == 4, 1.0, xyz))
+    )
+    return jnp.concatenate([high, middle, low, high, middle, high], axis=0)
+
+
+def own_features(column, centre):
+    row, xyz, norm = centred(column, centre)
+    high, middle, low = split_three(
+        jnp.where(row == 3, 1.0, jnp.where(row == 4, norm, -32.0 * xyz))
+    )
+    return jnp.concatenate([high, high, high, middle, middle, low], axis=0)
+
+
+def scaled_wendland(square16):
+    square16 = jnp.maximum(square16, 1e-6)
+    four = square16 * lax.rsqrt(square16)
+    remain = jnp.maximum(4.0 - four, 0.0)
+    remain = remain * remain
+    return remain * remain * (four + 1.0)
+
+
+def bf16_dot(left, right):
+    return jnp.dot(left, right, preferred_element_type=F32)
+
+
+def full_dot(left, right, transposed=False):
+    dims = (((1,), (1 if transposed else 0,)), ((), ()))
+    return lax.dot_general(
+        left, right, dims, precision=HIGHEST_PRECISION, preferred_element_type=F32
+    )
+
+
+def swap_partner(index, peers, odd):
+    step = 1 - 2 * lax.rem(index + odd, 2)
+    partner = index + step
+    good = jnp.logical_and(partner >= 0, partner < peers)
+    return jnp.where(good, partner, index)
+
+
+def swap(x, axis, odd):
+    peers = lax.axis_size(axis)
+    pairs = []
+    for i in range(odd, peers - 1, 2):
+        pairs += [(i, i + 1), (i + 1, i)]
+    return lax.ppermute(x, axis, pairs)
+
+
+class Shape:
+    def __init__(self, positions, landmark_index, nx, ny):
+        self.nx, self.ny = nx, ny
+        self.devices = nx * ny
+        self.layers, self.slots = positions.shape[3], positions.shape[4]
+        self.points = self.layers * self.slots
+        self.owned = landmark_index.shape[2]
+        self.row_landmarks = ny * self.owned
+        self.landmarks = nx * self.row_landmarks
+        self.window = 3 * self.row_landmarks
+        self.blocks = []
+        offset = 0
+        for layer in range(self.layers):
+            low, high = max(layer - 1, 0), min(layer + 2, self.layers)
+            self.blocks.append((low, high, offset))
+            offset += (high - low) * self.slots
+        self.pairs = offset
+
+    def centre(self, i, j):
+        return (i.astype(F32) + 0.5, j.astype(F32) + 0.5, 0.5 * self.layers)
+
+    def window_start(self, i):
+        start = jnp.clip(i - 1, 0, self.nx - 3) * self.row_landmarks
+        return pl.multiple_of(start, self.row_landmarks)
+
+    def near_ids(self, i, j):
+        rows = [i, swap_partner(i, self.nx, 0), swap_partner(i, self.nx, 1)]
+        cols = [j, swap_partner(j, self.ny, 0), swap_partner(j, self.ny, 1)]
+        return rows, cols
+
+
+def prepare_kernel(sh, pos_ref, counts_ref, tgt_ref, own_ref):
+    slot = lane_ids(1, sh.slots)
+    for layer in range(sh.layers):
+        live = (slot < counts_ref[0, 0, layer]).astype(F32)
+        at = pl.ds(layer * sh.slots, sh.slots)
+        own_ref[0:3, at] = pos_ref[:, 0, 0, layer, :]
+        own_ref[3:6, at] = live * tgt_ref[:, 0, 0, layer, :]
+        own_ref[6:7, at] = live
+        own_ref[7:8, at] = jnp.zeros_like(live)
+
+
+def terms_kernel(sh, index_ref, row_ref, even_ref, odd_ref, coarse_ref, pay_ref):
+    i, j = lax.axis_index("gx"), lax.axis_index("gy")
+    own = row_ref[0]
+    lane = lane_ids(8, sh.points)
+    row1 = lax.broadcasted_iota(jnp.int32, (8, 1), 0)
+    marks = []
+    for k in range(sh.owned):
+        hit = jnp.where(lane == index_ref[i, j, k], own, 0.0)
+        marks.append(jnp.sum(hit, axis=1, keepdims=True))
+    coords = []
+    for coord in range(3):
+        column = jnp.zeros((8, 1), F32)
+        for k in range(sh.owned):
+            column = jnp.where(row1 == k, marks[k][coord : coord + 1, :], column)
+        coords.append(column)
+
+    def add_column(column, sums):
+        square = jnp.zeros((8, sh.points), F32)
+        for coord in range(3):
+            offset = column[coord : coord + 1, :] - coords[coord]
+            square = square + offset * offset
+        kern = scaled_wendland(16.0 * square)
+        return tuple(
+            total + kern * column[3 + q : 4 + q, :] for q, total in enumerate(sums)
+        )
+
+    sums = tuple(jnp.zeros((8, sh.points), F32) for _ in range(3))
+    for ref in (row_ref, even_ref, odd_ref):
+        sums = lax.fori_loop(0, 3, lambda c, s, ref=ref: add_column(ref[c], s), sums)
+    terms = [jnp.sum(s, axis=1, keepdims=True) * (1.0 / KERN_SCALE) for s in sums]
+    lane8 = lane_ids(8, LANES)
+    first = (i * sh.ny + j) * sh.owned
+    tile = jnp.zeros((8, LANES), F32)
+    for k in range(sh.owned):
+        column = marks[k]
+        for q in range(3):
+            column = jnp.where(row1 == 3 + q, terms[q][k : k + 1, :], column)
+        tile = jnp.where(lane8 == first + k, column, tile)
+    extra = jnp.concatenate([coarse_ref[...], jnp.zeros((4, LANES), F32)], axis=0)
+    for d in range(sh.devices):
+        pay_ref[d, 0:8, :] = tile
+        pay_ref[d, 8:16, :] = extra
+
+
+def build_kernel(sh, row_ref, even_ref, odd_ref, high_ref, low_ref):
+    centre = sh.centre(lax.axis_index("gx"), lax.axis_index("gy"))
+    own = own_features(row_ref[0], centre).astype(BF16)
+
+    def one(ref, group, c):
+        near = near_features(ref[c], centre).T.astype(BF16)
+        for layer, (low, high, offset) in enumerate(sh.blocks):
+            lhs = near[layer * sh.slots : (layer + 1) * sh.slots]
+            for target in range(low, high):
+                square = bf16_dot(lhs, own[:, target * sh.slots : (target + 1) * sh.slots])
+                kern = scaled_wendland(square)
+                head = kern.astype(BF16)
+                at = offset + (target - low) * sh.slots
+                high_ref[group * 3 + c, :, at : at + sh.slots] = head
+                low_ref[group * 3 + c, :, at : at + sh.slots] = (
+                    kern - head.astype(F32)
+                ).astype(BF16)
+        return 0
+
+    for group, ref in enumerate((row_ref, even_ref, odd_ref)):
+        lax.fori_loop(0, 3, lambda c, _, ref=ref, group=group: one(ref, group, c), 0)
+
+
+def apply_column(sh, high_ref, low_ref, c, values, out_ref):
+    head = values.astype(BF16)
+    tail = values - head.astype(F32)
+    both = jnp.concatenate([head.astype(F32), tail], axis=0).astype(BF16)
+    for layer, (low, high, offset) in enumerate(sh.blocks):
+        at = slice(layer * sh.slots, (layer + 1) * sh.slots)
+        width = (high - low) * sh.slots
+        main = bf16_dot(both[:, at], high_ref[c, :, offset : offset + width])
+        rest = bf16_dot(head[:, at], low_ref[c, :, offset : offset + width])
+        out_ref[:, low * sh.slots : high * sh.slots] += main[:8] + main[8:] + rest
+
+
+def gathered_matrix(sh, recv_ref, gram_ref):
+    lane = lane_ids(sh.ny * 4, LANES)
+    width = sh.row_landmarks
+    groups = LANES // width
+    for g in range(groups):
+        total = jnp.zeros((sh.ny * 4, LANES), F32)
+        for i in range(sh.nx):
+            tiles = jnp.concatenate(
+                [recv_ref[i * sh.ny + j, 8:16, :][0:4] for j in range(sh.ny)], axis=0
+            )
+            shift = ((i - g) * width) % LANES
+            if shift:
+                tiles = pltpu.roll(tiles, shift, axis=1)
+            keep = jnp.logical_and(lane >= i * width, lane < (i + 1) * width)
+            total = jnp.where(keep, tiles, total)
+        for j in range(sh.ny):
+            for r in range(4):
+                p = groups * r + g
+                at = (p // sh.owned) * width + j * sh.owned + p % sh.owned
+                gram_ref[at : at + 1, :] = total[j * 4 + r : j * 4 + r + 1, :]
+
+
+def first_kernel(
+    sh, row_ref, even_ref, odd_ref, recv_ref, high_ref, low_ref,
+    pay_ref, search_ref, spread_ref, gram_ref, image_ref, mark_ref,
+):
+    i, j = lax.axis_index("gx"), lax.axis_index("gy")
+    centre = sh.centre(i, j)
+    gathered = recv_ref[0, 0:8, :]
+    for d in range(1, sh.devices):
+        gathered = gathered + recv_ref[d, 0:8, :]
+    gathered_matrix(sh, recv_ref, gram_ref)
+    mark_ref[...] = own_features(gathered, centre).T.astype(BF16)
+    row8 = row_ids(LANES)
+    terms = jnp.where(row8 < 3, jnp.concatenate([gathered[3:8], gathered[0:3]], axis=0), 0.0)
+    coarse = full_dot(terms, gram_ref[...], transposed=True)
+    image_ref[...] = jnp.zeros_like(image_ref)
+    rows, _ = sh.near_ids(i, j)
+    keep3 = row_ids(sh.points) < 3
+    for group, ref in enumerate((row_ref, even_ref, odd_ref)):
+        start = sh.window_start(rows[group])
+        marks = mark_ref[pl.ds(start, sh.window), :]
+        part = pltpu.roll(coarse, lax.rem(LANES - start, LANES), axis=1)[:, : sh.window]
+
+        def one(c, _, ref=ref, group=group, marks=marks, part=part):
+            column = ref[c]
+            near = near_features(column, centre).astype(BF16)
+            spread = scaled_wendland(bf16_dot(marks, near)) * (1.0 / KERN_SCALE)
+            spread_ref[group * 3 + c] = spread
+            residual = jnp.where(
+                keep3, jnp.concatenate([column[3:8], column[0:3]], axis=0), 0.0
+            )
+            search = residual * (1.0 / RIDGE_WEIGHT) + full_dot(part, spread)
+            search_ref[group * 3 + c] = search
+            apply_column(sh, high_ref, low_ref, group * 3 + c, search, image_ref)
+            return 0
+
+        lax.fori_loop(0, 3, one, 0)
+    own = row_ref[0]
+    residual = jnp.where(keep3, jnp.concatenate([own[3:8], own[0:3]], axis=0), 0.0)
+    search = search_ref[0]
+    image = image_ref[...] * (1.0 / KERN_SCALE) + RIDGE_WEIGHT * search
+    image_ref[...] = image
+    gamma = jnp.sum(residual * search, axis=1, keepdims=True)
+    delta = jnp.sum(search * image, axis=1, keepdims=True)
+    window = full_dot(image, spread_ref[0], transposed=True)
+    lane = lane_ids(8, LANES)
+    fill = jnp.zeros((8, LANES - sh.window), F32)
+    tile = jnp.concatenate([window, fill], axis=1)
+    tile = jnp.where(lane == sh.window, gamma, tile)
+    tile = jnp.where(lane == sh.window + 1, delta, tile)
+    for d in range(sh.devices):
+        for q in range(3):
+            pay_ref[d, :, q * sh.points : (q + 1) * sh.points] = image[q : q + 1, :]
+            at = 3 * sh.points + q * LANES
+            pay_ref[d, :, at : at + LANES] = tile[q : q + 1, :]
+
+
+def second_kernel(
+    sh, recv_ref, row_ref, search_ref, spread_ref, gram_ref, image_ref, high_ref, low_ref,
+    pay_ref, residual_ref, next_ref, product_ref,
+):
+    i, j = lax.axis_index("gx"), lax.axis_index("gy")
+    lane = lane_ids(8, LANES)
+    terms = jnp.zeros((8, LANES), F32)
+    scalars = jnp.zeros((8, LANES), F32)
+    fill = jnp.zeros((5, LANES), F32)
+    for a in range(sh.nx):
+        parts = []
+        for q in range(3):
+            at = 3 * sh.points + q * LANES
+            total = recv_ref[a * sh.ny, :, at : at + LANES]
+            for b in range(1, sh.ny):
+                total = total + recv_ref[a * sh.ny + b, :, at : at + LANES]
+            parts.append(total)
+        tile = jnp.concatenate(parts + [fill], axis=0)
+        scalars = scalars + tile
+        start = min(max(a - 1, 0), sh.nx - 3) * sh.row_landmarks
+        tile = jnp.where(lane < sh.window, tile, 0.0)
+        terms = terms + (pltpu.roll(tile, start, axis=1) if start else tile)
+    gamma = scalars[:, sh.window : sh.window + 1]
+    delta = scalars[:, sh.window + 1 : sh.window + 2]
+    row1 = lax.broadcasted_iota(jnp.int32, (8, 1), 0)
+    alpha = jnp.where(row1 < 3, gamma / jnp.where(row1 < 3, delta, 1.0), 0.0)
+    coarse = full_dot(terms, gram_ref[...], transposed=True)
+    product_ref[...] = jnp.zeros_like(product_ref)
+    rows, cols = sh.near_ids(i, j)
+    zeros5 = jnp.zeros((5, sh.points), F32)
+    for group in range(3):
+        start = sh.window_start(rows[group])
+        part = pltpu.roll(coarse, lax.rem(LANES - start, LANES), axis=1)[:, : sh.window]
+        for c in range(3):
+            at = group * 3 + c
+            source = rows[group] * sh.ny + cols[c]
+            image = jnp.concatenate(
+                [recv_ref[source, :, q * sh.points : (q + 1) * sh.points] for q in range(3)]
+                + [zeros5],
+                axis=0,
+            )
+            step = image * (1.0 / RIDGE_WEIGHT) + full_dot(part, spread_ref[at])
+            search = search_ref[at] - alpha * step
+            if at == 0:
+                next_ref[...] = search
+            apply_column(sh, high_ref, low_ref, at, search, product_ref)
+    own = row_ref[0]
+    keep3 = row_ids(sh.points) < 3
+    residual = jnp.where(keep3, jnp.concatenate([own[3:8], own[0:3]], axis=0), 0.0)
+    image = image_ref[...]
+    residual = residual - alpha * image
+    residual_ref[...] = residual
+    search = next_ref[...]
+    product = product_ref[...] * (1.0 / KERN_SCALE) + RIDGE_WEIGHT * search
+    product_ref[...] = product
+    sums = [
+        jnp.sum(residual * search, axis=1, keepdims=True),
+        jnp.sum(search * product, axis=1, keepdims=True),
+        jnp.sum(search * image, axis=1, keepdims=True)
+        + jnp.sum(search_ref[0] * product, axis=1, keepdims=True),
+        gamma,
+        delta,
+    ]
+    tile = jnp.zeros((8, LANES), F32)
+    for at, value in enumerate(sums):
+        tile = jnp.where(lane == at, value, tile)
+    for d in range(sh.devices):
+        pay_ref[d] = tile
+
+
+def last_kernel(
+    sh, recv_ref, sums_ref, search_ref, image_ref, residual_ref, next_ref, product_ref,
+    solution_ref, final_ref,
+):
+    total = recv_ref[0]
+    for d in range(1, sh.devices):
+        total = total + recv_ref[d]
+    own = sums_ref[0]
+    row1 = lax.broadcasted_iota(jnp.int32, (8, 1), 0)
+    good = row1 < 3
+    gamma, delta = own[:, 3:4], own[:, 4:5]
+    gamma_new, inner, cross = total[:, 0:1], total[:, 1:2], total[:, 2:3]
+    safe_gamma = jnp.where(good, gamma, 1.0)
+    safe_delta = jnp.where(good, delta, 1.0)
+    alpha = gamma / safe_delta
+    beta = gamma_new / safe_gamma
+    curve = inner + beta * cross + beta * beta * delta
+    step = gamma_new / jnp.where(good, curve, 1.0)
+    direction = next_ref[...] + beta * search_ref[0]
+    image = product_ref[...] + beta * image_ref[...]
+    solution = alpha * search_ref[0] + step * direction
+    residual = residual_ref[...] - step * image
+    for layer in range(sh.layers):
+        at = slice(layer * sh.slots, (layer + 1) * sh.slots)
+        solution_ref[:, 0, 0, layer, :] = solution[0:3, at]
+        final_ref[:, 0, 0, layer, :] = residual[0:3, at]
+
+
+def local_fast(positions, counts, targets, landmark_index, coarse_matrix):
+    both = ("gx", "gy")
+    sh = Shape(positions, landmark_index, lax.axis_size("gx"), lax.axis_size("gy"))
+    field = jax.ShapeDtypeStruct((8, sh.points), F32)
+    vmem = pl.BlockSpec(memory_space=pltpu.VMEM)
+    smem = pl.BlockSpec(memory_space=pltpu.SMEM)
+
+    def call(kernel, name, out_shape, in_specs, cost=10**6, limit=VMEM_BYTES, scratch=()):
+        return pl.pallas_call(
+            functools.partial(kernel, sh),
+            out_shape=out_shape,
+            in_specs=in_specs,
+            out_specs=jax.tree.map(lambda _: vmem, out_shape),
+            scratch_shapes=scratch,
+            name=name,
+            compiler_params=pltpu.CompilerParams(vmem_limit_bytes=limit),
+            cost_estimate=pl.CostEstimate(flops=cost, bytes_accessed=10**5, transcendentals=0),
+        )
+
+    def exchange(payload):
+        return lax.all_to_all(payload, both, 0, 0)
+
+    own = call(prepare_kernel, "prepare", field, [vmem, smem, vmem])(
+        positions, counts, targets
+    )
+    row = jnp.stack([own, swap(own, "gy", 0), swap(own, "gy", 1)])
+    even, odd = swap(row, "gx", 0), swap(row, "gx", 1)
+    coarse_rows = coarse_matrix.reshape(coarse_matrix.size // LANES, LANES)
+
+    terms = call(
+        terms_kernel,
+        "terms",
+        jax.ShapeDtypeStruct((sh.devices, 16, LANES), F32),
+        [smem, vmem, vmem, vmem, vmem],
+    )(landmark_index, row, even, odd, coarse_rows)
+    terms = exchange(terms)
+
+    kern = jax.ShapeDtypeStruct((9, sh.slots, sh.pairs), BF16)
+    high, low = call(
+        build_kernel, "build", (kern, kern), [vmem] * 3, cost=2 * 10**10
+    )(row, even, odd)
+
+    wide = 3 * sh.points + 3 * LANES
+    payload, search, spread, gram, image = call(
+        first_kernel,
+        "first",
+        (
+            jax.ShapeDtypeStruct((sh.devices, 1, wide), F32),
+            jax.ShapeDtypeStruct((9, 8, sh.points), F32),
+            jax.ShapeDtypeStruct((9, sh.window, sh.points), F32),
+            jax.ShapeDtypeStruct((sh.landmarks, LANES), F32),
+            field,
+        ),
+        [vmem] * 6,
+        scratch=[pltpu.VMEM((sh.landmarks, 48), BF16)],
+    )(row, even, odd, terms, high, low)
+    images = exchange(payload)
+
+    sums, residual, following, product = call(
+        second_kernel,
+        "second",
+        (jax.ShapeDtypeStruct((sh.devices, 8, LANES), F32), field, field, field),
+        [vmem] * 8,
+    )(images, row, search, spread, gram, image, high, low)
+    totals = exchange(sums)
+
+    out = jax.ShapeDtypeStruct(targets.shape, F32)
+    return call(last_kernel, "last", (out, out), [vmem] * 7)(
+        totals, sums, search, image, residual, following, product
+    )
+
+
+def local(positions, counts, targets, landmark_index, coarse_matrix):
+    nx, ny = lax.axis_size("gx"), lax.axis_size("gy")
+    landmarks = nx * ny * landmark_index.shape[2]
+    if landmarks == LANES and nx >= 3 and targets.shape[0] == 3:
+        return local_fast(positions, counts, targets, landmark_index, coarse_matrix)
+    return local_plain(positions, counts, targets, landmark_index, coarse_matrix)
+
+
 def solution(mesh):
     return jax.shard_map(
         local,

time: 364 us -> 106 us (0.29); the launches traced: 359 us -> 105 us
  blocking collectives: 178 us -> 30.5 us
  matrix products: 68.3 us -> 0 us
  Pallas kernels: 0 us -> 43.4 us
  starting transfers between devices: 56.6 us -> 15 us
  waiting for transfers between devices: 37.2 us -> 3.54 us
    psum x3 -> x0, blocking collectives: 121 us -> none  [global_inner(): return lax.psum(values, ('gx', 'gy'))]
    dot_general x14 -> x0, matrix products: 68.3 us -> none  [the longest x8 65.5 us: local(): jnp.einsum('bn,qn->qb', kern, near_values, precision=HIGHEST_PRECISION)]
    ppermute x28 -> x4, starting transfers between devices: 56.6 us -> 10.1 us  [swap(): return lax.ppermute(x, axis, pairs)]
    pallas_call x0 -> x6, Pallas kernels: none -> 43.4 us  [the longest x1 18.1 us: local_fast(): call(build_kernel, 'build', (kern, kern), [vmem] * 3, cost=2 * 10 ** 10)]
    unnamed x2 -> x0, blocking collectives: 42.8 us -> none
    ppermute x28 -> x4, waiting for transfers between devices: 37.2 us -> 3.54 us  [swap(): return lax.ppermute(x, axis, pairs)]
    all_to_all x0 -> x2, blocking collectives: none -> 30.5 us  [exchange(): return lax.all_to_all(payload, both, 0, 0)]
    all_gather x2 -> x0, blocking collectives: 13.8 us -> none  [coarse_solve(): row_terms = lax.all_gather(terms, 'gy', axis=0, tiled=True)]
  transfers between devices with their start and end apart: 28 -> 5, of which waited for: 13 -> 2; matrix products, arithmetic and copies ran while one was open for 4% -> 2% of each run, Pallas kernels for 0% -> 17%
where the time goes in v1:
time: 106 us; the launch traced here: 105 us
  Pallas kernels  43.4 us (41%)
  blocking collectives  30.5 us (29%)
  starting transfers between devices  15 us (14%)
  local copies, waits for them, and re-layouts  12.4 us (12%)
  waiting for transfers between devices  3.54 us (3%)
    all_to_all x2, blocking collectives, exchange(): return lax.all_to_all(payload, both, 0, 0)  30.5 us
    pallas_call x1, Pallas kernels, local_fast(): call(build_kernel, 'build', (kern, kern), [vmem] * 3, cost=2 * 10 ** 10)  18.1 us
    pallas_call x1, Pallas kernels, local_fast(): call(first_kernel, 'first', (jax.ShapeDtypeStruct((sh.devices, 1, wide),...  12.5 us
    unnamed x14, local copies, waits for them, and re-layouts  12.3 us
    ppermute x4, starting transfers between devices, swap(): return lax.ppermute(x, axis, pairs)  10.1 us
    pallas_call x1, Pallas kernels, local_fast(): call(second_kernel, 'second', (jax.ShapeDtypeStruct((sh.devices, 8, LANES...  9.3 us
    all_to_all x1, starting transfers between devices, exchange(): return lax.all_to_all(payload, both, 0, 0)  4.9 us
    ppermute x4, waiting for transfers between devices, swap(): return lax.ppermute(x, axis, pairs)  3.54 us
  transfers between devices with their start and end apart: 5, of which 2 were waited for; matrix products, arithmetic and copies ran while one was open for 2% of the time, Pallas kernels for 17%

profile of v1, /device:TPU:0, one launch (start us, length us, event | category | flops | bytes accessed | tf_op | source)
XLA Modules:
  0.0 105.5 jit_solution(6896756336701307654)
XLA Ops:
  0.6 0.0 copy-start.3
  0.6 0.7 copy-done.3
  1.3 0.0 copy-start.4
  1.3 0.7 copy-done.4
  2.0 0.0 copy-start.5
  2.0 0.7 copy-done.5
  2.7 0.6 prepare.1
  3.3 0.7 collective-permute-start.1
  3.9 4.4 %collective-permute-start = (f32[8,1024]{1,0:T(8,128)S(1)}, f32[8,1024]{1,0:T(8,128)S(1)}, u32[]{:S(2)}, u32[]{:S(2)}) collective-permute-start(f32[8,1024]{1,0:T(8,128)S(1)} %prepare.1), channel_id=1, source_target_pairs={{0,1},{1,0},{2,3},{3,2},{4,5},{5,4},{6,7},{7,6},{8,9},{9,8},{10,11... | collective-permute-start | bytes 98312 | tf_op jit(solution)/shard_map/ppermute | solution.py:213
  8.3 0.0 collective-permute-done.1
  8.3 0.9 collective-permute-done
  9.2 0.7 collective-permute-start.3
  9.9 4.3 %collective-permute-start.2 = (f32[3,8,1024]{2,1,0:T(8,128)S(1)}, f32[3,8,1024]{2,1,0:T(8,128)S(1)}, u32[]{:S(2)}, u32[]{:S(2)}) collective-permute-start(f32[3,8,1024]{2,1,0:T(8,128)S(1)} %pad_maximum_fusion.row_ref), channel_id=1, source_target_pairs={{0,4},{4,0},{8,12},{12,8},{16,20},{20,16},{24,28},{28,24},{1,5},{5... | collective-permute-start | bytes 294920 | tf_op jit(solution)/shard_map/ppermute | solution.py:213
  14.2 0.8 copy.10.index_ref
  15.0 0.8 copy.9
  15.8 0.1 reshape.7.coarse_ref
  15.9 0.0 collective-permute-done.3.odd_ref
  15.9 2.7 %collective-permute-done.2.even_ref = f32[3,8,1024]{2,1,0:T(8,128)S(1)} collective-permute-done((f32[3,8,1024]{2,1,0:T(8,128)S(1)}, f32[3,8,1024]{2,1,0:T(8,128)S(1)}, u32[]{:S(2)}, u32[]{:S(2)}) %collective-permute-start.2) | collective-permute-done | bytes 98336 | tf_op jit(solution)/shard_map/ppermute | solution.py:213
  18.5 2.1 %terms.1 = f32[32,16,128]{2,1,0:T(8,128)} custom-call(s32[8,4,4]{2,1,0:T(4,128)S(1)} %copy.10.index_ref, f32[3,8,1024]{2,1,0:T(8,128)S(1)} %pad_maximum_fusion.row_ref, f32[3,8,1024]{2,1,0:T(8,128)S(1)} %collective-permute-done.2.even_ref, f32[3,8,1024]{2,1,0:T(8,128)S(1)} %collective-permute-done.3.odd_ref, f32[4,128]{1,0:T(4,128)S(1)} %reshape.7.coarse_ref), custom_call_target="tpu_custom_call" | custom-call | flops 1000000 | bytes 100000 | tf_op jit(solution)/shard_map/terms/pallas_call | solution.py:542
  20.6 4.9 %all-to-all-start = ((f32[32,16,128]{2,1,0:T(8,128)}), f32[32,16,128]{2,1,0:T(8,128)S(1)}, u32[]{:S(2)}, u32[]{:S(2)}) async-start(f32[32,16,128]{2,1,0:T(8,128)} %terms.1), calls=%async_computation | async-start | bytes 524288 | tf_op jit(solution)/shard_map/all_to_all | solution.py:533
  25.5 18.1 %build.1 = (bf16[9,256,2560]{2,1,0:T(8,128)(2,1)S(1)}, bf16[9,256,2560]{2,1,0:T(8,128)(2,1)}) custom-call(f32[3,8,1024]{2,1,0:T(8,128)S(1)} %pad_maximum_fusion.row_ref, f32[3,8,1024]{2,1,0:T(8,128)S(1)} %collective-permute-done.2.even_ref, f32[3,8,1024]{2,1,0:T(8,128)S(1)} %collective-permute-done.3.odd_ref), custom_call_target="tpu_custom_call" | custom-call | flops 20000000000 | bytes 100000 | tf_op jit(solution)/shard_map/build/pallas_call | solution.py:551
  43.6 0.0 copy-start
  43.6 4.3 %copy-done = bf16[9,256,2560]{2,1,0:T(8,128)(2,1)} copy-done((bf16[9,256,2560]{2,1,0:T(8,128)(2,1)}, bf16[9,256,2560]{2,1,0:T(8,128)(2,1)S(1)}, u32[]{:S(2)}) %copy-start) | copy-done | bytes 11796504
  47.9 0.0 all-to-all-done.recv_ref
  47.9 0.0 copy-start.1
  47.9 4.4 %copy-done.1 = bf16[9,256,2560]{2,1,0:T(8,128)(2,1)S(1)} copy-done((bf16[9,256,2560]{2,1,0:T(8,128)(2,1)S(1)}, bf16[9,256,2560]{2,1,0:T(8,128)(2,1)}, u32[]{:S(2)}) %copy-start.1) | copy-done | bytes 11796504
  52.2 0.0 copy-start.2
  52.2 12.5 %first.1 = (f32[32,1,3456]{2,1,0:T(1,128)S(1)}, f32[9,8,1024]{2,1,0:T(8,128)S(1)}, f32[9,48,1024]{2,1,0:T(8,128)S(1)}, f32[128,128]{1,0:T(8,128)S(1)}, f32[8,1024]{1,0:T(8,128)S(1)}) custom-call(f32[3,8,1024]{2,1,0:T(8,128)S(1)} %pad_maximum_fusion.row_ref, f32[3,8,1024]{2,1,0:T(8,128)S(1)} %collective-permute-done.2.even_ref, ...), custom_call_target="tpu_custom_call" | custom-call | flops 1000000 | bytes 100000 | tf_op jit(solution)/shard_map/first/pallas_call | solution.py:556
  64.8 19.8 %all_to_all.15.recv_ref = f32[32,1,3456]{2,1,0:T(1,128)S(1)} all-to-all(f32[32,1,3456]{2,1,0:T(1,128)S(1)} %get-tuple-element.15), channel_id=1, replica_groups=mesh['gx'=8,'gy'=4] {'gx','gy'}, dimensions={0} | all-to-all | bytes 884736 | tf_op jit(solution)/shard_map/all_to_all | solution.py:533
  84.5 0.0 copy-done.2
  84.5 9.3 %second.1 = (f32[32,8,128]{2,1,0:T(8,128)S(1)}, f32[8,1024]{1,0:T(8,128)S(1)}, f32[8,1024]{1,0:T(8,128)S(1)}, f32[8,1024]{1,0:T(8,128)S(1)}) custom-call(f32[32,1,3456]{2,1,0:T(1,128)S(1)} %all_to_all.15.recv_ref, f32[3,8,1024]{2,1,0:T(8,128)S(1)} %pad_maximum_fusion.row_ref, f32[9,8,1024]{2,1,0:T(8,128)S(1)} %get-tuple-element.16.search_ref, ...), custom_call_target="tpu_custom_call" | custom-call | flops 1000000 | bytes 100000 | tf_op jit(solution)/shard_map/second/pallas_call | solution.py:571
  93.9 10.7 %all_to_all.16.recv_ref = f32[32,8,128]{2,1,0:T(8,128)S(1)} all-to-all(f32[32,8,128]{2,1,0:T(8,128)S(1)} %get-tuple-element.20.sums_ref), channel_id=1, replica_groups=mesh['gx'=8,'gy'=4] {'gx','gy'}, dimensions={0} | all-to-all | bytes 262144 | tf_op jit(solution)/shard_map/all_to_all | solution.py:533
  104.6 0.9 last.1
  (1 shorter events, 0.0 us)
Async XLA Ops:
  0.6 0.7 copy-start.3
  1.3 0.7 copy-start.4
  2.0 0.7 copy-start.5
  3.3 5.1 %collective-permute-start.1 = (f32[8,1024]{1,0:T(8,128)S(1)}, f32[8,1024]{1,0:T(8,128)S(1)}, u32[]{:S(2)}, u32[]{:S(2)}) collective-permute-start(f32[8,1024]{1,0:T(8,128)S(1)} %prepare.1), channel_id=1, source_target_pairs={{1,2},{2,1},{5,6},{6,5},{9,10},{10,9},{13,14},{14,13},{17,18},{18,... | collective-permute-start | bytes 98312 | tf_op jit(solution)/shard_map/ppermute | solution.py:213
  3.9 5.3 %collective-permute-start = (f32[8,1024]{1,0:T(8,128)S(1)}, f32[8,1024]{1,0:T(8,128)S(1)}, u32[]{:S(2)}, u32[]{:S(2)}) collective-permute-start(f32[8,1024]{1,0:T(8,128)S(1)} %prepare.1), channel_id=1, source_target_pairs={{0,1},{1,0},{2,3},{3,2},{4,5},{5,4},{6,7},{7,6},{8,9},{9,8},{10,11... | collective-permute-start | bytes 98312 | tf_op jit(solution)/shard_map/ppermute | solution.py:213
  9.2 6.7 %collective-permute-start.3 = (f32[3,8,1024]{2,1,0:T(8,128)S(1)}, f32[3,8,1024]{2,1,0:T(8,128)S(1)}, u32[]{:S(2)}, u32[]{:S(2)}) collective-permute-start(f32[3,8,1024]{2,1,0:T(8,128)S(1)} %pad_maximum_fusion.row_ref), channel_id=1, source_target_pairs={{4,8},{8,4},{12,16},{16,12},{20,24},{24,20},{5,9},{9,5},{13,17},{1... | collective-permute-start | bytes 294920 | tf_op jit(solution)/shard_map/ppermute | solution.py:213
  9.9 8.7 %collective-permute-start.2 = (f32[3,8,1024]{2,1,0:T(8,128)S(1)}, f32[3,8,1024]{2,1,0:T(8,128)S(1)}, u32[]{:S(2)}, u32[]{:S(2)}) collective-permute-start(f32[3,8,1024]{2,1,0:T(8,128)S(1)} %pad_maximum_fusion.row_ref), channel_id=1, source_target_pairs={{0,4},{4,0},{8,12},{12,8},{16,20},{20,16},{24,28},{28,24},{1,5},{5... | collective-permute-start | bytes 294920 | tf_op jit(solution)/shard_map/ppermute | solution.py:213
  20.6 27.3 %all-to-all-start = ((f32[32,16,128]{2,1,0:T(8,128)}), f32[32,16,128]{2,1,0:T(8,128)S(1)}, u32[]{:S(2)}, u32[]{:S(2)}) async-start(f32[32,16,128]{2,1,0:T(8,128)} %terms.1), calls=%async_computation | async-start | bytes 524288 | tf_op jit(solution)/shard_map/all_to_all | solution.py:533
  43.6 4.3 %copy-start = (bf16[9,256,2560]{2,1,0:T(8,128)(2,1)}, bf16[9,256,2560]{2,1,0:T(8,128)(2,1)S(1)}, u32[]{:S(2)}) copy-start(bf16[9,256,2560]{2,1,0:T(8,128)(2,1)S(1)} %get-tuple-element.13.high_ref) | copy-start | bytes 35389444
  47.9 4.4 %copy-start.1 = (bf16[9,256,2560]{2,1,0:T(8,128)(2,1)S(1)}, bf16[9,256,2560]{2,1,0:T(8,128)(2,1)}, u32[]{:S(2)}) copy-start(bf16[9,256,2560]{2,1,0:T(8,128)(2,1)} %copy-done) | copy-start | bytes 35389444
  52.2 32.3 %copy-start.2 = (bf16[9,256,2560]{2,1,0:T(8,128)(2,1)S(1)}, bf16[9,256,2560]{2,1,0:T(8,128)(2,1)}, u32[]{:S(2)}) copy-start(bf16[9,256,2560]{2,1,0:T(8,128)(2,1)} %copy-done) | copy-start | bytes 35389444

commit v2 on v1

--- a/solution.py
+++ b/solution.py
@@ -18,7 +18,7 @@
 LANES = 128
 FAR = 4096.0
 KERN_SCALE = 256.0
-VMEM_BYTES = 34 * 2**20
+VMEM_BYTES = 24 * 2**20
 
 
 def with_halo(x, sides, width):
@@ -545,7 +545,7 @@
         jax.ShapeDtypeStruct((sh.devices, 16, LANES), F32),
         [smem, vmem, vmem, vmem, vmem],
     )(landmark_index, row, even, odd, coarse_rows)
-    terms = exchange(terms)
+    terms, row, even, odd = lax.optimization_barrier((exchange(terms), row, even, odd))
 
     kern = jax.ShapeDtypeStruct((9, sh.slots, sh.pairs), BF16)
     high, low = call(

time: 106 us -> 90.3 us (0.85)
  Pallas kernels: 43.4 us -> 29.5 us
  blocking collectives: 30.5 us -> 42.3 us
  local copies, waits for them, and re-layouts: 12.4 us -> 3.71 us
  starting transfers between devices: 15 us -> 10.1 us
    all_to_all x2 -> x3, blocking collectives: 30.5 us -> 42.3 us  [exchange(): return lax.all_to_all(payload, both, 0, 0)]
    unnamed x14 -> x8, local copies, waits for them, and re-layouts: 12.3 us -> 3.62 us
    all_to_all x1 -> x0, starting transfers between devices: 4.9 us -> none  [exchange(): return lax.all_to_all(payload, both, 0, 0)]
    pallas_call x1, Pallas kernels: 12.5 us -> 8.04 us  [local_fast(): call(first_kernel, 'first', (jax.ShapeDtypeStruct((sh.devices, 1, wide),...]
    pallas_call x1, Pallas kernels: 18.1 us -> 13.7 us  [local_fast(): call(build_kernel, 'build', (kern, kern), [vmem] * 3, cost=2 * 10 ** 10)]
    pallas_call x1, Pallas kernels: 9.3 us -> 4.95 us  [local_fast(): call(second_kernel, 'second', (jax.ShapeDtypeStruct((sh.devices, 8, LANES...]
  transfers between devices with their start and end apart: 5 -> 4, of which waited for: 2 -> 2; matrix products, arithmetic and copies ran while one was open for 2% -> 2% of each run, Pallas kernels for 17% -> 0%
where the time goes in v2:
time: 90.3 us; the launch traced here: 89.8 us
  blocking collectives  42.3 us (47%)
  Pallas kernels  29.5 us (33%)
  starting transfers between devices  10.1 us (11%)
  local copies, waits for them, and re-layouts  3.71 us (4%)
  waiting for transfers between devices  3.54 us (4%)
    all_to_all x3, blocking collectives, exchange(): return lax.all_to_all(payload, both, 0, 0)  42.3 us
    pallas_call x1, Pallas kernels, local_fast(): call(build_kernel, 'build', (kern, kern), [vmem] * 3, cost=2 * 10 ** 10)  13.7 us
    ppermute x4, starting transfers between devices, swap(): return lax.ppermute(x, axis, pairs)  10.1 us
    pallas_call x1, Pallas kernels, local_fast(): call(first_kernel, 'first', (jax.ShapeDtypeStruct((sh.devices, 1, wide),...  8.04 us
    pallas_call x1, Pallas kernels, local_fast(): call(second_kernel, 'second', (jax.ShapeDtypeStruct((sh.devices, 8, LANES...  4.95 us
    unnamed x8, local copies, waits for them, and re-layouts  3.62 us
    ppermute x4, waiting for transfers between devices, swap(): return lax.ppermute(x, axis, pairs)  3.54 us
  transfers between devices with their start and end apart: 4, of which 2 were waited for; matrix products, arithmetic and copies ran while one was open for 2% of the time, Pallas kernels for 0%

profile of v2, /device:TPU:0, one launch (start us, length us, event | category | flops | bytes accessed | tf_op | source)
XLA Modules:
  0.0 89.8 jit_solution(10970290237989357150)
XLA Ops:
  0.6 0.0 copy-start
  0.6 0.7 copy-done
  1.3 0.0 copy-start.1
  1.3 0.7 copy-done.1
  2.0 0.0 copy-start.2
  2.0 0.7 copy-done.2
  2.7 0.6 prepare.1
  3.3 0.7 collective-permute-start.1
  3.9 4.4 %collective-permute-start = (f32[8,1024]{1,0:T(8,128)S(1)}, f32[8,1024]{1,0:T(8,128)S(1)}, u32[]{:S(2)}, u32[]{:S(2)}) collective-permute-start(f32[8,1024]{1,0:T(8,128)S(1)} %prepare.1), channel_id=1, source_target_pairs={{0,1},{1,0},{2,3},{3,2},{4,5},{5,4},{6,7},{7,6},{8,9},{9,8},{10,11... | collective-permute-start | bytes 98312 | tf_op jit(solution)/shard_map/ppermute | solution.py:213
  8.3 0.0 collective-permute-done.1
  8.3 0.9 collective-permute-done
  9.2 0.7 collective-permute-start.3
  9.9 4.3 %collective-permute-start.2 = (f32[3,8,1024]{2,1,0:T(8,128)S(1)}, f32[3,8,1024]{2,1,0:T(8,128)S(1)}, u32[]{:S(2)}, u32[]{:S(2)}) collective-permute-start(f32[3,8,1024]{2,1,0:T(8,128)S(1)} %pad_maximum_fusion.row_ref), channel_id=1, source_target_pairs={{0,4},{4,0},{8,12},{12,8},{16,20},{20,16},{24,28},{28,24},{1,5},{5... | collective-permute-start | bytes 294920 | tf_op jit(solution)/shard_map/ppermute | solution.py:213
  14.2 0.8 copy.10.index_ref
  15.0 0.8 copy.9
  15.8 0.1 reshape.7.coarse_ref
  15.9 0.0 collective-permute-done.3.odd_ref
  15.9 2.7 %collective-permute-done.2.even_ref = f32[3,8,1024]{2,1,0:T(8,128)S(1)} collective-permute-done((f32[3,8,1024]{2,1,0:T(8,128)S(1)}, f32[3,8,1024]{2,1,0:T(8,128)S(1)}, u32[]{:S(2)}, u32[]{:S(2)}) %collective-permute-start.2) | collective-permute-done | bytes 98336 | tf_op jit(solution)/shard_map/ppermute | solution.py:213
  18.5 1.3 %terms.1 = f32[32,16,128]{2,1,0:T(8,128)S(1)} custom-call(s32[8,4,4]{2,1,0:T(4,128)S(1)} %copy.10.index_ref, f32[3,8,1024]{2,1,0:T(8,128)S(1)} %pad_maximum_fusion.row_ref, f32[3,8,1024]{2,1,0:T(8,128)S(1)} %collective-permute-done.2.even_ref, f32[3,8,1024]{2,1,0:T(8,128)S(1)} %collective-permute-done.3.odd_ref, f32[4,128]{1,0:T(4,128)S(1)} %reshape.7.coarse_ref), custom_call_target="tpu_custom_call" | custom-call | flops 1000000 | bytes 100000 | tf_op jit(solution)/shard_map/terms/pallas_call | solution.py:542
  19.9 15.3 %all_to_all.15.recv_ref = f32[32,16,128]{2,1,0:T(8,128)S(1)} all-to-all(f32[32,16,128]{2,1,0:T(8,128)S(1)} %terms.1), channel_id=1, replica_groups=mesh['gx'=8,'gy'=4] {'gx','gy'}, dimensions={0} | all-to-all | bytes 524288 | tf_op jit(solution)/shard_map/all_to_all | solution.py:533
  35.2 13.7 %build.1 = (bf16[9,256,2560]{2,1,0:T(8,128)(2,1)S(1)}, bf16[9,256,2560]{2,1,0:T(8,128)(2,1)S(1)}) custom-call(f32[3,8,1024]{2,1,0:T(8,128)S(1)} %pad_maximum_fusion.row_ref, f32[3,8,1024]{2,1,0:T(8,128)S(1)} %collective-permute-done.2.even_ref, f32[3,8,1024]{2,1,0:T(8,128)S(1)} %collective-permute-done.3.odd_ref), custom_call_target="tpu_custom_call" | custom-call | flops 20000000000 | bytes 100000 | tf_op jit(solution)/shard_map/build/pallas_call | solution.py:551
  48.8 8.0 %first.1 = (f32[32,1,3456]{2,1,0:T(1,128)S(1)}, f32[9,8,1024]{2,1,0:T(8,128)S(1)}, f32[9,48,1024]{2,1,0:T(8,128)S(1)}, f32[128,128]{1,0:T(8,128)S(1)}, f32[8,1024]{1,0:T(8,128)S(1)}) custom-call(f32[3,8,1024]{2,1,0:T(8,128)S(1)} %pad_maximum_fusion.row_ref, f32[3,8,1024]{2,1,0:T(8,128)S(1)} %collective-permute-done.2.even_ref, ...), custom_call_target="tpu_custom_call" | custom-call | flops 1000000 | bytes 100000 | tf_op jit(solution)/shard_map/first/pallas_call | solution.py:556
  56.9 16.3 %all_to_all.16.recv_ref = f32[32,1,3456]{2,1,0:T(1,128)S(1)} all-to-all(f32[32,1,3456]{2,1,0:T(1,128)S(1)} %get-tuple-element.23), channel_id=1, replica_groups=mesh['gx'=8,'gy'=4] {'gx','gy'}, dimensions={0} | all-to-all | bytes 884736 | tf_op jit(solution)/shard_map/all_to_all | solution.py:533
  73.2 4.9 %second.1 = (f32[32,8,128]{2,1,0:T(8,128)S(1)}, f32[8,1024]{1,0:T(8,128)S(1)}, f32[8,1024]{1,0:T(8,128)S(1)}, f32[8,1024]{1,0:T(8,128)S(1)}) custom-call(f32[32,1,3456]{2,1,0:T(1,128)S(1)} %all_to_all.16.recv_ref, f32[3,8,1024]{2,1,0:T(8,128)S(1)} %pad_maximum_fusion.row_ref, f32[9,8,1024]{2,1,0:T(8,128)S(1)} %get-tuple-element.24.search_ref, ...), custom_call_target="tpu_custom_call" | custom-call | flops 1000000 | bytes 100000 | tf_op jit(solution)/shard_map/second/pallas_call | solution.py:571
  78.2 10.7 %all_to_all.17.recv_ref = f32[32,8,128]{2,1,0:T(8,128)S(1)} all-to-all(f32[32,8,128]{2,1,0:T(8,128)S(1)} %get-tuple-element.28.sums_ref), channel_id=1, replica_groups=mesh['gx'=8,'gy'=4] {'gx','gy'}, dimensions={0} | all-to-all | bytes 262144 | tf_op jit(solution)/shard_map/all_to_all | solution.py:533
  88.9 0.9 %last.1 = (f32[3,1,1,4,256]{4,3,2,1,0:T(4,128)}, f32[3,1,1,4,256]{4,3,2,1,0:T(4,128)}) custom-call(f32[32,8,128]{2,1,0:T(8,128)S(1)} %all_to_all.17.recv_ref, f32[32,8,128]{2,1,0:T(8,128)S(1)} %get-tuple-element.28.sums_ref, f32[9,8,1024]{2,1,0:T(8,128)S(1)} %get-tuple-element.24.search_ref, f32[8,1024]{1,0:T(8,128)S(1)} %get-tuple-element.27.image_ref, ...), custom_call_target="tpu_custom_call" | custom-call | flops 1000000 | bytes 100000 | tf_op jit(solution)/shard_map/last/pallas_call | solution.py:580
  (1 shorter events, 0.0 us)
Async XLA Ops:
  0.6 0.7 copy-start
  1.3 0.7 copy-start.1
  2.0 0.7 copy-start.2
  3.3 5.1 %collective-permute-start.1 = (f32[8,1024]{1,0:T(8,128)S(1)}, f32[8,1024]{1,0:T(8,128)S(1)}, u32[]{:S(2)}, u32[]{:S(2)}) collective-permute-start(f32[8,1024]{1,0:T(8,128)S(1)} %prepare.1), channel_id=1, source_target_pairs={{1,2},{2,1},{5,6},{6,5},{9,10},{10,9},{13,14},{14,13},{17,18},{18,... | collective-permute-start | bytes 98312 | tf_op jit(solution)/shard_map/ppermute | solution.py:213
  3.9 5.3 %collective-permute-start = (f32[8,1024]{1,0:T(8,128)S(1)}, f32[8,1024]{1,0:T(8,128)S(1)}, u32[]{:S(2)}, u32[]{:S(2)}) collective-permute-start(f32[8,1024]{1,0:T(8,128)S(1)} %prepare.1), channel_id=1, source_target_pairs={{0,1},{1,0},{2,3},{3,2},{4,5},{5,4},{6,7},{7,6},{8,9},{9,8},{10,11... | collective-permute-start | bytes 98312 | tf_op jit(solution)/shard_map/ppermute | solution.py:213
  9.2 6.7 %collective-permute-start.3 = (f32[3,8,1024]{2,1,0:T(8,128)S(1)}, f32[3,8,1024]{2,1,0:T(8,128)S(1)}, u32[]{:S(2)}, u32[]{:S(2)}) collective-permute-start(f32[3,8,1024]{2,1,0:T(8,128)S(1)} %pad_maximum_fusion.row_ref), channel_id=1, source_target_pairs={{4,8},{8,4},{12,16},{16,12},{20,24},{24,20},{5,9},{9,5},{13,17},{1... | collective-permute-start | bytes 294920 | tf_op jit(solution)/shard_map/ppermute | solution.py:213
  9.9 8.7 %collective-permute-start.2 = (f32[3,8,1024]{2,1,0:T(8,128)S(1)}, f32[3,8,1024]{2,1,0:T(8,128)S(1)}, u32[]{:S(2)}, u32[]{:S(2)}) collective-permute-start(f32[3,8,1024]{2,1,0:T(8,128)S(1)} %pad_maximum_fusion.row_ref), channel_id=1, source_target_pairs={{0,4},{4,0},{8,12},{12,8},{16,20},{20,16},{24,28},{28,24},{1,5},{5... | collective-permute-start | bytes 294920 | tf_op jit(solution)/shard_map/ppermute | solution.py:213

commit v3 on v2

--- a/solution.py
+++ b/solution.py
@@ -18,7 +18,7 @@
 LANES = 128
 FAR = 4096.0
 KERN_SCALE = 256.0
-VMEM_BYTES = 24 * 2**20
+VMEM_BYTES = 8 * 2**20
 
 
 def with_halo(x, sides, width):
@@ -244,7 +244,16 @@
         return rows, cols
 
 
-def prepare_kernel(sh, pos_ref, counts_ref, tgt_ref, own_ref):
+def prepare_kernel(sh, pos_hbm, counts_hbm, tgt_hbm, own_ref, pos_ref, counts_ref, tgt_ref, sems):
+    copies = [
+        pltpu.make_async_copy(counts_hbm, counts_ref, sems.at[0]),
+        pltpu.make_async_copy(pos_hbm, pos_ref, sems.at[1]),
+        pltpu.make_async_copy(tgt_hbm, tgt_ref, sems.at[2]),
+    ]
+    for copy in copies:
+        copy.start()
+    for copy in copies:
+        copy.wait()
     slot = lane_ids(1, sh.slots)
     for layer in range(sh.layers):
         live = (slot < counts_ref[0, 0, layer]).astype(F32)
@@ -255,7 +264,18 @@
         own_ref[7:8, at] = jnp.zeros_like(live)
 
 
-def terms_kernel(sh, index_ref, row_ref, even_ref, odd_ref, coarse_ref, pay_ref):
+def terms_kernel(
+    sh, index_hbm, coarse_hbm, after_ref, row_ref, even_ref, odd_ref, pay_ref,
+    index_ref, coarse_ref, sems,
+):
+    copies = [
+        pltpu.make_async_copy(index_hbm, index_ref, sems.at[0]),
+        pltpu.make_async_copy(coarse_hbm, coarse_ref, sems.at[1]),
+    ]
+    for copy in copies:
+        copy.start()
+    for copy in copies:
+        copy.wait()
     i, j = lax.axis_index("gx"), lax.axis_index("gy")
     own = row_ref[0]
     lane = lane_ids(8, sh.points)
@@ -286,25 +306,33 @@
         sums = lax.fori_loop(0, 3, lambda c, s, ref=ref: add_column(ref[c], s), sums)
     terms = [jnp.sum(s, axis=1, keepdims=True) * (1.0 / KERN_SCALE) for s in sums]
     lane8 = lane_ids(8, LANES)
+    row8 = row_ids(LANES)
+    half = LANES // 2
     first = (i * sh.ny + j) * sh.owned
     tile = jnp.zeros((8, LANES), F32)
     for k in range(sh.owned):
-        column = marks[k]
+        column = jnp.where(row1 < 3, marks[k], 0.0)
         for q in range(3):
             column = jnp.where(row1 == 3 + q, terms[q][k : k + 1, :], column)
         tile = jnp.where(lane8 == first + k, column, tile)
-    extra = jnp.concatenate([coarse_ref[...], jnp.zeros((4, LANES), F32)], axis=0)
+    groups = half // sh.row_landmarks
+    pieces = [coarse_ref[pl.ds(g, 8, stride=groups), :] for g in range(groups)]
+    block = jnp.concatenate(pieces + pieces, axis=1)
+    own_half = (lane8 >= half) == (first >= half)
+    tile = jnp.where(own_half, tile, block)
     for d in range(sh.devices):
-        pay_ref[d, 0:8, :] = tile
-        pay_ref[d, 8:16, :] = extra
-
-
-def build_kernel(sh, row_ref, even_ref, odd_ref, high_ref, low_ref):
+        pay_ref[d] = tile
+
+
+def build_kernel(sh, count, row_ref, *refs):
+    group_refs, (high_ref, low_ref, near_ref) = refs[: count], refs[count :]
     centre = sh.centre(lax.axis_index("gx"), lax.axis_index("gy"))
     own = own_features(row_ref[0], centre).astype(BF16)
 
     def one(ref, group, c):
-        near = near_features(ref[c], centre).T.astype(BF16)
+        features = near_features(ref[c], centre)
+        near_ref[group * 3 + c] = features.astype(BF16)
+        near = features.T.astype(BF16)
         for layer, (low, high, offset) in enumerate(sh.blocks):
             lhs = near[layer * sh.slots : (layer + 1) * sh.slots]
             for target in range(low, high):
@@ -318,14 +346,18 @@
                 ).astype(BF16)
         return 0
 
-    for group, ref in enumerate((row_ref, even_ref, odd_ref)):
+    for group, ref in enumerate(group_refs):
         lax.fori_loop(0, 3, lambda c, _, ref=ref, group=group: one(ref, group, c), 0)
 
 
-def apply_column(sh, high_ref, low_ref, c, values, out_ref):
+def split_rows(values):
     head = values.astype(BF16)
     tail = values - head.astype(F32)
-    both = jnp.concatenate([head.astype(F32), tail], axis=0).astype(BF16)
+    return head, jnp.concatenate([head.astype(F32), tail], axis=0).astype(BF16)
+
+
+def apply_column(sh, high_ref, low_ref, c, values, out_ref):
+    head, both = split_rows(values)
     for layer, (low, high, offset) in enumerate(sh.blocks):
         at = slice(layer * sh.slots, (layer + 1) * sh.slots)
         width = (high - low) * sh.slots
@@ -334,72 +366,95 @@
         out_ref[:, low * sh.slots : high * sh.slots] += main[:8] + main[8:] + rest
 
 
+def spread_dot(part, high, low):
+    head, both = split_rows(part)
+    main = bf16_dot(both, high)
+    return main[:8] + main[8:] + bf16_dot(head, low)
+
+
 def gathered_matrix(sh, recv_ref, gram_ref):
-    lane = lane_ids(sh.ny * 4, LANES)
     width = sh.row_landmarks
-    groups = LANES // width
+    half = LANES // 2
+    groups = half // width
+    lane = lane_ids(sh.ny * 8, LANES)
     for g in range(groups):
-        total = jnp.zeros((sh.ny * 4, LANES), F32)
+        total = jnp.zeros((sh.ny * 8, LANES), F32)
         for i in range(sh.nx):
-            tiles = jnp.concatenate(
-                [recv_ref[i * sh.ny + j, 8:16, :][0:4] for j in range(sh.ny)], axis=0
-            )
-            shift = ((i - g) * width) % LANES
+            tiles = jnp.concatenate([recv_ref[i * sh.ny + j] for j in range(sh.ny)], axis=0)
+            base = half if i * width < half else 0
+            shift = (i * width - base - g * width) % LANES
             if shift:
                 tiles = pltpu.roll(tiles, shift, axis=1)
             keep = jnp.logical_and(lane >= i * width, lane < (i + 1) * width)
             total = jnp.where(keep, tiles, total)
         for j in range(sh.ny):
-            for r in range(4):
+            for r in range(8):
                 p = groups * r + g
                 at = (p // sh.owned) * width + j * sh.owned + p % sh.owned
-                gram_ref[at : at + 1, :] = total[j * 4 + r : j * 4 + r + 1, :]
+                gram_ref[at : at + 1, :] = total[j * 8 + r : j * 8 + r + 1, :]
+
+
+def rhs_rows(column, lanes):
+    return jnp.where(
+        row_ids(lanes) < 3, jnp.concatenate([column[3:8], column[0:3]], axis=0), 0.0
+    )
 
 
 def first_kernel(
-    sh, row_ref, even_ref, odd_ref, recv_ref, high_ref, low_ref,
-    pay_ref, search_ref, spread_ref, gram_ref, image_ref, mark_ref,
+    sh, row_ref, even_ref, odd_ref, recv_ref, near0_ref, near1_ref,
+    high0_ref, low0_ref, high1_ref, low1_ref,
+    pay_ref, search_ref, spread_ref, rest_ref, gram_ref, image_ref, mark_ref,
 ):
     i, j = lax.axis_index("gx"), lax.axis_index("gy")
     centre = sh.centre(i, j)
-    gathered = recv_ref[0, 0:8, :]
-    for d in range(1, sh.devices):
-        gathered = gathered + recv_ref[d, 0:8, :]
+    half = LANES // 2
+    totals = [jnp.zeros((8, LANES), F32), jnp.zeros((8, LANES), F32)]
+    for d in range(sh.devices):
+        side = 0 if d * sh.owned < half else 1
+        totals[side] = totals[side] + recv_ref[d]
+    gathered = jnp.where(lane_ids(8, LANES) < half, totals[0], totals[1])
+    gathered = jnp.where(row_ids(LANES) == 6, 1.0, gathered)
     gathered_matrix(sh, recv_ref, gram_ref)
     mark_ref[...] = own_features(gathered, centre).T.astype(BF16)
-    row8 = row_ids(LANES)
-    terms = jnp.where(row8 < 3, jnp.concatenate([gathered[3:8], gathered[0:3]], axis=0), 0.0)
-    coarse = full_dot(terms, gram_ref[...], transposed=True)
+    coarse = full_dot(rhs_rows(gathered, LANES), gram_ref[...], transposed=True)
     image_ref[...] = jnp.zeros_like(image_ref)
     rows, _ = sh.near_ids(i, j)
-    keep3 = row_ids(sh.points) < 3
     for group, ref in enumerate((row_ref, even_ref, odd_ref)):
         start = sh.window_start(rows[group])
         marks = mark_ref[pl.ds(start, sh.window), :]
         part = pltpu.roll(coarse, lax.rem(LANES - start, LANES), axis=1)[:, : sh.window]
-
-        def one(c, _, ref=ref, group=group, marks=marks, part=part):
-            column = ref[c]
-            near = near_features(column, centre).astype(BF16)
-            spread = scaled_wendland(bf16_dot(marks, near)) * (1.0 / KERN_SCALE)
-            spread_ref[group * 3 + c] = spread
-            residual = jnp.where(
-                keep3, jnp.concatenate([column[3:8], column[0:3]], axis=0), 0.0
-            )
-            search = residual * (1.0 / RIDGE_WEIGHT) + full_dot(part, spread)
+        near_ref = near1_ref if group else near0_ref
+        high_ref = high1_ref if group else high0_ref
+        low_ref = low1_ref if group else low0_ref
+        base = max(group - 1, 0) * 3
+
+        def one(
+            c, _, ref=ref, group=group, marks=marks, part=part,
+            near_ref=near_ref, high_ref=high_ref, low_ref=low_ref, base=base,
+        ):
+            spread = scaled_wendland(bf16_dot(marks, near_ref[base + c])) * (1.0 / KERN_SCALE)
+            head = spread.astype(BF16)
+            rest = (spread - head.astype(F32)).astype(BF16)
+            spread_ref[group * 3 + c] = head
+            rest_ref[group * 3 + c] = rest
+            residual = rhs_rows(ref[c], sh.points)
+            search = residual * (1.0 / RIDGE_WEIGHT) + spread_dot(part, head, rest)
             search_ref[group * 3 + c] = search
-            apply_column(sh, high_ref, low_ref, group * 3 + c, search, image_ref)
+            apply_column(sh, high_ref, low_ref, base + c, search, image_ref)
             return 0
 
         lax.fori_loop(0, 3, one, 0)
-    own = row_ref[0]
-    residual = jnp.where(keep3, jnp.concatenate([own[3:8], own[0:3]], axis=0), 0.0)
+    residual = rhs_rows(row_ref[0], sh.points)
     search = search_ref[0]
     image = image_ref[...] * (1.0 / KERN_SCALE) + RIDGE_WEIGHT * search
     image_ref[...] = image
     gamma = jnp.sum(residual * search, axis=1, keepdims=True)
     delta = jnp.sum(search * image, axis=1, keepdims=True)
-    window = full_dot(image, spread_ref[0], transposed=True)
+    head, both = split_rows(image)
+    across = (((1,), (1,)), ((), ()))
+    main = lax.dot_general(both, spread_ref[0], across, preferred_element_type=F32)
+    tail = lax.dot_general(head, rest_ref[0], across, preferred_element_type=F32)
+    window = main[:8] + main[8:] + tail
     lane = lane_ids(8, LANES)
     fill = jnp.zeros((8, LANES - sh.window), F32)
     tile = jnp.concatenate([window, fill], axis=1)
@@ -413,8 +468,9 @@
 
 
 def second_kernel(
-    sh, recv_ref, row_ref, search_ref, spread_ref, gram_ref, image_ref, high_ref, low_ref,
-    pay_ref, residual_ref, next_ref, product_ref,
+    sh, recv_ref, row_ref, search_ref, spread_ref, rest_ref, gram_ref, image_ref,
+    high0_ref, low0_ref, high1_ref, low1_ref,
+    pay_ref, sums_ref, residual_ref, next_ref, product_ref,
 ):
     i, j = lax.axis_index("gx"), lax.axis_index("gy")
     lane = lane_ids(8, LANES)
@@ -445,6 +501,9 @@
     for group in range(3):
         start = sh.window_start(rows[group])
         part = pltpu.roll(coarse, lax.rem(LANES - start, LANES), axis=1)[:, : sh.window]
+        high_ref = high1_ref if group else high0_ref
+        low_ref = low1_ref if group else low0_ref
+        base = max(group - 1, 0) * 3
         for c in range(3):
             at = group * 3 + c
             source = rows[group] * sh.ny + cols[c]
@@ -453,14 +512,12 @@
                 + [zeros5],
                 axis=0,
             )
-            step = image * (1.0 / RIDGE_WEIGHT) + full_dot(part, spread_ref[at])
+            step = image * (1.0 / RIDGE_WEIGHT) + spread_dot(part, spread_ref[at], rest_ref[at])
             search = search_ref[at] - alpha * step
             if at == 0:
                 next_ref[...] = search
-            apply_column(sh, high_ref, low_ref, at, search, product_ref)
-    own = row_ref[0]
-    keep3 = row_ids(sh.points) < 3
-    residual = jnp.where(keep3, jnp.concatenate([own[3:8], own[0:3]], axis=0), 0.0)
+            apply_column(sh, high_ref, low_ref, base + c, search, product_ref)
+    residual = rhs_rows(row_ref[0], sh.points)
     image = image_ref[...]
     residual = residual - alpha * image
     residual_ref[...] = residual
@@ -472,14 +529,15 @@
         jnp.sum(search * product, axis=1, keepdims=True),
         jnp.sum(search * image, axis=1, keepdims=True)
         + jnp.sum(search_ref[0] * product, axis=1, keepdims=True),
-        gamma,
-        delta,
     ]
-    tile = jnp.zeros((8, LANES), F32)
+    line = jnp.zeros((1, LANES), F32)
+    lane1 = lane_ids(1, LANES)
     for at, value in enumerate(sums):
-        tile = jnp.where(lane == at, value, tile)
+        for q in range(3):
+            line = jnp.where(lane1 == 3 * at + q, value[q : q + 1, :], line)
     for d in range(sh.devices):
-        pay_ref[d] = tile
+        pay_ref[d] = line
+    sums_ref[...] = jnp.where(lane == 0, gamma, jnp.where(lane == 1, delta, 0.0))
 
 
 def last_kernel(
@@ -489,11 +547,18 @@
     total = recv_ref[0]
     for d in range(1, sh.devices):
         total = total + recv_ref[d]
-    own = sums_ref[0]
     row1 = lax.broadcasted_iota(jnp.int32, (8, 1), 0)
     good = row1 < 3
-    gamma, delta = own[:, 3:4], own[:, 4:5]
-    gamma_new, inner, cross = total[:, 0:1], total[:, 1:2], total[:, 2:3]
+
+    def column(at):
+        value = jnp.zeros((8, 1), F32)
+        for q in range(3):
+            value = jnp.where(row1 == q, total[:, 3 * at + q : 3 * at + q + 1], value)
+        return value
+
+    own = sums_ref[...]
+    gamma, delta = own[:, 0:1], own[:, 1:2]
+    gamma_new, inner, cross = column(0), column(1), column(2)
     safe_gamma = jnp.where(good, gamma, 1.0)
     safe_delta = jnp.where(good, delta, 1.0)
     alpha = gamma / safe_delta
@@ -515,77 +580,112 @@
     sh = Shape(positions, landmark_index, lax.axis_size("gx"), lax.axis_size("gy"))
     field = jax.ShapeDtypeStruct((8, sh.points), F32)
     vmem = pl.BlockSpec(memory_space=pltpu.VMEM)
-    smem = pl.BlockSpec(memory_space=pltpu.SMEM)
-
-    def call(kernel, name, out_shape, in_specs, cost=10**6, limit=VMEM_BYTES, scratch=()):
+    anyw = pl.BlockSpec(memory_space=pltpu.HBM)
+
+    def call(kernel, name, out_shape, in_specs, cost=10**6, scratch=()):
         return pl.pallas_call(
-            functools.partial(kernel, sh),
+            kernel,
             out_shape=out_shape,
             in_specs=in_specs,
             out_specs=jax.tree.map(lambda _: vmem, out_shape),
             scratch_shapes=scratch,
             name=name,
-            compiler_params=pltpu.CompilerParams(vmem_limit_bytes=limit),
+            compiler_params=pltpu.CompilerParams(vmem_limit_bytes=VMEM_BYTES),
             cost_estimate=pl.CostEstimate(flops=cost, bytes_accessed=10**5, transcendentals=0),
         )
 
+    def part(kernel, *fixed):
+        return functools.partial(kernel, sh, *fixed)
+
     def exchange(payload):
         return lax.all_to_all(payload, both, 0, 0)
 
-    own = call(prepare_kernel, "prepare", field, [vmem, smem, vmem])(
-        positions, counts, targets
-    )
+    own = call(
+        part(prepare_kernel),
+        "prepare",
+        field,
+        [anyw] * 3,
+        scratch=[
+            pltpu.VMEM(positions.shape, F32),
+            pltpu.SMEM(counts.shape, jnp.int32),
+            pltpu.VMEM(targets.shape, F32),
+            pltpu.SemaphoreType.DMA((3,)),
+        ],
+    )(positions, counts, targets)
     row = jnp.stack([own, swap(own, "gy", 0), swap(own, "gy", 1)])
     even, odd = swap(row, "gx", 0), swap(row, "gx", 1)
-    coarse_rows = coarse_matrix.reshape(coarse_matrix.size // LANES, LANES)
-
+
+    def build(name, *groups):
+        columns = 3 * len(groups)
+        kern = jax.ShapeDtypeStruct((columns, sh.slots, sh.pairs), BF16)
+        near = jax.ShapeDtypeStruct((columns, 48, sh.points), BF16)
+        return call(
+            part(build_kernel, len(groups)),
+            name,
+            (kern, kern, near),
+            [vmem] * (1 + len(groups)),
+            cost=len(groups) * 10**10,
+        )(row, *groups)
+
+    high0, low0, near0 = build("build_row", row)
     terms = call(
-        terms_kernel,
+        part(terms_kernel),
         "terms",
-        jax.ShapeDtypeStruct((sh.devices, 16, LANES), F32),
-        [smem, vmem, vmem, vmem, vmem],
-    )(landmark_index, row, even, odd, coarse_rows)
-    terms, row, even, odd = lax.optimization_barrier((exchange(terms), row, even, odd))
-
-    kern = jax.ShapeDtypeStruct((9, sh.slots, sh.pairs), BF16)
-    high, low = call(
-        build_kernel, "build", (kern, kern), [vmem] * 3, cost=2 * 10**10
-    )(row, even, odd)
+        jax.ShapeDtypeStruct((sh.devices, 8, LANES), F32),
+        [anyw, anyw, anyw, vmem, vmem, vmem],
+        scratch=[
+            pltpu.SMEM(landmark_index.shape, jnp.int32),
+            pltpu.VMEM(coarse_matrix.shape, F32),
+            pltpu.SemaphoreType.DMA((2,)),
+        ],
+    )(landmark_index, coarse_matrix, near0, row, even, odd)
+    terms, even, odd = lax.optimization_barrier((exchange(terms), even, odd))
+    high1, low1, near1 = build("build_rest", even, odd)
 
     wide = 3 * sh.points + 3 * LANES
-    payload, search, spread, gram, image = call(
-        first_kernel,
+    spread_shape = jax.ShapeDtypeStruct((9, sh.window, sh.points), BF16)
+    payload, search, spread, rest, gram, image = call(
+        part(first_kernel),
         "first",
         (
             jax.ShapeDtypeStruct((sh.devices, 1, wide), F32),
             jax.ShapeDtypeStruct((9, 8, sh.points), F32),
-            jax.ShapeDtypeStruct((9, sh.window, sh.points), F32),
+            spread_shape,
+            spread_shape,
             jax.ShapeDtypeStruct((sh.landmarks, LANES), F32),
             field,
         ),
-        [vmem] * 6,
+        [vmem] * 10,
         scratch=[pltpu.VMEM((sh.landmarks, 48), BF16)],
-    )(row, even, odd, terms, high, low)
+    )(row, even, odd, terms, near0, near1, high0, low0, high1, low1)
     images = exchange(payload)
 
-    sums, residual, following, product = call(
-        second_kernel,
-        "second",
-        (jax.ShapeDtypeStruct((sh.devices, 8, LANES), F32), field, field, field),
-        [vmem] * 8,
-    )(images, row, search, spread, gram, image, high, low)
-    totals = exchange(sums)
+    line = jax.ShapeDtypeStruct((sh.devices, 1, LANES), F32)
+    tile = jax.ShapeDtypeStruct((8, LANES), F32)
+    totals, sums, residual, following, product = call(
+        part(second_kernel), "second", (line, tile, field, field, field), [vmem] * 11
+    )(images, row, search, spread, rest, gram, image, high0, low0, high1, low1)
+    totals = exchange(totals)
 
     out = jax.ShapeDtypeStruct(targets.shape, F32)
-    return call(last_kernel, "last", (out, out), [vmem] * 7)(
+    return call(part(last_kernel), "last", (out, out), [vmem] * 7)(
         totals, sums, search, image, residual, following, product
     )
 
 
+def fits_fast(positions, targets, landmark_index, coarse_matrix, nx, ny):
+    owned = landmark_index.shape[2]
+    return (
+        nx * ny * owned == LANES
+        and nx >= 3
+        and targets.shape[0] == 3
+        and coarse_matrix.shape[0] == 8 * (LANES // 2 // (ny * owned))
+    )
+
+
 def local(positions, counts, targets, landmark_index, coarse_matrix):
     nx, ny = lax.axis_size("gx"), lax.axis_size("gy")
-    landmarks = nx * ny * landmark_index.shape[2]
-    if landmarks == LANES and nx >= 3 and targets.shape[0] == 3:
+    if fits_fast(positions, targets, landmark_index, coarse_matrix, nx, ny):
         return local_fast(positions, counts, targets, landmark_index, coarse_matrix)
     return local_plain(positions, counts, targets, landmark_index, coarse_matrix)
 

time: 90.3 us -> 81.9 us (0.907)
  blocking collectives: 42.3 us -> 38.4 us
  waiting for transfers between devices: 3.54 us -> 0.01 us
  Pallas kernels: 29.5 us -> 28.5 us
    all_to_all x3, blocking collectives: 42.3 us -> 38.4 us  [exchange(): return lax.all_to_all(payload, both, 0, 0)]
    ppermute x4, waiting for transfers between devices: 3.54 us -> 0.01 us  [swap(): return lax.ppermute(x, axis, pairs)]
    pallas_call x6 -> x7, Pallas kernels: 29.5 us -> 28.5 us  [the longest x2 13.4 us: build(): call(part(build_kernel, len(groups)), name, (kern, kern, near), [vmem] *...]
  transfers between devices with their start and end apart: 4 -> 4, of which waited for: 2 -> 0; matrix products, arithmetic and copies ran while one was open for 2% -> 2% of each run, Pallas kernels for 0% -> 5%
where the time goes in v3:
time: 81.9 us; the launch traced here: 81.4 us
  blocking collectives  38.4 us (47%)
  Pallas kernels  28.5 us (35%)
  starting transfers between devices  10.1 us (12%)
  local copies, waits for them, and re-layouts  3.62 us (4%)
    all_to_all x3, blocking collectives, exchange(): return lax.all_to_all(payload, both, 0, 0)  38.4 us
    pallas_call x2, Pallas kernels, build(): call(part(build_kernel, len(groups)), name, (kern, kern, near), [vmem] *...  13.4 us
    ppermute x4, starting transfers between devices, swap(): return lax.ppermute(x, axis, pairs)  10.1 us
    pallas_call x1, Pallas kernels, local_fast(): call(part(first_kernel), 'first', (jax.ShapeDtypeStruct((sh.devices, 1, w...  7.47 us
    pallas_call x1, Pallas kernels, local_fast(): call(part(second_kernel), 'second', (line, tile, field, field, field), [v...  4.71 us
    unnamed x8, local copies, waits for them, and re-layouts  3.62 us
  transfers between devices with their start and end apart: 4, of which 0 were waited for; matrix products, arithmetic and copies ran while one was open for 2% of the time, Pallas kernels for 5%

profile of v3, /device:TPU:0, one launch (start us, length us, event | category | flops | bytes accessed | tf_op | source)
XLA Modules:
  0.0 81.4 jit_solution(6837803764509916434)
XLA Ops:
  0.6 0.0 copy-start
  0.6 0.7 copy-done
  1.3 0.0 copy-start.1
  1.3 0.7 copy-done.1
  2.0 0.0 copy-start.2
  2.0 0.7 copy-done.2
  2.7 0.6 prepare.1
  3.3 0.7 collective-permute-start.1
  4.0 4.4 %collective-permute-start = (f32[8,1024]{1,0:T(8,128)S(1)}, f32[8,1024]{1,0:T(8,128)S(1)}, u32[]{:S(2)}, u32[]{:S(2)}) collective-permute-start(f32[8,1024]{1,0:T(8,128)S(1)} %prepare.1), channel_id=1, source_target_pairs={{0,1},{1,0},{2,3},{3,2},{4,5},{5,4},{6,7},{7,6},{8,9},{9,8},{10,11... | collective-permute-start | bytes 98312 | tf_op jit(solution)/shard_map/ppermute | solution.py:213
  8.4 0.8 copy.7.index_hbm
  9.2 0.8 copy.8.coarse_hbm
  9.9 0.0 collective-permute-done.1
  9.9 0.0 collective-permute-done
  10.0 0.7 collective-permute-start.3
  10.6 4.3 %collective-permute-start.2 = (f32[3,8,1024]{2,1,0:T(8,128)S(1)}, f32[3,8,1024]{2,1,0:T(8,128)S(1)}, u32[]{:S(2)}, u32[]{:S(2)}) collective-permute-start(f32[3,8,1024]{2,1,0:T(8,128)S(1)} %pad_maximum_fusion.row_ref.refs_0_), channel_id=1, source_target_pairs={{0,4},{4,0},{8,12},{12,8},{16,20},{20,16},{24,28},{28,24},{1,5},{5... | collective-permute-start | bytes 294920 | tf_op jit(solution)/shard_map/ppermute | solution.py:213
  15.0 4.5 %build_row.1 = (bf16[3,256,2560]{2,1,0:T(8,128)(2,1)S(1)}, bf16[3,256,2560]{2,1,0:T(8,128)(2,1)S(1)}, bf16[3,48,1024]{2,1,0:T(8,128)(2,1)S(1)}) custom-call(f32[3,8,1024]{2,1,0:T(8,128)S(1)} %pad_maximum_fusion.row_ref.refs_0_, f32[3,8,1024]{2,1,0:T(8,128)S(1)} %pad_maximum_fusion.row_ref.refs_0_), custom_call_target="tpu_custom_call" | custom-call | flops 10000000000 | bytes 100000 | tf_op jit(solution)/shard_map/build_row/pallas_call | solution.py:622
  19.4 0.0 collective-permute-done.3.odd_ref.refs_1_
  19.5 0.0 collective-permute-done.2.even_ref.refs_0_
  19.5 1.4 %terms.1 = f32[32,8,128]{2,1,0:T(8,128)S(1)} custom-call(s32[8,4,4]{2,1,0:T(4,128)S(1)} %copy.7.index_hbm, f32[32,16]{1,0:T(8,128)S(1)} %copy.8.coarse_hbm, bf16[3,48,1024]{2,1,0:T(8,128)(2,1)S(1)} %get-tuple-element.22.after_ref.near0_ref, f32[3,8,1024]{2,1,0:T(8,128)S(1)} %pad_maximum_fusion.row_ref.refs_0_, ...), custom_call_target="tpu_custom_call" | custom-call | flops 1000000 | bytes 100000 | tf_op jit(solution)/shard_map/terms/pallas_call | solution.py:631
  20.8 12.8 %all_to_all.15.recv_ref = f32[32,8,128]{2,1,0:T(8,128)S(1)} all-to-all(f32[32,8,128]{2,1,0:T(8,128)S(1)} %terms.1), channel_id=1, replica_groups=mesh['gx'=8,'gy'=4] {'gx','gy'}, dimensions={0} | all-to-all | bytes 262144 | tf_op jit(solution)/shard_map/all_to_all | solution.py:601
  33.6 8.9 %build_rest.1 = (bf16[6,256,2560]{2,1,0:T(8,128)(2,1)S(1)}, bf16[6,256,2560]{2,1,0:T(8,128)(2,1)S(1)}, bf16[6,48,1024]{2,1,0:T(8,128)(2,1)S(1)}) custom-call(f32[3,8,1024]{2,1,0:T(8,128)S(1)} %pad_maximum_fusion.row_ref.refs_0_, f32[3,8,1024]{2,1,0:T(8,128)S(1)} %collective-permute-done.2.even_ref.refs_0_, ...), custom_call_target="tpu_custom_call" | custom-call | flops 20000000000 | bytes 100000 | tf_op jit(solution)/shard_map/build_rest/pallas_call | solution.py:622
  42.5 7.5 %first.1 = (f32[32,1,3456]{2,1,0:T(1,128)S(1)}, f32[9,8,1024]{2,1,0:T(8,128)S(1)}, bf16[9,48,1024]{2,1,0:T(8,128)(2,1)S(1)}, bf16[9,48,1024]{2,1,0:T(8,128)(2,1)...) custom-call(f32[3,8,1024]{2,1,0:T(8,128)S(1)} %pad_maximum_fusion.row_ref.refs_0_, ...), custom_call_target="tpu_custom_call" | custom-call | flops 1000000 | bytes 100000 | tf_op jit(solution)/shard_map/first/pallas_call | solution.py:647
  50.0 15.9 %all_to_all.16.recv_ref = f32[32,1,3456]{2,1,0:T(1,128)S(1)} all-to-all(f32[32,1,3456]{2,1,0:T(1,128)S(1)} %get-tuple-element.31), channel_id=1, replica_groups=mesh['gx'=8,'gy'=4] {'gx','gy'}, dimensions={0} | all-to-all | bytes 884736 | tf_op jit(solution)/shard_map/all_to_all | solution.py:601
  65.9 4.7 %second.1 = (f32[32,1,128]{2,1,0:T(1,128)S(1)}, f32[8,128]{1,0:T(8,128)S(1)}, f32[8,1024]{1,0:T(8,128)S(1)}, f32[8,1024]{1,0:T(8,128)S(1)}, f32[8,1024]{1,0:T(8,128)S(1)}) custom-call(f32[32,1,3456]{2,1,0:T(1,128)S(1)} %all_to_all.16.recv_ref, f32[3,8,1024]{2,1,0:T(8,128)S(1)} %pad_maximum_fusion.row_ref.refs_0_, ...), custom_call_target="tpu_custom_call" | custom-call | flops 1000000 | bytes 100000 | tf_op jit(solution)/shard_map/second/pallas_call | solution.py:665
  70.6 9.7 %all_to_all.17.recv_ref = f32[32,1,128]{2,1,0:T(1,128)S(1)} all-to-all(f32[32,1,128]{2,1,0:T(1,128)S(1)} %get-tuple-element.37), channel_id=1, replica_groups=mesh['gx'=8,'gy'=4] {'gx','gy'}, dimensions={0} | all-to-all | bytes 32768 | tf_op jit(solution)/shard_map/all_to_all | solution.py:601
  80.3 1.1 %last.1 = (f32[3,1,1,4,256]{4,3,2,1,0:T(4,128)}, f32[3,1,1,4,256]{4,3,2,1,0:T(4,128)}) custom-call(f32[32,1,128]{2,1,0:T(1,128)S(1)} %all_to_all.17.recv_ref, f32[8,128]{1,0:T(8,128)S(1)} %get-tuple-element.38.sums_ref, f32[9,8,1024]{2,1,0:T(8,128)S(1)} %get-tuple-element.32.search_ref, f32[8,1024]{1,0:T(8,128)S(1)} %get-tuple-element.36.image_ref, ...), custom_call_target="tpu_custom_call" | custom-call | flops 1000000 | bytes 100000 | tf_op jit(solution)/shard_map/last/pallas_call | solution.py:671
  (1 shorter events, 0.0 us)
Async XLA Ops:
  0.6 0.7 copy-start
  1.3 0.7 copy-start.1
  2.0 0.7 copy-start.2
  3.3 6.6 %collective-permute-start.1 = (f32[8,1024]{1,0:T(8,128)S(1)}, f32[8,1024]{1,0:T(8,128)S(1)}, u32[]{:S(2)}, u32[]{:S(2)}) collective-permute-start(f32[8,1024]{1,0:T(8,128)S(1)} %prepare.1), channel_id=1, source_target_pairs={{1,2},{2,1},{5,6},{6,5},{9,10},{10,9},{13,14},{14,13},{17,18},{18,... | collective-permute-start | bytes 98312 | tf_op jit(solution)/shard_map/ppermute | solution.py:213
  4.0 6.0 %collective-permute-start = (f32[8,1024]{1,0:T(8,128)S(1)}, f32[8,1024]{1,0:T(8,128)S(1)}, u32[]{:S(2)}, u32[]{:S(2)}) collective-permute-start(f32[8,1024]{1,0:T(8,128)S(1)} %prepare.1), channel_id=1, source_target_pairs={{0,1},{1,0},{2,3},{3,2},{4,5},{5,4},{6,7},{7,6},{8,9},{9,8},{10,11... | collective-permute-start | bytes 98312 | tf_op jit(solution)/shard_map/ppermute | solution.py:213
  10.0 9.5 %collective-permute-start.3 = (f32[3,8,1024]{2,1,0:T(8,128)S(1)}, f32[3,8,1024]{2,1,0:T(8,128)S(1)}, u32[]{:S(2)}, u32[]{:S(2)}) collective-permute-start(f32[3,8,1024]{2,1,0:T(8,128)S(1)} %pad_maximum_fusion.row_ref.refs_0_), channel_id=1, source_target_pairs={{4,8},{8,4},{12,16},{16,12},{20,24},{24,20},{5,9},{9,5},{13,17},{1... | collective-permute-start | bytes 294920 | tf_op jit(solution)/shard_map/ppermute | solution.py:213
  10.6 8.8 %collective-permute-start.2 = (f32[3,8,1024]{2,1,0:T(8,128)S(1)}, f32[3,8,1024]{2,1,0:T(8,128)S(1)}, u32[]{:S(2)}, u32[]{:S(2)}) collective-permute-start(f32[3,8,1024]{2,1,0:T(8,128)S(1)} %pad_maximum_fusion.row_ref.refs_0_), channel_id=1, source_target_pairs={{0,4},{4,0},{8,12},{12,8},{16,20},{20,16},{24,28},{28,24},{1,5},{5... | collective-permute-start | bytes 294920 | tf_op jit(solution)/shard_map/ppermute | solution.py:213

commit v4 on v3

--- a/solution.py
+++ b/solution.py
@@ -244,11 +244,21 @@
         return rows, cols
 
 
-def prepare_kernel(sh, pos_hbm, counts_hbm, tgt_hbm, own_ref, pos_ref, counts_ref, tgt_ref, sems):
+def prepare_kernel(
+    sh, pos_hbm, counts_hbm, tgt_hbm, index_hbm, coarse_hbm, own_ref, mark_ref, block_ref,
+    pos_ref, counts_ref, tgt_ref, index_ref, coarse_ref, turned_ref, sems,
+):
     copies = [
-        pltpu.make_async_copy(counts_hbm, counts_ref, sems.at[0]),
-        pltpu.make_async_copy(pos_hbm, pos_ref, sems.at[1]),
-        pltpu.make_async_copy(tgt_hbm, tgt_ref, sems.at[2]),
+        pltpu.make_async_copy(source, target, sems.at[at])
+        for at, (source, target) in enumerate(
+            (
+                (counts_hbm, counts_ref),
+                (pos_hbm, pos_ref),
+                (tgt_hbm, tgt_ref),
+                (index_hbm, index_ref),
+                (coarse_hbm, coarse_ref),
+            )
+        )
     ]
     for copy in copies:
         copy.start()
@@ -262,28 +272,29 @@
         own_ref[3:6, at] = live * tgt_ref[:, 0, 0, layer, :]
         own_ref[6:7, at] = live
         own_ref[7:8, at] = jnp.zeros_like(live)
+    i, j = lax.axis_index("gx"), lax.axis_index("gy")
+    own = own_ref[...]
+    lane = lane_ids(8, sh.points)
+    lane8 = lane_ids(8, LANES)
+    marks = jnp.zeros((8, LANES), F32)
+    for k in range(sh.owned):
+        hit = jnp.where(lane == index_ref[j, k, i], own, 0.0)
+        marks = jnp.where(lane8 == k, jnp.sum(hit, axis=1, keepdims=True), marks)
+    mark_ref[...] = marks
+    count, width = coarse_ref.shape[1], coarse_ref.shape[0]
+    fill = jnp.zeros((width, LANES - count), F32)
+    turned_ref[...] = jnp.concatenate([coarse_ref[...], fill], axis=1).T
+    groups = LANES // 2 // width
+    pieces = [turned_ref[pl.ds(g, 8, stride=groups), :] for g in range(groups)]
+    block_ref[...] = jnp.concatenate(pieces + pieces, axis=1)
 
 
 def terms_kernel(
-    sh, index_hbm, coarse_hbm, after_ref, row_ref, even_ref, odd_ref, pay_ref,
-    index_ref, coarse_ref, sems,
+    sh, after_ref, mark_ref, block_ref, row_ref, even_ref, odd_ref, pay_ref,
 ):
-    copies = [
-        pltpu.make_async_copy(index_hbm, index_ref, sems.at[0]),
-        pltpu.make_async_copy(coarse_hbm, coarse_ref, sems.at[1]),
-    ]
-    for copy in copies:
-        copy.start()
-    for copy in copies:
-        copy.wait()
     i, j = lax.axis_index("gx"), lax.axis_index("gy")
-    own = row_ref[0]
-    lane = lane_ids(8, sh.points)
     row1 = lax.broadcasted_iota(jnp.int32, (8, 1), 0)
-    marks = []
-    for k in range(sh.owned):
-        hit = jnp.where(lane == index_ref[i, j, k], own, 0.0)
-        marks.append(jnp.sum(hit, axis=1, keepdims=True))
+    marks = [mark_ref[:, k : k + 1] for k in range(sh.owned)]
     coords = []
     for coord in range(3):
         column = jnp.zeros((8, 1), F32)
@@ -315,9 +326,7 @@
         for q in range(3):
             column = jnp.where(row1 == 3 + q, terms[q][k : k + 1, :], column)
         tile = jnp.where(lane8 == first + k, column, tile)
-    groups = half // sh.row_landmarks
-    pieces = [coarse_ref[pl.ds(g, 8, stride=groups), :] for g in range(groups)]
-    block = jnp.concatenate(pieces + pieces, axis=1)
+    block = block_ref[...]
     own_half = (lane8 >= half) == (first >= half)
     tile = jnp.where(own_half, tile, block)
     for d in range(sh.devices):
@@ -330,9 +339,9 @@
     own = own_features(row_ref[0], centre).astype(BF16)
 
     def one(ref, group, c):
-        features = near_features(ref[c], centre)
-        near_ref[group * 3 + c] = features.astype(BF16)
-        near = features.T.astype(BF16)
+        features = near_features(ref[c], centre).astype(BF16)
+        near_ref[group * 3 + c] = features
+        near = features.T
         for layer, (low, high, offset) in enumerate(sh.blocks):
             lhs = near[layer * sh.slots : (layer + 1) * sh.slots]
             for target in range(low, high):
@@ -341,6 +350,7 @@
                 head = kern.astype(BF16)
                 at = offset + (target - low) * sh.slots
                 high_ref[group * 3 + c, :, at : at + sh.slots] = head
+                head = high_ref[group * 3 + c, :, at : at + sh.slots]
                 low_ref[group * 3 + c, :, at : at + sh.slots] = (
                     kern - head.astype(F32)
                 ).astype(BF16)
@@ -428,10 +438,7 @@
         low_ref = low1_ref if group else low0_ref
         base = max(group - 1, 0) * 3
 
-        def one(
-            c, _, ref=ref, group=group, marks=marks, part=part,
-            near_ref=near_ref, high_ref=high_ref, low_ref=low_ref, base=base,
-        ):
+        for c in range(3):
             spread = scaled_wendland(bf16_dot(marks, near_ref[base + c])) * (1.0 / KERN_SCALE)
             head = spread.astype(BF16)
             rest = (spread - head.astype(F32)).astype(BF16)
@@ -441,9 +448,6 @@
             search = residual * (1.0 / RIDGE_WEIGHT) + spread_dot(part, head, rest)
             search_ref[group * 3 + c] = search
             apply_column(sh, high_ref, low_ref, base + c, search, image_ref)
-            return 0
-
-        lax.fori_loop(0, 3, one, 0)
     residual = rhs_rows(row_ref[0], sh.points)
     search = search_ref[0]
     image = image_ref[...] * (1.0 / KERN_SCALE) + RIDGE_WEIGHT * search
@@ -600,18 +604,25 @@
     def exchange(payload):
         return lax.all_to_all(payload, both, 0, 0)
 
-    own = call(
+    index = jnp.transpose(landmark_index, (1, 2, 0))
+    turned = jnp.transpose(coarse_matrix)
+    tile = jax.ShapeDtypeStruct((8, LANES), F32)
+    own, marks, block = call(
         part(prepare_kernel),
         "prepare",
-        field,
-        [anyw] * 3,
+        (field, tile, tile),
+        [anyw] * 5,
         scratch=[
             pltpu.VMEM(positions.shape, F32),
             pltpu.SMEM(counts.shape, jnp.int32),
             pltpu.VMEM(targets.shape, F32),
-            pltpu.SemaphoreType.DMA((3,)),
+            pltpu.SMEM(index.shape, jnp.int32),
+            pltpu.VMEM(turned.shape, F32),
+            pltpu.VMEM((LANES, turned.shape[0]), F32),
+            pltpu.SemaphoreType.DMA((5,)),
         ],
-    )(positions, counts, targets)
+    )(*(pltpu.with_memory_space_constraint(x, pltpu.HBM)
+        for x in (positions, counts, targets, index, turned)))
     row = jnp.stack([own, swap(own, "gy", 0), swap(own, "gy", 1)])
     even, odd = swap(row, "gx", 0), swap(row, "gx", 1)
 
@@ -632,13 +643,8 @@
         part(terms_kernel),
         "terms",
         jax.ShapeDtypeStruct((sh.devices, 8, LANES), F32),
-        [anyw, anyw, anyw, vmem, vmem, vmem],
-        scratch=[
-            pltpu.SMEM(landmark_index.shape, jnp.int32),
-            pltpu.VMEM(coarse_matrix.shape, F32),
-            pltpu.SemaphoreType.DMA((2,)),
-        ],
-    )(landmark_index, coarse_matrix, near0, row, even, odd)
+        [anyw] + [vmem] * 5,
+    )(near0, marks, block, row, even, odd)
     terms, even, odd = lax.optimization_barrier((exchange(terms), even, odd))
     high1, low1, near1 = build("build_rest", even, odd)
 
@@ -661,7 +667,6 @@
     images = exchange(payload)
 
     line = jax.ShapeDtypeStruct((sh.devices, 1, LANES), F32)
-    tile = jax.ShapeDtypeStruct((8, LANES), F32)
     totals, sums, residual, following, product = call(
         part(second_kernel), "second", (line, tile, field, field, field), [vmem] * 11
     )(images, row, search, spread, rest, gram, image, high0, low0, high1, low1)

time: 81.9 us -> 78 us (0.952)
  local copies, waits for them, and re-layouts: 3.62 us -> 0 us
  Pallas kernels: 28.5 us -> 26.9 us
  waiting for transfers between devices: 0.01 us -> 1.13 us
    unnamed x8 -> x0, local copies, waits for them, and re-layouts: 3.62 us -> none
    pallas_call x2, Pallas kernels: 13.4 us -> 12.1 us  [build(): call(part(build_kernel, len(groups)), name, (kern, kern, near), [vmem] *...]
    ppermute x4, waiting for transfers between devices: 0.01 us -> 1.13 us  [swap(): return lax.ppermute(x, axis, pairs)]
    pallas_call x1, Pallas kernels: 7.47 us -> 6.62 us  [local_fast(): call(part(first_kernel), 'first', (jax.ShapeDtypeStruct((sh.devices, 1, w...]
  transfers between devices with their start and end apart: 4 -> 4, of which waited for: 0 -> 2; matrix products, arithmetic and copies ran while one was open for 2% -> 0% of each run, Pallas kernels for 5% -> 5%
where the time goes in v4:
time: 78 us; the launch traced here: 77.7 us
  blocking collectives  38.9 us (50%)
  Pallas kernels  26.9 us (34%)
  starting transfers between devices  10.1 us (13%)
  waiting for transfers between devices  1.13 us (1%)
    all_to_all x3, blocking collectives, exchange(): return lax.all_to_all(payload, both, 0, 0)  38.9 us
    pallas_call x2, Pallas kernels, build(): call(part(build_kernel, len(groups)), name, (kern, kern, near), [vmem] *...  12.1 us
    ppermute x4, starting transfers between devices, swap(): return lax.ppermute(x, axis, pairs)  10.1 us
    pallas_call x1, Pallas kernels, local_fast(): call(part(first_kernel), 'first', (jax.ShapeDtypeStruct((sh.devices, 1, w...  6.62 us
    pallas_call x1, Pallas kernels, local_fast(): call(part(second_kernel), 'second', (line, tile, field, field, field), [v...  4.71 us
  transfers between devices with their start and end apart: 4, of which 2 were waited for; matrix products, arithmetic and copies ran while one was open for 0% of the time, Pallas kernels for 5%

profile of v4, /device:TPU:0, one launch (start us, length us, event | category | flops | bytes accessed | tf_op | source)
XLA Modules:
  0.0 77.7 jit_solution(5442374361994368247)
XLA Ops:
  0.6 1.1 %prepare.1 = (f32[8,1024]{1,0:T(8,128)S(1)}, f32[8,128]{1,0:T(8,128)S(1)}, f32[8,128]{1,0:T(8,128)S(1)}) custom-call(f32[3,1,1,4,256]{4,3,2,1,0:T(4,128)} %pos_hbm.1, s32[1,1,4]{2,1,0:T(1,128)} %counts_hbm.1, f32[3,1,1,4,256]{4,3,2,1,0:T(4,128)} %tgt_hbm.1, s32[4,4,8]{2,1,0:T(4,128)} %bitcast.8, f32[16,32]{1,0:T(8,128)} %bitcast.9), custom_call_target="tpu_custom_call" | custom-call | flops 1000000 | bytes 100000 | tf_op jit(solution)/shard_map/prepare/pallas_call | solution.py:610
  1.8 0.7 collective-permute-start.1
  2.4 4.4 %collective-permute-start = (f32[8,1024]{1,0:T(8,128)S(1)}, f32[8,1024]{1,0:T(8,128)S(1)}, u32[]{:S(2)}, u32[]{:S(2)}) collective-permute-start(f32[8,1024]{1,0:T(8,128)S(1)} %get-tuple-element.25), channel_id=1, source_target_pairs={{0,1},{1,0},{2,3},{3,2},{4,5},{5,4},{6,7},{7,6},{8,9},{9,8},{10,11... | collective-permute-start | bytes 98312 | tf_op jit(solution)/shard_map/ppermute | solution.py:213
  6.8 0.0 collective-permute-done.1
  6.8 0.9 %collective-permute-done = f32[8,1024]{1,0:T(8,128)S(1)} collective-permute-done((f32[8,1024]{1,0:T(8,128)S(1)}, f32[8,1024]{1,0:T(8,128)S(1)}, u32[]{:S(2)}, u32[]{:S(2)}) %collective-permute-start) | collective-permute-done | bytes 32800 | tf_op jit(solution)/shard_map/ppermute | solution.py:213
  7.7 0.7 collective-permute-start.3
  8.4 4.3 %collective-permute-start.2 = (f32[3,8,1024]{2,1,0:T(8,128)S(1)}, f32[3,8,1024]{2,1,0:T(8,128)S(1)}, u32[]{:S(2)}, u32[]{:S(2)}) collective-permute-start(f32[3,8,1024]{2,1,0:T(8,128)S(1)} %pad_maximum_fusion.row_ref.refs_0_), channel_id=1, source_target_pairs={{0,4},{4,0},{8,12},{12,8},{16,20},{20,16},{24,28},{28,24},{1,5},{5... | collective-permute-start | bytes 294920 | tf_op jit(solution)/shard_map/ppermute | solution.py:213
  12.7 4.0 %build_row.1 = (bf16[3,256,2560]{2,1,0:T(8,128)(2,1)S(1)}, bf16[3,256,2560]{2,1,0:T(8,128)(2,1)S(1)}, bf16[3,48,1024]{2,1,0:T(8,128)(2,1)S(1)}) custom-call(f32[3,8,1024]{2,1,0:T(8,128)S(1)} %pad_maximum_fusion.row_ref.refs_0_, f32[3,8,1024]{2,1,0:T(8,128)S(1)} %pad_maximum_fusion.row_ref.refs_0_), custom_call_target="tpu_custom_call" | custom-call | flops 10000000000 | bytes 100000 | tf_op jit(solution)/shard_map/build_row/pallas_call | solution.py:633
  16.8 0.0 collective-permute-done.3.odd_ref.refs_1_
  16.8 0.3 collective-permute-done.2.even_ref.refs_0_
  17.0 1.3 %terms.1 = f32[32,8,128]{2,1,0:T(8,128)S(1)} custom-call(bf16[3,48,1024]{2,1,0:T(8,128)(2,1)S(1)} %get-tuple-element.26.after_ref.near0_ref, f32[8,128]{1,0:T(8,128)S(1)} %get-tuple-element.27.mark_ref, f32[8,128]{1,0:T(8,128)S(1)} %get-tuple-element.28.block_ref, f32[3,8,1024]{2,1,0:T(8,128)S(1)} %pad_maximum_fusion.row_ref.refs_0_, ...), custom_call_target="tpu_custom_call" | custom-call | flops 1000000 | bytes 100000 | tf_op jit(solution)/shard_map/terms/pallas_call | solution.py:642
  18.4 13.3 %all_to_all.15.recv_ref = f32[32,8,128]{2,1,0:T(8,128)S(1)} all-to-all(f32[32,8,128]{2,1,0:T(8,128)S(1)} %terms.1), channel_id=1, replica_groups=mesh['gx'=8,'gy'=4] {'gx','gy'}, dimensions={0} | all-to-all | bytes 262144 | tf_op jit(solution)/shard_map/all_to_all | solution.py:605
  31.7 8.0 %build_rest.1 = (bf16[6,256,2560]{2,1,0:T(8,128)(2,1)S(1)}, bf16[6,256,2560]{2,1,0:T(8,128)(2,1)S(1)}, bf16[6,48,1024]{2,1,0:T(8,128)(2,1)S(1)}) custom-call(f32[3,8,1024]{2,1,0:T(8,128)S(1)} %pad_maximum_fusion.row_ref.refs_0_, f32[3,8,1024]{2,1,0:T(8,128)S(1)} %collective-permute-done.2.even_ref.refs_0_, ...), custom_call_target="tpu_custom_call" | custom-call | flops 20000000000 | bytes 100000 | tf_op jit(solution)/shard_map/build_rest/pallas_call | solution.py:633
  39.7 6.6 %first.1 = (f32[32,1,3456]{2,1,0:T(1,128)S(1)}, f32[9,8,1024]{2,1,0:T(8,128)S(1)}, bf16[9,48,1024]{2,1,0:T(8,128)(2,1)S(1)}, bf16[9,48,1024]{2,1,0:T(8,128)(2,1)...) custom-call(f32[3,8,1024]{2,1,0:T(8,128)S(1)} %pad_maximum_fusion.row_ref.refs_0_, ...), custom_call_target="tpu_custom_call" | custom-call | flops 1000000 | bytes 100000 | tf_op jit(solution)/shard_map/first/pallas_call | solution.py:653
  46.3 15.9 %all_to_all.16.recv_ref = f32[32,1,3456]{2,1,0:T(1,128)S(1)} all-to-all(f32[32,1,3456]{2,1,0:T(1,128)S(1)} %get-tuple-element.37), channel_id=1, replica_groups=mesh['gx'=8,'gy'=4] {'gx','gy'}, dimensions={0} | all-to-all | bytes 884736 | tf_op jit(solution)/shard_map/all_to_all | solution.py:605
  62.2 4.7 %second.1 = (f32[32,1,128]{2,1,0:T(1,128)S(1)}, f32[8,128]{1,0:T(8,128)S(1)}, f32[8,1024]{1,0:T(8,128)S(1)}, f32[8,1024]{1,0:T(8,128)S(1)}, f32[8,1024]{1,0:T(8,128)S(1)}) custom-call(f32[32,1,3456]{2,1,0:T(1,128)S(1)} %all_to_all.16.recv_ref, f32[3,8,1024]{2,1,0:T(8,128)S(1)} %pad_maximum_fusion.row_ref.refs_0_, ...), custom_call_target="tpu_custom_call" | custom-call | flops 1000000 | bytes 100000 | tf_op jit(solution)/shard_map/second/pallas_call | solution.py:670
  67.0 9.7 %all_to_all.17.recv_ref = f32[32,1,128]{2,1,0:T(1,128)S(1)} all-to-all(f32[32,1,128]{2,1,0:T(1,128)S(1)} %get-tuple-element.43), channel_id=1, replica_groups=mesh['gx'=8,'gy'=4] {'gx','gy'}, dimensions={0} | all-to-all | bytes 32768 | tf_op jit(solution)/shard_map/all_to_all | solution.py:605
  76.6 1.1 %last.1 = (f32[3,1,1,4,256]{4,3,2,1,0:T(4,128)}, f32[3,1,1,4,256]{4,3,2,1,0:T(4,128)}) custom-call(f32[32,1,128]{2,1,0:T(1,128)S(1)} %all_to_all.17.recv_ref, f32[8,128]{1,0:T(8,128)S(1)} %get-tuple-element.44.sums_ref, f32[9,8,1024]{2,1,0:T(8,128)S(1)} %get-tuple-element.38.search_ref, f32[8,1024]{1,0:T(8,128)S(1)} %get-tuple-element.42.image_ref, ...), custom_call_target="tpu_custom_call" | custom-call | flops 1000000 | bytes 100000 | tf_op jit(solution)/shard_map/last/pallas_call | solution.py:676
  (1 shorter events, 0.0 us)
Async XLA Ops:
  1.8 5.1 %collective-permute-start.1 = (f32[8,1024]{1,0:T(8,128)S(1)}, f32[8,1024]{1,0:T(8,128)S(1)}, u32[]{:S(2)}, u32[]{:S(2)}) collective-permute-start(f32[8,1024]{1,0:T(8,128)S(1)} %get-tuple-element.25), channel_id=1, source_target_pairs={{1,2},{2,1},{5,6},{6,5},{9,10},{10,9},{13,14},{14,13},{17,18},{18,... | collective-permute-start | bytes 98312 | tf_op jit(solution)/shard_map/ppermute | solution.py:213
  2.4 5.3 %collective-permute-start = (f32[8,1024]{1,0:T(8,128)S(1)}, f32[8,1024]{1,0:T(8,128)S(1)}, u32[]{:S(2)}, u32[]{:S(2)}) collective-permute-start(f32[8,1024]{1,0:T(8,128)S(1)} %get-tuple-element.25), channel_id=1, source_target_pairs={{0,1},{1,0},{2,3},{3,2},{4,5},{5,4},{6,7},{7,6},{8,9},{9,8},{10,11... | collective-permute-start | bytes 98312 | tf_op jit(solution)/shard_map/ppermute | solution.py:213
  7.7 9.1 %collective-permute-start.3 = (f32[3,8,1024]{2,1,0:T(8,128)S(1)}, f32[3,8,1024]{2,1,0:T(8,128)S(1)}, u32[]{:S(2)}, u32[]{:S(2)}) collective-permute-start(f32[3,8,1024]{2,1,0:T(8,128)S(1)} %pad_maximum_fusion.row_ref.refs_0_), channel_id=1, source_target_pairs={{4,8},{8,4},{12,16},{16,12},{20,24},{24,20},{5,9},{9,5},{13,17},{1... | collective-permute-start | bytes 294920 | tf_op jit(solution)/shard_map/ppermute | solution.py:213
  8.4 8.7 %collective-permute-start.2 = (f32[3,8,1024]{2,1,0:T(8,128)S(1)}, f32[3,8,1024]{2,1,0:T(8,128)S(1)}, u32[]{:S(2)}, u32[]{:S(2)}) collective-permute-start(f32[3,8,1024]{2,1,0:T(8,128)S(1)} %pad_maximum_fusion.row_ref.refs_0_), channel_id=1, source_target_pairs={{0,4},{4,0},{8,12},{12,8},{16,20},{20,16},{24,28},{28,24},{1,5},{5... | collective-permute-start | bytes 294920 | tf_op jit(solution)/shard_map/ppermute | solution.py:213

commit v5 on v4

--- a/solution.py
+++ b/solution.py
@@ -237,6 +237,10 @@
     def window_start(self, i):
         start = jnp.clip(i - 1, 0, self.nx - 3) * self.row_landmarks
         return pl.multiple_of(start, self.row_landmarks)
+
+    def window_of(self, lanes, start):
+        shift = lax.rem(LANES - start, LANES)
+        return pltpu.roll(lanes, shift, axis=1)[:, : self.window]
 
     def near_ids(self, i, j):
         rows = [i, swap_partner(i, self.nx, 0), swap_partner(i, self.nx, 1)]
@@ -314,7 +318,8 @@
 
     sums = tuple(jnp.zeros((8, sh.points), F32) for _ in range(3))
     for ref in (row_ref, even_ref, odd_ref):
-        sums = lax.fori_loop(0, 3, lambda c, s, ref=ref: add_column(ref[c], s), sums)
+        for c in range(3):
+            sums = add_column(ref[c], sums)
     terms = [jnp.sum(s, axis=1, keepdims=True) * (1.0 / KERN_SCALE) for s in sums]
     lane8 = lane_ids(8, LANES)
     row8 = row_ids(LANES)
@@ -333,14 +338,14 @@
         pay_ref[d] = tile
 
 
-def build_kernel(sh, count, row_ref, *refs):
-    group_refs, (high_ref, low_ref, near_ref) = refs[: count], refs[count :]
+def build_kernel(sh, spans, own_ref, *refs):
+    group_refs, (high_ref, low_ref, near_ref) = refs[: len(spans)], refs[len(spans) :]
     centre = sh.centre(lax.axis_index("gx"), lax.axis_index("gy"))
-    own = own_features(row_ref[0], centre).astype(BF16)
-
-    def one(ref, group, c):
+    own = own_features(own_ref[...], centre).astype(BF16)
+
+    def one(ref, c, to):
         features = near_features(ref[c], centre).astype(BF16)
-        near_ref[group * 3 + c] = features
+        near_ref[to] = features
         near = features.T
         for layer, (low, high, offset) in enumerate(sh.blocks):
             lhs = near[layer * sh.slots : (layer + 1) * sh.slots]
@@ -349,15 +354,24 @@
                 kern = scaled_wendland(square)
                 head = kern.astype(BF16)
                 at = offset + (target - low) * sh.slots
-                high_ref[group * 3 + c, :, at : at + sh.slots] = head
-                head = high_ref[group * 3 + c, :, at : at + sh.slots]
-                low_ref[group * 3 + c, :, at : at + sh.slots] = (
+                high_ref[to, :, at : at + sh.slots] = head
+                head = high_ref[to, :, at : at + sh.slots]
+                low_ref[to, :, at : at + sh.slots] = (
                     kern - head.astype(F32)
                 ).astype(BF16)
         return 0
 
-    for group, ref in enumerate(group_refs):
-        lax.fori_loop(0, 3, lambda c, _, ref=ref, group=group: one(ref, group, c), 0)
+    base = 0
+    for ref, (start, stop) in zip(group_refs, spans):
+        shift = base - start
+        lax.fori_loop(start, stop, lambda c, _, ref=ref, shift=shift: one(ref, c, c + shift), 0)
+        base += stop - start
+
+
+def built(refs, group, c):
+    if group:
+        return refs[2], (group - 1) * 3 + c
+    return (refs[1], c - 1) if c else (refs[0], 0)
 
 
 def split_rows(values):
@@ -380,6 +394,12 @@
     head, both = split_rows(part)
     main = bf16_dot(both, high)
     return main[:8] + main[8:] + bf16_dot(head, low)
+
+
+def coarse_dot(terms, gram_ref):
+    gram = gram_ref[...]
+    high = gram.astype(BF16)
+    return spread_dot(terms, high, (gram - high.astype(F32)).astype(BF16))
 
 
 def gathered_matrix(sh, recv_ref, gram_ref):
@@ -411,8 +431,14 @@
 
 
 def first_kernel(
-    sh, row_ref, even_ref, odd_ref, recv_ref, near0_ref, near1_ref,
-    high0_ref, low0_ref, high1_ref, low1_ref,
+    sh, row_ref, even_ref, odd_ref, recv_ref, *refs,
+):
+    near_refs, high_refs, low_refs = refs[0:3], refs[3:6], refs[6:9]
+    first_body(sh, row_ref, even_ref, odd_ref, recv_ref, near_refs, high_refs, low_refs, *refs[9:])
+
+
+def first_body(
+    sh, row_ref, even_ref, odd_ref, recv_ref, near_refs, high_refs, low_refs,
     pay_ref, search_ref, spread_ref, rest_ref, gram_ref, image_ref, mark_ref,
 ):
     i, j = lax.axis_index("gx"), lax.axis_index("gy")
@@ -426,28 +452,27 @@
     gathered = jnp.where(row_ids(LANES) == 6, 1.0, gathered)
     gathered_matrix(sh, recv_ref, gram_ref)
     mark_ref[...] = own_features(gathered, centre).T.astype(BF16)
-    coarse = full_dot(rhs_rows(gathered, LANES), gram_ref[...], transposed=True)
+    coarse = coarse_dot(rhs_rows(gathered, LANES), gram_ref)
     image_ref[...] = jnp.zeros_like(image_ref)
     rows, _ = sh.near_ids(i, j)
+    marks, parts = [], []
+    for near_row in rows:
+        start = sh.window_start(near_row)
+        marks.append(mark_ref[pl.ds(start, sh.window), :])
+        parts.append(sh.window_of(coarse, start))
     for group, ref in enumerate((row_ref, even_ref, odd_ref)):
-        start = sh.window_start(rows[group])
-        marks = mark_ref[pl.ds(start, sh.window), :]
-        part = pltpu.roll(coarse, lax.rem(LANES - start, LANES), axis=1)[:, : sh.window]
-        near_ref = near1_ref if group else near0_ref
-        high_ref = high1_ref if group else high0_ref
-        low_ref = low1_ref if group else low0_ref
-        base = max(group - 1, 0) * 3
-
         for c in range(3):
-            spread = scaled_wendland(bf16_dot(marks, near_ref[base + c])) * (1.0 / KERN_SCALE)
+            near_ref, at = built(near_refs, group, c)
+            high_ref, low_ref = built(high_refs, group, c)[0], built(low_refs, group, c)[0]
+            spread = scaled_wendland(bf16_dot(marks[c], near_ref[at])) * (1.0 / KERN_SCALE)
             head = spread.astype(BF16)
             rest = (spread - head.astype(F32)).astype(BF16)
             spread_ref[group * 3 + c] = head
             rest_ref[group * 3 + c] = rest
             residual = rhs_rows(ref[c], sh.points)
-            search = residual * (1.0 / RIDGE_WEIGHT) + spread_dot(part, head, rest)
+            search = residual * (1.0 / RIDGE_WEIGHT) + spread_dot(parts[c], head, rest)
             search_ref[group * 3 + c] = search
-            apply_column(sh, high_ref, low_ref, base + c, search, image_ref)
+            apply_column(sh, high_ref, low_ref, at, search, image_ref)
     residual = rhs_rows(row_ref[0], sh.points)
     search = search_ref[0]
     image = image_ref[...] * (1.0 / KERN_SCALE) + RIDGE_WEIGHT * search
@@ -462,65 +487,90 @@
     lane = lane_ids(8, LANES)
     fill = jnp.zeros((8, LANES - sh.window), F32)
     tile = jnp.concatenate([window, fill], axis=1)
-    tile = jnp.where(lane == sh.window, gamma, tile)
-    tile = jnp.where(lane == sh.window + 1, delta, tile)
+    tile = jnp.where(lane == 2 * sh.window, gamma, tile)
+    tile = jnp.where(lane == 2 * sh.window + 1, delta, tile)
+    moved = pltpu.roll(tile, sh.window, axis=1)
+    lane1 = lane_ids(1, LANES)
+    pair = jnp.where(
+        jnp.logical_and(lane1 >= sh.window, lane1 < 2 * sh.window), moved[1:2], tile[0:1]
+    )
+    ends = jnp.where(lane1 == 2 * sh.window + 2, gamma[1:2], pair)
+    ends = jnp.where(lane1 == 2 * sh.window + 3, delta[1:2], ends)
+    lines = [ends, tile[2:3]]
     for d in range(sh.devices):
         for q in range(3):
             pay_ref[d, :, q * sh.points : (q + 1) * sh.points] = image[q : q + 1, :]
-            at = 3 * sh.points + q * LANES
-            pay_ref[d, :, at : at + LANES] = tile[q : q + 1, :]
+        for at, line in enumerate(lines):
+            start = 3 * sh.points + at * LANES
+            pay_ref[d, :, start : start + LANES] = line
 
 
 def second_kernel(
+    sh, recv_ref, row_ref, search_ref, spread_ref, rest_ref, gram_ref, image_ref, *refs,
+):
+    second_body(
+        sh, recv_ref, row_ref, search_ref, spread_ref, rest_ref, gram_ref, image_ref,
+        refs[0:3], refs[3:6], *refs[6:],
+    )
+
+
+def second_body(
     sh, recv_ref, row_ref, search_ref, spread_ref, rest_ref, gram_ref, image_ref,
-    high0_ref, low0_ref, high1_ref, low1_ref,
-    pay_ref, sums_ref, residual_ref, next_ref, product_ref,
+    high_refs, low_refs, pay_ref, sums_ref, residual_ref, next_ref, product_ref,
 ):
     i, j = lax.axis_index("gx"), lax.axis_index("gy")
     lane = lane_ids(8, LANES)
+    row8 = row_ids(LANES)
     terms = jnp.zeros((8, LANES), F32)
     scalars = jnp.zeros((8, LANES), F32)
-    fill = jnp.zeros((5, LANES), F32)
     for a in range(sh.nx):
-        parts = []
-        for q in range(3):
-            at = 3 * sh.points + q * LANES
+        lines = []
+        for at in (3 * sh.points, 3 * sh.points + LANES):
             total = recv_ref[a * sh.ny, :, at : at + LANES]
             for b in range(1, sh.ny):
                 total = total + recv_ref[a * sh.ny + b, :, at : at + LANES]
-            parts.append(total)
-        tile = jnp.concatenate(parts + [fill], axis=0)
+            lines.append(total)
+        pair = jnp.broadcast_to(lines[0], (8, LANES))
+        third = jnp.broadcast_to(lines[1], (8, LANES))
+        tile = jnp.where(row8 == 2, third, pair)
         scalars = scalars + tile
         start = min(max(a - 1, 0), sh.nx - 3) * sh.row_landmarks
-        tile = jnp.where(lane < sh.window, tile, 0.0)
-        terms = terms + (pltpu.roll(tile, start, axis=1) if start else tile)
-    gamma = scalars[:, sh.window : sh.window + 1]
-    delta = scalars[:, sh.window + 1 : sh.window + 2]
+        first = pltpu.roll(tile, start, axis=1) if start else tile
+        other = pltpu.roll(tile, (start - sh.window) % LANES, axis=1)
+        inside = jnp.logical_and(lane >= start, lane < start + sh.window)
+        value = jnp.where(row8 == 1, other, first)
+        terms = terms + jnp.where(jnp.logical_and(inside, row8 < 3), value, 0.0)
+    ends = 2 * sh.window
+
+    def column(at):
+        second = scalars[:, ends + 2 + at : ends + 3 + at]
+        value = scalars[:, ends + at : ends + at + 1]
+        return jnp.where(lax.broadcasted_iota(jnp.int32, (8, 1), 0) == 1, second, value)
+
+    gamma, delta = column(0), column(1)
     row1 = lax.broadcasted_iota(jnp.int32, (8, 1), 0)
     alpha = jnp.where(row1 < 3, gamma / jnp.where(row1 < 3, delta, 1.0), 0.0)
-    coarse = full_dot(terms, gram_ref[...], transposed=True)
+    coarse = coarse_dot(terms, gram_ref)
     product_ref[...] = jnp.zeros_like(product_ref)
     rows, cols = sh.near_ids(i, j)
     zeros5 = jnp.zeros((5, sh.points), F32)
+    parts = [sh.window_of(coarse, sh.window_start(near_row)) for near_row in rows]
     for group in range(3):
-        start = sh.window_start(rows[group])
-        part = pltpu.roll(coarse, lax.rem(LANES - start, LANES), axis=1)[:, : sh.window]
-        high_ref = high1_ref if group else high0_ref
-        low_ref = low1_ref if group else low0_ref
-        base = max(group - 1, 0) * 3
         for c in range(3):
             at = group * 3 + c
-            source = rows[group] * sh.ny + cols[c]
+            high_ref, kern_at = built(high_refs, group, c)
+            low_ref = built(low_refs, group, c)[0]
+            source = rows[c] * sh.ny + cols[group]
             image = jnp.concatenate(
                 [recv_ref[source, :, q * sh.points : (q + 1) * sh.points] for q in range(3)]
                 + [zeros5],
                 axis=0,
             )
-            step = image * (1.0 / RIDGE_WEIGHT) + spread_dot(part, spread_ref[at], rest_ref[at])
+            step = image * (1.0 / RIDGE_WEIGHT) + spread_dot(parts[c], spread_ref[at], rest_ref[at])
             search = search_ref[at] - alpha * step
             if at == 0:
                 next_ref[...] = search
-            apply_column(sh, high_ref, low_ref, base + c, search, product_ref)
+            apply_column(sh, high_ref, low_ref, kern_at, search, product_ref)
     residual = rhs_rows(row_ref[0], sh.points)
     image = image_ref[...]
     residual = residual - alpha * image
@@ -623,32 +673,34 @@
         ],
     )(*(pltpu.with_memory_space_constraint(x, pltpu.HBM)
         for x in (positions, counts, targets, index, turned)))
-    row = jnp.stack([own, swap(own, "gy", 0), swap(own, "gy", 1)])
-    even, odd = swap(row, "gx", 0), swap(row, "gx", 1)
-
-    def build(name, *groups):
-        columns = 3 * len(groups)
+    row = jnp.stack([own, swap(own, "gx", 0), swap(own, "gx", 1)])
+
+    def build(name, spans, *groups):
+        columns = sum(stop - start for start, stop in spans)
         kern = jax.ShapeDtypeStruct((columns, sh.slots, sh.pairs), BF16)
         near = jax.ShapeDtypeStruct((columns, 48, sh.points), BF16)
         return call(
-            part(build_kernel, len(groups)),
+            part(build_kernel, spans),
             name,
             (kern, kern, near),
             [vmem] * (1 + len(groups)),
-            cost=len(groups) * 10**10,
-        )(row, *groups)
-
-    high0, low0, near0 = build("build_row", row)
+            cost=columns * 3 * 10**9,
+        )(own, *groups)
+
+    high0, low0, near0 = build("build_own", [(0, 1)], own[None])
+    row, near0 = lax.optimization_barrier((row, near0))
+    even, odd = swap(row, "gy", 0), swap(row, "gy", 1)
+    high1, low1, near1 = build("build_pair", [(1, 3)], row)
     terms = call(
         part(terms_kernel),
         "terms",
         jax.ShapeDtypeStruct((sh.devices, 8, LANES), F32),
         [anyw] + [vmem] * 5,
-    )(near0, marks, block, row, even, odd)
+    )(near1, marks, block, row, even, odd)
     terms, even, odd = lax.optimization_barrier((exchange(terms), even, odd))
-    high1, low1, near1 = build("build_rest", even, odd)
-
-    wide = 3 * sh.points + 3 * LANES
+    high2, low2, near2 = build("build_rest", [(0, 3), (0, 3)], even, odd)
+
+    wide = 3 * sh.points + 2 * LANES
     spread_shape = jax.ShapeDtypeStruct((9, sh.window, sh.points), BF16)
     payload, search, spread, rest, gram, image = call(
         part(first_kernel),
@@ -661,15 +713,15 @@
             jax.ShapeDtypeStruct((sh.landmarks, LANES), F32),
             field,
         ),
-        [vmem] * 10,
+        [vmem] * 13,
         scratch=[pltpu.VMEM((sh.landmarks, 48), BF16)],
-    )(row, even, odd, terms, near0, near1, high0, low0, high1, low1)
+    )(row, even, odd, terms, near0, near1, near2, high0, high1, high2, low0, low1, low2)
     images = exchange(payload)
 
     line = jax.ShapeDtypeStruct((sh.devices, 1, LANES), F32)
     totals, sums, residual, following, product = call(
-        part(second_kernel), "second", (line, tile, field, field, field), [vmem] * 11
-    )(images, row, search, spread, rest, gram, image, high0, low0, high1, low1)
+        part(second_kernel), "second", (line, tile, field, field, field), [vmem] * 13
+    )(images, row, search, spread, rest, gram, image, high0, high1, high2, low0, low1, low2)
     totals = exchange(totals)
 
     out = jax.ShapeDtypeStruct(targets.shape, F32)
@@ -682,6 +734,7 @@
     owned = landmark_index.shape[2]
     return (
         nx * ny * owned == LANES
+        and 6 * ny * owned + 4 <= LANES
         and nx >= 3
         and targets.shape[0] == 3
         and coarse_matrix.shape[0] == 8 * (LANES // 2 // (ny * owned))

time: 78 us -> 75.9 us (0.973)
    pallas_call x2 -> x3, Pallas kernels: 12.1 us -> 12.1 us  [build(): call(part(build_kernel, spans), name, (kern, kern, near), [vmem] * (1 + l...]
  transfers between devices with their start and end apart: 4 -> 4, of which waited for: 2 -> 1; matrix products, arithmetic and copies ran while one was open for 0% -> 0% of each run, Pallas kernels for 5% -> 5%
where the time goes in v5:
time: 75.9 us; the launch traced here: 75.7 us
  blocking collectives  38.2 us (50%)
  Pallas kernels  26.2 us (35%)
  starting transfers between devices  10.1 us (13%)
    all_to_all x3, blocking collectives, exchange(): return lax.all_to_all(payload, both, 0, 0)  38.2 us
    pallas_call x3, Pallas kernels, build(): call(part(build_kernel, spans), name, (kern, kern, near), [vmem] * (1 + l...  12.1 us
    ppermute x4, starting transfers between devices, swap(): return lax.ppermute(x, axis, pairs)  10.1 us
    pallas_call x1, Pallas kernels, local_fast(): call(part(first_kernel), 'first', (jax.ShapeDtypeStruct((sh.devices, 1, w...  6.53 us
    pallas_call x1, Pallas kernels, local_fast(): call(part(second_kernel), 'second', (line, tile, field, field, field), [v...  4.62 us
  transfers between devices with their start and end apart: 4, of which 1 were waited for; matrix products, arithmetic and copies ran while one was open for 0% of the time, Pallas kernels for 5%

profile of v5, /device:TPU:0, one launch (start us, length us, event | category | flops | bytes accessed | tf_op | source)
XLA Modules:
  0.0 75.7 jit_solution(11349652915551452891)
XLA Ops:
  0.6 1.1 %prepare.1 = (f32[8,1024]{1,0:T(8,128)S(1)}, f32[8,128]{1,0:T(8,128)S(1)}, f32[8,128]{1,0:T(8,128)S(1)}) custom-call(f32[3,1,1,4,256]{4,3,2,1,0:T(4,128)} %pos_hbm.1, s32[1,1,4]{2,1,0:T(1,128)} %counts_hbm.1, f32[3,1,1,4,256]{4,3,2,1,0:T(4,128)} %tgt_hbm.1, s32[4,4,8]{2,1,0:T(4,128)} %bitcast.9, f32[16,32]{1,0:T(8,128)} %bitcast.10), custom_call_target="tpu_custom_call" | custom-call | flops 1000000 | bytes 100000 | tf_op jit(solution)/shard_map/prepare/pallas_call | solution.py:660
  1.8 0.7 collective-permute-start.1
  2.4 5.8 %collective-permute-start = (f32[8,1024]{1,0:T(8,128)S(1)}, f32[8,1024]{1,0:T(8,128)S(1)}, u32[]{:S(2)}, u32[]{:S(2)}) collective-permute-start(f32[8,1024]{1,0:T(8,128)S(1)} %get-tuple-element.30.own_ref), channel_id=1, source_target_pairs={{0,4},{4,0},{8,12},{12,8},{16,20},{20,16},{24,28},{28,24},{1,5},{5... | collective-permute-start | bytes 98312 | tf_op jit(solution)/shard_map/ppermute | solution.py:213
  8.3 1.3 %build_own.1 = (bf16[1,256,2560]{2,1,0:T(8,128)(2,1)S(1)}, bf16[1,256,2560]{2,1,0:T(8,128)(2,1)S(1)}, bf16[1,48,1024]{2,1,0:T(8,128)(2,1)S(1)}) custom-call(f32[8,1024]{1,0:T(8,128)S(1)} %get-tuple-element.30.own_ref, f32[1,8,1024]{2,1,0:T(8,128)S(1)} %bitcast.5), custom_call_target="tpu_custom_call" | custom-call | flops 3000000000 | bytes 100000 | tf_op jit(solution)/shard_map/build_own/pallas_call | solution.py:682
  9.6 0.0 collective-permute-done.1
  9.6 0.5 collective-permute-done
  10.2 0.7 collective-permute-start.3
  10.9 2.9 %collective-permute-start.2 = (f32[3,8,1024]{2,1,0:T(8,128)S(1)}, f32[3,8,1024]{2,1,0:T(8,128)S(1)}, u32[]{:S(2)}, u32[]{:S(2)}) collective-permute-start(f32[3,8,1024]{2,1,0:T(8,128)S(1)} %pad_maximum_fusion.refs_0_.row_ref), channel_id=1, source_target_pairs={{0,1},{1,0},{2,3},{3,2},{4,5},{5,4},{6,7},{7,6},{8,9},{9,8},{10,11... | collective-permute-start | bytes 294920 | tf_op jit(solution)/shard_map/ppermute | solution.py:213
  13.8 2.7 %build_pair.1 = (bf16[2,256,2560]{2,1,0:T(8,128)(2,1)S(1)}, bf16[2,256,2560]{2,1,0:T(8,128)(2,1)S(1)}, bf16[2,48,1024]{2,1,0:T(8,128)(2,1)S(1)}) custom-call(f32[8,1024]{1,0:T(8,128)S(1)} %get-tuple-element.30.own_ref, f32[3,8,1024]{2,1,0:T(8,128)S(1)} %pad_maximum_fusion.refs_0_.row_ref), custom_call_target="tpu_custom_call" | custom-call | flops 6000000000 | bytes 100000 | tf_op jit(solution)/shard_map/build_pair/pallas_call | solution.py:682
  16.5 0.0 collective-permute-done.3.odd_ref.refs_1_
  16.5 0.0 collective-permute-done.2.even_ref.refs_0_
  16.5 0.7 terms.1
  17.2 13.0 %all_to_all.15.recv_ref = f32[32,8,128]{2,1,0:T(8,128)S(1)} all-to-all(f32[32,8,128]{2,1,0:T(8,128)S(1)} %terms.1), channel_id=1, replica_groups=mesh['gx'=8,'gy'=4] {'gx','gy'}, dimensions={0} | all-to-all | bytes 262144 | tf_op jit(solution)/shard_map/all_to_all | solution.py:655
  30.2 8.0 %build_rest.1 = (bf16[6,256,2560]{2,1,0:T(8,128)(2,1)S(1)}, bf16[6,256,2560]{2,1,0:T(8,128)(2,1)S(1)}, bf16[6,48,1024]{2,1,0:T(8,128)(2,1)S(1)}) custom-call(f32[8,1024]{1,0:T(8,128)S(1)} %get-tuple-element.30.own_ref, f32[3,8,1024]{2,1,0:T(8,128)S(1)} %collective-permute-done.2.even_ref.refs_0_, f32[3,8,1024]{2,1,0:T(8,128)S(1)} %collective-permute-done.3.odd_ref.refs_1_), custom_call_target="tpu_custom_call" | custom-call | flops 17999998976 | bytes 100000 | tf_op jit(solution)/shard_map/build_rest/pallas_call | solution.py:682
  38.2 6.5 %first.1 = (f32[32,1,3328]{2,1,0:T(1,128)S(1)}, f32[9,8,1024]{2,1,0:T(8,128)S(1)}, bf16[9,48,1024]{2,1,0:T(8,128)(2,1)S(1)}, bf16[9,48,1024]{2,1,0:T(8,128)(2,1)...) custom-call(f32[3,8,1024]{2,1,0:T(8,128)S(1)} %pad_maximum_fusion.refs_0_.row_ref, ...), custom_call_target="tpu_custom_call" | custom-call | flops 1000000 | bytes 100000 | tf_op jit(solution)/shard_map/first/pallas_call | solution.py:705
  44.8 15.6 %all_to_all.16.recv_ref = f32[32,1,3328]{2,1,0:T(1,128)S(1)} all-to-all(f32[32,1,3328]{2,1,0:T(1,128)S(1)} %get-tuple-element.47), channel_id=1, replica_groups=mesh['gx'=8,'gy'=4] {'gx','gy'}, dimensions={0} | all-to-all | bytes 851968 | tf_op jit(solution)/shard_map/all_to_all | solution.py:655
  60.4 4.6 %second.1 = (f32[32,1,128]{2,1,0:T(1,128)S(1)}, f32[8,128]{1,0:T(8,128)S(1)}, f32[8,1024]{1,0:T(8,128)S(1)}, f32[8,1024]{1,0:T(8,128)S(1)}, f32[8,1024]{1,0:T(8,128)S(1)}) custom-call(f32[32,1,3328]{2,1,0:T(1,128)S(1)} %all_to_all.16.recv_ref, f32[3,8,1024]{2,1,0:T(8,128)S(1)} %pad_maximum_fusion.refs_0_.row_ref, ...), custom_call_target="tpu_custom_call" | custom-call | flops 1000000 | bytes 100000 | tf_op jit(solution)/shard_map/second/pallas_call | solution.py:722
  65.0 9.6 %all_to_all.17.recv_ref = f32[32,1,128]{2,1,0:T(1,128)S(1)} all-to-all(f32[32,1,128]{2,1,0:T(1,128)S(1)} %get-tuple-element.53), channel_id=1, replica_groups=mesh['gx'=8,'gy'=4] {'gx','gy'}, dimensions={0} | all-to-all | bytes 32768 | tf_op jit(solution)/shard_map/all_to_all | solution.py:655
  74.6 1.1 %last.1 = (f32[3,1,1,4,256]{4,3,2,1,0:T(4,128)}, f32[3,1,1,4,256]{4,3,2,1,0:T(4,128)}) custom-call(f32[32,1,128]{2,1,0:T(1,128)S(1)} %all_to_all.17.recv_ref, f32[8,128]{1,0:T(8,128)S(1)} %get-tuple-element.54.sums_ref, f32[9,8,1024]{2,1,0:T(8,128)S(1)} %get-tuple-element.48.search_ref, f32[8,1024]{1,0:T(8,128)S(1)} %get-tuple-element.52.image_ref, ...), custom_call_target="tpu_custom_call" | custom-call | flops 1000000 | bytes 100000 | tf_op jit(solution)/shard_map/last/pallas_call | solution.py:728
  (1 shorter events, 0.0 us)
Async XLA Ops:
  1.8 7.9 %collective-permute-start.1 = (f32[8,1024]{1,0:T(8,128)S(1)}, f32[8,1024]{1,0:T(8,128)S(1)}, u32[]{:S(2)}, u32[]{:S(2)}) collective-permute-start(f32[8,1024]{1,0:T(8,128)S(1)} %get-tuple-element.30.own_ref), channel_id=1, source_target_pairs={{4,8},{8,4},{12,16},{16,12},{20,24},{24,20},{5,9},{9,5},{13,17},{1... | collective-permute-start | bytes 98312 | tf_op jit(solution)/shard_map/ppermute | solution.py:213
  2.4 7.7 %collective-permute-start = (f32[8,1024]{1,0:T(8,128)S(1)}, f32[8,1024]{1,0:T(8,128)S(1)}, u32[]{:S(2)}, u32[]{:S(2)}) collective-permute-start(f32[8,1024]{1,0:T(8,128)S(1)} %get-tuple-element.30.own_ref), channel_id=1, source_target_pairs={{0,4},{4,0},{8,12},{12,8},{16,20},{20,16},{24,28},{28,24},{1,5},{5... | collective-permute-start | bytes 98312 | tf_op jit(solution)/shard_map/ppermute | solution.py:213
  10.2 6.3 %collective-permute-start.3 = (f32[3,8,1024]{2,1,0:T(8,128)S(1)}, f32[3,8,1024]{2,1,0:T(8,128)S(1)}, u32[]{:S(2)}, u32[]{:S(2)}) collective-permute-start(f32[3,8,1024]{2,1,0:T(8,128)S(1)} %pad_maximum_fusion.refs_0_.row_ref), channel_id=1, source_target_pairs={{1,2},{2,1},{5,6},{6,5},{9,10},{10,9},{13,14},{14,13},{17,18},{18,... | collective-permute-start | bytes 294920 | tf_op jit(solution)/shard_map/ppermute | solution.py:213
  10.9 5.6 %collective-permute-start.2 = (f32[3,8,1024]{2,1,0:T(8,128)S(1)}, f32[3,8,1024]{2,1,0:T(8,128)S(1)}, u32[]{:S(2)}, u32[]{:S(2)}) collective-permute-start(f32[3,8,1024]{2,1,0:T(8,128)S(1)} %pad_maximum_fusion.refs_0_.row_ref), channel_id=1, source_target_pairs={{0,1},{1,0},{2,3},{3,2},{4,5},{5,4},{6,7},{7,6},{8,9},{9,8},{10,11... | collective-permute-start | bytes 294920 | tf_op jit(solution)/shard_map/ppermute | solution.py:213

commit v6 on v5

--- a/solution.py
+++ b/solution.py
@@ -338,6 +338,18 @@
         pay_ref[d] = tile
 
 
+def build_layer(sh, near, own, layer, high_ref, low_ref, to):
+    low, high, offset = sh.blocks[layer]
+    lhs = near[layer * sh.slots : (layer + 1) * sh.slots]
+    for target in range(low, high):
+        square = bf16_dot(lhs, own[:, target * sh.slots : (target + 1) * sh.slots])
+        kern = scaled_wendland(square)
+        at = slice(offset + (target - low) * sh.slots, offset + (target - low + 1) * sh.slots)
+        high_ref[to, :, at] = kern.astype(BF16)
+        head = high_ref[to, :, at].astype(F32)
+        low_ref[to, :, at] = (kern - head).astype(BF16)
+
+
 def build_kernel(sh, spans, own_ref, *refs):
     group_refs, (high_ref, low_ref, near_ref) = refs[: len(spans)], refs[len(spans) :]
     centre = sh.centre(lax.axis_index("gx"), lax.axis_index("gy"))
@@ -347,24 +359,13 @@
         features = near_features(ref[c], centre).astype(BF16)
         near_ref[to] = features
         near = features.T
-        for layer, (low, high, offset) in enumerate(sh.blocks):
-            lhs = near[layer * sh.slots : (layer + 1) * sh.slots]
-            for target in range(low, high):
-                square = bf16_dot(lhs, own[:, target * sh.slots : (target + 1) * sh.slots])
-                kern = scaled_wendland(square)
-                head = kern.astype(BF16)
-                at = offset + (target - low) * sh.slots
-                high_ref[to, :, at : at + sh.slots] = head
-                head = high_ref[to, :, at : at + sh.slots]
-                low_ref[to, :, at : at + sh.slots] = (
-                    kern - head.astype(F32)
-                ).astype(BF16)
-        return 0
+        for layer in range(sh.layers):
+            build_layer(sh, near, own, layer, high_ref, low_ref, to)
 
     base = 0
     for ref, (start, stop) in zip(group_refs, spans):
-        shift = base - start
-        lax.fori_loop(start, stop, lambda c, _, ref=ref, shift=shift: one(ref, c, c + shift), 0)
+        for c in range(start, stop):
+            one(ref, c, base + c - start)
         base += stop - start
 
 
@@ -380,14 +381,19 @@
     return head, jnp.concatenate([head.astype(F32), tail], axis=0).astype(BF16)
 
 
+def apply_layer(sh, high_ref, low_ref, c, head, both, layer, out_ref):
+    low, high, offset = sh.blocks[layer]
+    at = slice(layer * sh.slots, (layer + 1) * sh.slots)
+    width = (high - low) * sh.slots
+    main = bf16_dot(both[:, at], high_ref[c, :, offset : offset + width])
+    rest = bf16_dot(head[:, at], low_ref[c, :, offset : offset + width])
+    out_ref[:, low * sh.slots : high * sh.slots] += main[:8] + main[8:] + rest
+
+
 def apply_column(sh, high_ref, low_ref, c, values, out_ref):
     head, both = split_rows(values)
-    for layer, (low, high, offset) in enumerate(sh.blocks):
-        at = slice(layer * sh.slots, (layer + 1) * sh.slots)
-        width = (high - low) * sh.slots
-        main = bf16_dot(both[:, at], high_ref[c, :, offset : offset + width])
-        rest = bf16_dot(head[:, at], low_ref[c, :, offset : offset + width])
-        out_ref[:, low * sh.slots : high * sh.slots] += main[:8] + main[8:] + rest
+    for layer in range(sh.layers):
+        apply_layer(sh, high_ref, low_ref, c, head, both, layer, out_ref)
 
 
 def spread_dot(part, high, low):
@@ -431,16 +437,13 @@
 
 
 def first_kernel(
-    sh, row_ref, even_ref, odd_ref, recv_ref, *refs,
+    sh, row_ref, even_ref, odd_ref, recv_ref, near0_ref, near1_ref,
+    high0_ref, high1_ref, low0_ref, low1_ref,
+    pay_ref, search_ref, spread_ref, rest_ref, gram_ref, image_ref, high2_ref, low2_ref,
+    mark_ref,
 ):
-    near_refs, high_refs, low_refs = refs[0:3], refs[3:6], refs[6:9]
-    first_body(sh, row_ref, even_ref, odd_ref, recv_ref, near_refs, high_refs, low_refs, *refs[9:])
-
-
-def first_body(
-    sh, row_ref, even_ref, odd_ref, recv_ref, near_refs, high_refs, low_refs,
-    pay_ref, search_ref, spread_ref, rest_ref, gram_ref, image_ref, mark_ref,
-):
+    high_refs = (high0_ref, high1_ref, high2_ref)
+    low_refs = (low0_ref, low1_ref, low2_ref)
     i, j = lax.axis_index("gx"), lax.axis_index("gy")
     centre = sh.centre(i, j)
     half = LANES // 2
@@ -460,19 +463,43 @@
         start = sh.window_start(near_row)
         marks.append(mark_ref[pl.ds(start, sh.window), :])
         parts.append(sh.window_of(coarse, start))
-    for group, ref in enumerate((row_ref, even_ref, odd_ref)):
-        for c in range(3):
-            near_ref, at = built(near_refs, group, c)
-            high_ref, low_ref = built(high_refs, group, c)[0], built(low_refs, group, c)[0]
-            spread = scaled_wendland(bf16_dot(marks[c], near_ref[at])) * (1.0 / KERN_SCALE)
-            head = spread.astype(BF16)
-            rest = (spread - head.astype(F32)).astype(BF16)
-            spread_ref[group * 3 + c] = head
-            rest_ref[group * 3 + c] = rest
-            residual = rhs_rows(ref[c], sh.points)
-            search = residual * (1.0 / RIDGE_WEIGHT) + spread_dot(parts[c], head, rest)
-            search_ref[group * 3 + c] = search
-            apply_column(sh, high_ref, low_ref, at, search, image_ref)
+    column_refs = (row_ref, even_ref, odd_ref)
+    near_values = {}
+
+    def start_column(at):
+        group, c = divmod(at, 3)
+        near = near_values.pop(at) if group else (near1_ref[c - 1] if c else near0_ref[0])
+        spread = scaled_wendland(bf16_dot(marks[c], near)) * (1.0 / KERN_SCALE)
+        head = spread.astype(BF16)
+        rest = (spread - head.astype(F32)).astype(BF16)
+        spread_ref[at] = head
+        rest_ref[at] = rest
+        residual = rhs_rows(column_refs[group][c], sh.points)
+        search = residual * (1.0 / RIDGE_WEIGHT) + spread_dot(parts[c], head, rest)
+        search_ref[at] = search
+        return at, split_rows(search)
+
+    own_side = own_features(row_ref[0], centre).astype(BF16)
+    waiting = [0, 1, 2]
+    for step in range(6):
+        group, c = divmod(step + 3, 3)
+        features = near_features(column_refs[group][c], centre).astype(BF16)
+        near_values[step + 3] = features
+        near = features.T
+        busy = [start_column(waiting.pop(0)) for _ in range(2 if len(waiting) > 1 else 1)]
+        for layer in range(sh.layers):
+            build_layer(sh, near, own_side, layer, high2_ref, low2_ref, step)
+            for at, (head, both) in busy:
+                high_ref, kern_at = built(high_refs, *divmod(at, 3))
+                low_ref, _ = built(low_refs, *divmod(at, 3))
+                apply_layer(sh, high_ref, low_ref, kern_at, head, both, layer, image_ref)
+        waiting.append(step + 3)
+    for at in waiting:
+        at, (head, both) = start_column(at)
+        high_ref, kern_at = built(high_refs, *divmod(at, 3))
+        low_ref, _ = built(low_refs, *divmod(at, 3))
+        for layer in range(sh.layers):
+            apply_layer(sh, high_ref, low_ref, kern_at, head, both, layer, image_ref)
     residual = rhs_rows(row_ref[0], sh.points)
     search = search_ref[0]
     image = image_ref[...] * (1.0 / KERN_SCALE) + RIDGE_WEIGHT * search
@@ -698,11 +725,10 @@
         [anyw] + [vmem] * 5,
     )(near1, marks, block, row, even, odd)
     terms, even, odd = lax.optimization_barrier((exchange(terms), even, odd))
-    high2, low2, near2 = build("build_rest", [(0, 3), (0, 3)], even, odd)
-
     wide = 3 * sh.points + 2 * LANES
     spread_shape = jax.ShapeDtypeStruct((9, sh.window, sh.points), BF16)
-    payload, search, spread, rest, gram, image = call(
+    kern = jax.ShapeDtypeStruct((6, sh.slots, sh.pairs), BF16)
+    payload, search, spread, rest, gram, image, high2, low2 = call(
         part(first_kernel),
         "first",
         (
@@ -712,10 +738,12 @@
             spread_shape,
             jax.ShapeDtypeStruct((sh.landmarks, LANES), F32),
             field,
+            kern,
+            kern,
         ),
-        [vmem] * 13,
+        [vmem] * 10,
         scratch=[pltpu.VMEM((sh.landmarks, 48), BF16)],
-    )(row, even, odd, terms, near0, near1, near2, high0, high1, high2, low0, low1, low2)
+    )(row, even, odd, terms, near0, near1, high0, high1, low0, low1)
     images = exchange(payload)
 
     line = jax.ShapeDtypeStruct((sh.devices, 1, LANES), F32)

time: 75.9 us -> 72.3 us (0.953)
  Pallas kernels: 26.2 us -> 22.3 us
    pallas_call x3 -> x2, Pallas kernels: 12.1 us -> 3.93 us  [build(): call(part(build_kernel, spans), name, (kern, kern, near), [vmem] * (1 + l...]
    pallas_call x1, Pallas kernels: 6.53 us -> 10.9 us  [local_fast(): call(part(first_kernel), 'first', (jax.ShapeDtypeStruct((sh.devices, 1, w...]
where the time goes in v6:
time: 72.3 us; the launch traced here: 72 us
  blocking collectives  38.3 us (53%)
  Pallas kernels  22.3 us (31%)
  starting transfers between devices  10.1 us (14%)
    all_to_all x3, blocking collectives, exchange(): return lax.all_to_all(payload, both, 0, 0)  38.3 us
    pallas_call x1, Pallas kernels, local_fast(): call(part(first_kernel), 'first', (jax.ShapeDtypeStruct((sh.devices, 1, w...  10.9 us
    ppermute x4, starting transfers between devices, swap(): return lax.ppermute(x, axis, pairs)  10.1 us
    pallas_call x1, Pallas kernels, local_fast(): call(part(second_kernel), 'second', (line, tile, field, field, field), [v...  4.61 us
    pallas_call x2, Pallas kernels, build(): call(part(build_kernel, spans), name, (kern, kern, near), [vmem] * (1 + l...  3.93 us
  transfers between devices with their start and end apart: 4, of which 1 were waited for; matrix products, arithmetic and copies ran while one was open for 0% of the time, Pallas kernels for 5%

profile of v6, /device:TPU:0, one launch (start us, length us, event | category | flops | bytes accessed | tf_op | source)
XLA Modules:
  0.0 72.0 jit_solution(18393282791757856058)
XLA Ops:
  0.6 1.1 %prepare.1 = (f32[8,1024]{1,0:T(8,128)S(1)}, f32[8,128]{1,0:T(8,128)S(1)}, f32[8,128]{1,0:T(8,128)S(1)}) custom-call(f32[3,1,1,4,256]{4,3,2,1,0:T(4,128)} %pos_hbm.1, s32[1,1,4]{2,1,0:T(1,128)} %counts_hbm.1, f32[3,1,1,4,256]{4,3,2,1,0:T(4,128)} %tgt_hbm.1, s32[4,4,8]{2,1,0:T(4,128)} %bitcast.9, f32[16,32]{1,0:T(8,128)} %bitcast.10), custom_call_target="tpu_custom_call" | custom-call | flops 1000000 | bytes 100000 | tf_op jit(solution)/shard_map/prepare/pallas_call | solution.py:687
  1.8 0.7 collective-permute-start.1
  2.4 5.8 %collective-permute-start = (f32[8,1024]{1,0:T(8,128)S(1)}, f32[8,1024]{1,0:T(8,128)S(1)}, u32[]{:S(2)}, u32[]{:S(2)}) collective-permute-start(f32[8,1024]{1,0:T(8,128)S(1)} %get-tuple-element.29.own_ref), channel_id=1, source_target_pairs={{0,4},{4,0},{8,12},{12,8},{16,20},{20,16},{24,28},{28,24},{1,5},{5... | collective-permute-start | bytes 98312 | tf_op jit(solution)/shard_map/ppermute | solution.py:213
  8.3 1.3 %build_own.1 = (bf16[1,256,2560]{2,1,0:T(8,128)(2,1)S(1)}, bf16[1,256,2560]{2,1,0:T(8,128)(2,1)S(1)}, bf16[1,48,1024]{2,1,0:T(8,128)(2,1)S(1)}) custom-call(f32[8,1024]{1,0:T(8,128)S(1)} %get-tuple-element.29.own_ref, f32[1,8,1024]{2,1,0:T(8,128)S(1)} %bitcast.5), custom_call_target="tpu_custom_call" | custom-call | flops 3000000000 | bytes 100000 | tf_op jit(solution)/shard_map/build_own/pallas_call | solution.py:709
  9.6 0.0 collective-permute-done.1
  9.6 0.5 collective-permute-done
  10.2 0.7 collective-permute-start.3
  10.9 2.9 %collective-permute-start.2 = (f32[3,8,1024]{2,1,0:T(8,128)S(1)}, f32[3,8,1024]{2,1,0:T(8,128)S(1)}, u32[]{:S(2)}, u32[]{:S(2)}) collective-permute-start(f32[3,8,1024]{2,1,0:T(8,128)S(1)} %pad_maximum_fusion.refs_0_.row_ref), channel_id=1, source_target_pairs={{0,1},{1,0},{2,3},{3,2},{4,5},{5,4},{6,7},{7,6},{8,9},{9,8},{10,11... | collective-permute-start | bytes 294920 | tf_op jit(solution)/shard_map/ppermute | solution.py:213
  13.8 2.6 %build_pair.1 = (bf16[2,256,2560]{2,1,0:T(8,128)(2,1)S(1)}, bf16[2,256,2560]{2,1,0:T(8,128)(2,1)S(1)}, bf16[2,48,1024]{2,1,0:T(8,128)(2,1)S(1)}) custom-call(f32[8,1024]{1,0:T(8,128)S(1)} %get-tuple-element.29.own_ref, f32[3,8,1024]{2,1,0:T(8,128)S(1)} %pad_maximum_fusion.refs_0_.row_ref), custom_call_target="tpu_custom_call" | custom-call | flops 6000000000 | bytes 100000 | tf_op jit(solution)/shard_map/build_pair/pallas_call | solution.py:709
  16.3 0.0 collective-permute-done.3.odd_ref
  16.4 0.0 collective-permute-done.2.even_ref
  16.4 0.7 terms.1
  17.1 13.1 %all_to_all.15.recv_ref = f32[32,8,128]{2,1,0:T(8,128)S(1)} all-to-all(f32[32,8,128]{2,1,0:T(8,128)S(1)} %terms.1), channel_id=1, replica_groups=mesh['gx'=8,'gy'=4] {'gx','gy'}, dimensions={0} | all-to-all | bytes 262144 | tf_op jit(solution)/shard_map/all_to_all | solution.py:682
  30.2 10.9 %first.1 = (f32[32,1,3328]{2,1,0:T(1,128)S(1)}, f32[9,8,1024]{2,1,0:T(8,128)S(1)}, bf16[9,48,1024]{2,1,0:T(8,128)(2,1)S(1)}, bf16[9,48,1024]{2,1,0:T(8,128)(2,1)...) custom-call(f32[3,8,1024]{2,1,0:T(8,128)S(1)} %pad_maximum_fusion.re, ...), custom_call_target="tpu_custom_call" | custom-call | flops 1000000 | bytes 100000 | tf_op jit(solution)/shard_map/first/pallas_call | solution.py:731
  41.1 15.6 %all_to_all.16.recv_ref = f32[32,1,3328]{2,1,0:T(1,128)S(1)} all-to-all(f32[32,1,3328]{2,1,0:T(1,128)S(1)} %get-tuple-element.43), channel_id=1, replica_groups=mesh['gx'=8,'gy'=4] {'gx','gy'}, dimensions={0} | all-to-all | bytes 851968 | tf_op jit(solution)/shard_map/all_to_all | solution.py:682
  56.7 4.6 %second.1 = (f32[32,1,128]{2,1,0:T(1,128)S(1)}, f32[8,128]{1,0:T(8,128)S(1)}, f32[8,1024]{1,0:T(8,128)S(1)}, f32[8,1024]{1,0:T(8,128)S(1)}, f32[8,1024]{1,0:T(8,128)S(1)}) custom-call(f32[32,1,3328]{2,1,0:T(1,128)S(1)} %all_to_all.16.recv_ref, f32[3,8,1024]{2,1,0:T(8,128)S(1)} %pad_maximum_fusion.refs_0_.row_ref, ...), custom_call_target="tpu_custom_call" | custom-call | flops 1000000 | bytes 100000 | tf_op jit(solution)/shard_map/second/pallas_call | solution.py:750
  61.3 9.6 %all_to_all.17.recv_ref = f32[32,1,128]{2,1,0:T(1,128)S(1)} all-to-all(f32[32,1,128]{2,1,0:T(1,128)S(1)} %get-tuple-element.51), channel_id=1, replica_groups=mesh['gx'=8,'gy'=4] {'gx','gy'}, dimensions={0} | all-to-all | bytes 32768 | tf_op jit(solution)/shard_map/all_to_all | solution.py:682
  70.9 1.1 %last.1 = (f32[3,1,1,4,256]{4,3,2,1,0:T(4,128)}, f32[3,1,1,4,256]{4,3,2,1,0:T(4,128)}) custom-call(f32[32,1,128]{2,1,0:T(1,128)S(1)} %all_to_all.17.recv_ref, f32[8,128]{1,0:T(8,128)S(1)} %get-tuple-element.52.sums_ref, f32[9,8,1024]{2,1,0:T(8,128)S(1)} %get-tuple-element.44.search_ref, f32[8,1024]{1,0:T(8,128)S(1)} %get-tuple-element.48.image_ref, ...), custom_call_target="tpu_custom_call" | custom-call | flops 1000000 | bytes 100000 | tf_op jit(solution)/shard_map/last/pallas_call | solution.py:756
  (1 shorter events, 0.0 us)
Async XLA Ops:
  1.8 7.9 %collective-permute-start.1 = (f32[8,1024]{1,0:T(8,128)S(1)}, f32[8,1024]{1,0:T(8,128)S(1)}, u32[]{:S(2)}, u32[]{:S(2)}) collective-permute-start(f32[8,1024]{1,0:T(8,128)S(1)} %get-tuple-element.29.own_ref), channel_id=1, source_target_pairs={{4,8},{8,4},{12,16},{16,12},{20,24},{24,20},{5,9},{9,5},{13,17},{1... | collective-permute-start | bytes 98312 | tf_op jit(solution)/shard_map/ppermute | solution.py:213
  2.4 7.7 %collective-permute-start = (f32[8,1024]{1,0:T(8,128)S(1)}, f32[8,1024]{1,0:T(8,128)S(1)}, u32[]{:S(2)}, u32[]{:S(2)}) collective-permute-start(f32[8,1024]{1,0:T(8,128)S(1)} %get-tuple-element.29.own_ref), channel_id=1, source_target_pairs={{0,4},{4,0},{8,12},{12,8},{16,20},{20,16},{24,28},{28,24},{1,5},{5... | collective-permute-start | bytes 98312 | tf_op jit(solution)/shard_map/ppermute | solution.py:213
  10.2 6.2 %collective-permute-start.3 = (f32[3,8,1024]{2,1,0:T(8,128)S(1)}, f32[3,8,1024]{2,1,0:T(8,128)S(1)}, u32[]{:S(2)}, u32[]{:S(2)}) collective-permute-start(f32[3,8,1024]{2,1,0:T(8,128)S(1)} %pad_maximum_fusion.refs_0_.row_ref), channel_id=1, source_target_pairs={{1,2},{2,1},{5,6},{6,5},{9,10},{10,9},{13,14},{14,13},{17,18},{18,... | collective-permute-start | bytes 294920 | tf_op jit(solution)/shard_map/ppermute | solution.py:213
  10.9 5.5 %collective-permute-start.2 = (f32[3,8,1024]{2,1,0:T(8,128)S(1)}, f32[3,8,1024]{2,1,0:T(8,128)S(1)}, u32[]{:S(2)}, u32[]{:S(2)}) collective-permute-start(f32[3,8,1024]{2,1,0:T(8,128)S(1)} %pad_maximum_fusion.refs_0_.row_ref), channel_id=1, source_target_pairs={{0,1},{1,0},{2,3},{3,2},{4,5},{5,4},{6,7},{7,6},{8,9},{9,8},{10,11... | collective-permute-start | bytes 294920 | tf_op jit(solution)/shard_map/ppermute | solution.py:213

commit v7 on v6

--- a/solution.py
+++ b/solution.py
@@ -447,24 +447,27 @@
     i, j = lax.axis_index("gx"), lax.axis_index("gy")
     centre = sh.centre(i, j)
     half = LANES // 2
-    totals = [jnp.zeros((8, LANES), F32), jnp.zeros((8, LANES), F32)]
-    for d in range(sh.devices):
-        side = 0 if d * sh.owned < half else 1
-        totals[side] = totals[side] + recv_ref[d]
-    gathered = jnp.where(lane_ids(8, LANES) < half, totals[0], totals[1])
-    gathered = jnp.where(row_ids(LANES) == 6, 1.0, gathered)
-    gathered_matrix(sh, recv_ref, gram_ref)
-    mark_ref[...] = own_features(gathered, centre).T.astype(BF16)
-    coarse = coarse_dot(rhs_rows(gathered, LANES), gram_ref)
     image_ref[...] = jnp.zeros_like(image_ref)
     rows, _ = sh.near_ids(i, j)
-    marks, parts = [], []
-    for near_row in rows:
-        start = sh.window_start(near_row)
-        marks.append(mark_ref[pl.ds(start, sh.window), :])
-        parts.append(sh.window_of(coarse, start))
     column_refs = (row_ref, even_ref, odd_ref)
-    near_values = {}
+    near_values, marks, parts, ready = {}, [], [], {}
+
+    def gather():
+        totals = [jnp.zeros((8, LANES), F32), jnp.zeros((8, LANES), F32)]
+        for d in range(sh.devices):
+            side = 0 if d * sh.owned < half else 1
+            totals[side] = totals[side] + recv_ref[d]
+        gathered = jnp.where(lane_ids(8, LANES) < half, totals[0], totals[1])
+        gathered_matrix(sh, recv_ref, gram_ref)
+        return jnp.where(row_ids(LANES) == 6, 1.0, gathered)
+
+    def solve(gathered):
+        mark_ref[...] = own_features(gathered, centre).T.astype(BF16)
+        coarse = coarse_dot(rhs_rows(gathered, LANES), gram_ref)
+        for near_row in rows:
+            start = sh.window_start(near_row)
+            marks.append(mark_ref[pl.ds(start, sh.window), :])
+            parts.append(sh.window_of(coarse, start))
 
     def start_column(at):
         group, c = divmod(at, 3)
@@ -477,29 +480,34 @@
         residual = rhs_rows(column_refs[group][c], sh.points)
         search = residual * (1.0 / RIDGE_WEIGHT) + spread_dot(parts[c], head, rest)
         search_ref[at] = search
-        return at, split_rows(search)
+        ready[at] = split_rows(search)
+
+    def apply_piece(at, layer):
+        head, both = ready[at]
+        high_ref, kern_at = built(high_refs, *divmod(at, 3))
+        low_ref, _ = built(low_refs, *divmod(at, 3))
+        apply_layer(sh, high_ref, low_ref, kern_at, head, both, layer, image_ref)
 
     own_side = own_features(row_ref[0], centre).astype(BF16)
-    waiting = [0, 1, 2]
+    plan = [[], [0, 1], [2, 3], [4, 5], [6], [7], [8]]
     for step in range(6):
         group, c = divmod(step + 3, 3)
-        features = near_features(column_refs[group][c], centre).astype(BF16)
-        near_values[step + 3] = features
-        near = features.T
-        busy = [start_column(waiting.pop(0)) for _ in range(2 if len(waiting) > 1 else 1)]
+        near_values[step + 3] = near_features(column_refs[group][c], centre).astype(BF16)
+        near = near_values[step + 3].T
+        following = list(plan[step + 1])
         for layer in range(sh.layers):
             build_layer(sh, near, own_side, layer, high2_ref, low2_ref, step)
-            for at, (head, both) in busy:
-                high_ref, kern_at = built(high_refs, *divmod(at, 3))
-                low_ref, _ = built(low_refs, *divmod(at, 3))
-                apply_layer(sh, high_ref, low_ref, kern_at, head, both, layer, image_ref)
-        waiting.append(step + 3)
-    for at in waiting:
-        at, (head, both) = start_column(at)
-        high_ref, kern_at = built(high_refs, *divmod(at, 3))
-        low_ref, _ = built(low_refs, *divmod(at, 3))
+            for at in plan[step]:
+                apply_piece(at, layer)
+            if step == 0 and layer == 0:
+                gathered = gather()
+            if step == 0 and layer == 1:
+                solve(gathered)
+            if layer >= 2 and following:
+                start_column(following.pop(0))
+    for at in plan[6]:
         for layer in range(sh.layers):
-            apply_layer(sh, high_ref, low_ref, kern_at, head, both, layer, image_ref)
+            apply_piece(at, layer)
     residual = rhs_rows(row_ref[0], sh.points)
     search = search_ref[0]
     image = image_ref[...] * (1.0 / KERN_SCALE) + RIDGE_WEIGHT * search

time: 72.3 us -> 71.5 us (0.989)
    pallas_call x1, Pallas kernels: 10.9 us -> 10.2 us  [local_fast(): call(part(first_kernel), 'first', (jax.ShapeDtypeStruct((sh.devices, 1, w...]
  transfers between devices with their start and end apart: 4 -> 4, of which waited for: 1 -> 1; matrix products, arithmetic and copies ran while one was open for 0% -> 0% of each run, Pallas kernels for 5% -> 6%
where the time goes in v7:
time: 71.5 us; the launch traced here: 71.2 us
  blocking collectives  38.3 us (54%)
  Pallas kernels  21.6 us (30%)
  starting transfers between devices  10.1 us (14%)
  between operations  0.72 us (1%)
    all_to_all x3, blocking collectives, exchange(): return lax.all_to_all(payload, both, 0, 0)  38.3 us
    pallas_call x1, Pallas kernels, local_fast(): call(part(first_kernel), 'first', (jax.ShapeDtypeStruct((sh.devices, 1, w...  10.2 us
    ppermute x4, starting transfers between devices, swap(): return lax.ppermute(x, axis, pairs)  10.1 us
    pallas_call x1, Pallas kernels, local_fast(): call(part(second_kernel), 'second', (line, tile, field, field, field), [v...  4.61 us
    pallas_call x2, Pallas kernels, build(): call(part(build_kernel, spans), name, (kern, kern, near), [vmem] * (1 + l...  3.93 us
  transfers between devices with their start and end apart: 4, of which 1 were waited for; matrix products, arithmetic and copies ran while one was open for 0% of the time, Pallas kernels for 6%

profile of v7, /device:TPU:0, one launch (start us, length us, event | category | flops | bytes accessed | tf_op | source)
XLA Modules:
  0.0 71.2 jit_solution(4595093678878664821)
XLA Ops:
  0.6 1.1 %prepare.1 = (f32[8,1024]{1,0:T(8,128)S(1)}, f32[8,128]{1,0:T(8,128)S(1)}, f32[8,128]{1,0:T(8,128)S(1)}) custom-call(f32[3,1,1,4,256]{4,3,2,1,0:T(4,128)} %pos_hbm.1, s32[1,1,4]{2,1,0:T(1,128)} %counts_hbm.1, f32[3,1,1,4,256]{4,3,2,1,0:T(4,128)} %tgt_hbm.1, s32[4,4,8]{2,1,0:T(4,128)} %bitcast.9, f32[16,32]{1,0:T(8,128)} %bitcast.10), custom_call_target="tpu_custom_call" | custom-call | flops 1000000 | bytes 100000 | tf_op jit(solution)/shard_map/prepare/pallas_call | solution.py:695
  1.8 0.7 collective-permute-start.1
  2.4 5.8 %collective-permute-start = (f32[8,1024]{1,0:T(8,128)S(1)}, f32[8,1024]{1,0:T(8,128)S(1)}, u32[]{:S(2)}, u32[]{:S(2)}) collective-permute-start(f32[8,1024]{1,0:T(8,128)S(1)} %get-tuple-element.29.own_ref), channel_id=1, source_target_pairs={{0,4},{4,0},{8,12},{12,8},{16,20},{20,16},{24,28},{28,24},{1,5},{5... | collective-permute-start | bytes 98312 | tf_op jit(solution)/shard_map/ppermute | solution.py:213
  8.3 1.3 %build_own.1 = (bf16[1,256,2560]{2,1,0:T(8,128)(2,1)S(1)}, bf16[1,256,2560]{2,1,0:T(8,128)(2,1)S(1)}, bf16[1,48,1024]{2,1,0:T(8,128)(2,1)S(1)}) custom-call(f32[8,1024]{1,0:T(8,128)S(1)} %get-tuple-element.29.own_ref, f32[1,8,1024]{2,1,0:T(8,128)S(1)} %bitcast.5), custom_call_target="tpu_custom_call" | custom-call | flops 3000000000 | bytes 100000 | tf_op jit(solution)/shard_map/build_own/pallas_call | solution.py:717
  9.6 0.0 collective-permute-done.1
  9.6 0.5 collective-permute-done
  10.2 0.7 collective-permute-start.3
  10.9 2.9 %collective-permute-start.2 = (f32[3,8,1024]{2,1,0:T(8,128)S(1)}, f32[3,8,1024]{2,1,0:T(8,128)S(1)}, u32[]{:S(2)}, u32[]{:S(2)}) collective-permute-start(f32[3,8,1024]{2,1,0:T(8,128)S(1)} %pad_maximum_fusion.refs_0_.row_ref), channel_id=1, source_target_pairs={{0,1},{1,0},{2,3},{3,2},{4,5},{5,4},{6,7},{7,6},{8,9},{9,8},{10,11... | collective-permute-start | bytes 294920 | tf_op jit(solution)/shard_map/ppermute | solution.py:213
  13.8 2.6 %build_pair.1 = (bf16[2,256,2560]{2,1,0:T(8,128)(2,1)S(1)}, bf16[2,256,2560]{2,1,0:T(8,128)(2,1)S(1)}, bf16[2,48,1024]{2,1,0:T(8,128)(2,1)S(1)}) custom-call(f32[8,1024]{1,0:T(8,128)S(1)} %get-tuple-element.29.own_ref, f32[3,8,1024]{2,1,0:T(8,128)S(1)} %pad_maximum_fusion.refs_0_.row_ref), custom_call_target="tpu_custom_call" | custom-call | flops 6000000000 | bytes 100000 | tf_op jit(solution)/shard_map/build_pair/pallas_call | solution.py:717
  16.3 0.0 collective-permute-done.3.odd_ref
  16.4 0.0 collective-permute-done.2.even_ref
  16.4 0.7 terms.1
  17.1 13.1 %all_to_all.15.recv_ref = f32[32,8,128]{2,1,0:T(8,128)S(1)} all-to-all(f32[32,8,128]{2,1,0:T(8,128)S(1)} %terms.1), channel_id=1, replica_groups=mesh['gx'=8,'gy'=4] {'gx','gy'}, dimensions={0} | all-to-all | bytes 262144 | tf_op jit(solution)/shard_map/all_to_all | solution.py:690
  30.2 10.2 %first.1 = (f32[32,1,3328]{2,1,0:T(1,128)S(1)}, f32[9,8,1024]{2,1,0:T(8,128)S(1)}, bf16[9,48,1024]{2,1,0:T(8,128)(2,1)S(1)}, bf16[9,48,1024]{2,1,0:T(8,128)(2,1)...) custom-call(f32[3,8,1024]{2,1,0:T(8,128)S(1)} %pad_maximum_fusion.re, ...), custom_call_target="tpu_custom_call" | custom-call | flops 1000000 | bytes 100000 | tf_op jit(solution)/shard_map/first/pallas_call | solution.py:739
  40.3 15.6 %all_to_all.16.recv_ref = f32[32,1,3328]{2,1,0:T(1,128)S(1)} all-to-all(f32[32,1,3328]{2,1,0:T(1,128)S(1)} %get-tuple-element.43), channel_id=1, replica_groups=mesh['gx'=8,'gy'=4] {'gx','gy'}, dimensions={0} | all-to-all | bytes 851968 | tf_op jit(solution)/shard_map/all_to_all | solution.py:690
  55.9 4.6 %second.1 = (f32[32,1,128]{2,1,0:T(1,128)S(1)}, f32[8,128]{1,0:T(8,128)S(1)}, f32[8,1024]{1,0:T(8,128)S(1)}, f32[8,1024]{1,0:T(8,128)S(1)}, f32[8,1024]{1,0:T(8,128)S(1)}) custom-call(f32[32,1,3328]{2,1,0:T(1,128)S(1)} %all_to_all.16.recv_ref, f32[3,8,1024]{2,1,0:T(8,128)S(1)} %pad_maximum_fusion.refs_0_.row_ref, ...), custom_call_target="tpu_custom_call" | custom-call | flops 1000000 | bytes 100000 | tf_op jit(solution)/shard_map/second/pallas_call | solution.py:758
  60.5 9.6 %all_to_all.17.recv_ref = f32[32,1,128]{2,1,0:T(1,128)S(1)} all-to-all(f32[32,1,128]{2,1,0:T(1,128)S(1)} %get-tuple-element.51), channel_id=1, replica_groups=mesh['gx'=8,'gy'=4] {'gx','gy'}, dimensions={0} | all-to-all | bytes 32768 | tf_op jit(solution)/shard_map/all_to_all | solution.py:690
  70.2 1.1 %last.1 = (f32[3,1,1,4,256]{4,3,2,1,0:T(4,128)}, f32[3,1,1,4,256]{4,3,2,1,0:T(4,128)}) custom-call(f32[32,1,128]{2,1,0:T(1,128)S(1)} %all_to_all.17.recv_ref, f32[8,128]{1,0:T(8,128)S(1)} %get-tuple-element.52.sums_ref, f32[9,8,1024]{2,1,0:T(8,128)S(1)} %get-tuple-element.44.search_ref, f32[8,1024]{1,0:T(8,128)S(1)} %get-tuple-element.48.image_ref, ...), custom_call_target="tpu_custom_call" | custom-call | flops 1000000 | bytes 100000 | tf_op jit(solution)/shard_map/last/pallas_call | solution.py:764
  (1 shorter events, 0.0 us)
Async XLA Ops:
  1.8 7.9 %collective-permute-start.1 = (f32[8,1024]{1,0:T(8,128)S(1)}, f32[8,1024]{1,0:T(8,128)S(1)}, u32[]{:S(2)}, u32[]{:S(2)}) collective-permute-start(f32[8,1024]{1,0:T(8,128)S(1)} %get-tuple-element.29.own_ref), channel_id=1, source_target_pairs={{4,8},{8,4},{12,16},{16,12},{20,24},{24,20},{5,9},{9,5},{13,17},{1... | collective-permute-start | bytes 98312 | tf_op jit(solution)/shard_map/ppermute | solution.py:213
  2.4 7.7 %collective-permute-start = (f32[8,1024]{1,0:T(8,128)S(1)}, f32[8,1024]{1,0:T(8,128)S(1)}, u32[]{:S(2)}, u32[]{:S(2)}) collective-permute-start(f32[8,1024]{1,0:T(8,128)S(1)} %get-tuple-element.29.own_ref), channel_id=1, source_target_pairs={{0,4},{4,0},{8,12},{12,8},{16,20},{20,16},{24,28},{28,24},{1,5},{5... | collective-permute-start | bytes 98312 | tf_op jit(solution)/shard_map/ppermute | solution.py:213
  10.2 6.2 %collective-permute-start.3 = (f32[3,8,1024]{2,1,0:T(8,128)S(1)}, f32[3,8,1024]{2,1,0:T(8,128)S(1)}, u32[]{:S(2)}, u32[]{:S(2)}) collective-permute-start(f32[3,8,1024]{2,1,0:T(8,128)S(1)} %pad_maximum_fusion.refs_0_.row_ref), channel_id=1, source_target_pairs={{1,2},{2,1},{5,6},{6,5},{9,10},{10,9},{13,14},{14,13},{17,18},{18,... | collective-permute-start | bytes 294920 | tf_op jit(solution)/shard_map/ppermute | solution.py:213
  10.9 5.5 %collective-permute-start.2 = (f32[3,8,1024]{2,1,0:T(8,128)S(1)}, f32[3,8,1024]{2,1,0:T(8,128)S(1)}, u32[]{:S(2)}, u32[]{:S(2)}) collective-permute-start(f32[3,8,1024]{2,1,0:T(8,128)S(1)} %pad_maximum_fusion.refs_0_.row_ref), channel_id=1, source_target_pairs={{0,1},{1,0},{2,3},{3,2},{4,5},{5,4},{6,7},{7,6},{8,9},{9,8},{10,11... | collective-permute-start | bytes 294920 | tf_op jit(solution)/shard_map/ppermute | solution.py:213

commit v8 on v7

--- a/solution.py
+++ b/solution.py
@@ -499,15 +499,18 @@
             build_layer(sh, near, own_side, layer, high2_ref, low2_ref, step)
             for at in plan[step]:
                 apply_piece(at, layer)
+            if step == 5:
+                if layer == 0:
+                    start_column(following.pop(0))
+                else:
+                    apply_piece(8, layer - 1)
             if step == 0 and layer == 0:
                 gathered = gather()
             if step == 0 and layer == 1:
                 solve(gathered)
             if layer >= 2 and following:
                 start_column(following.pop(0))
-    for at in plan[6]:
-        for layer in range(sh.layers):
-            apply_piece(at, layer)
+    apply_piece(8, sh.layers - 1)
     residual = rhs_rows(row_ref[0], sh.points)
     search = search_ref[0]
     image = image_ref[...] * (1.0 / KERN_SCALE) + RIDGE_WEIGHT * search

time: 71.5 us -> 71.4 us (level)
  no operation moved by 1% of the time
where the time goes in v8:
time: 71.4 us; the launch traced here: 71.1 us
  blocking collectives  38.3 us (54%)
  Pallas kernels  21.4 us (30%)
  starting transfers between devices  10.1 us (14%)
  between operations  0.72 us (1%)
    all_to_all x3, blocking collectives, exchange(): return lax.all_to_all(payload, both, 0, 0)  38.3 us
    ppermute x4, starting transfers between devices, swap(): return lax.ppermute(x, axis, pairs)  10.1 us
    pallas_call x1, Pallas kernels, local_fast(): call(part(first_kernel), 'first', (jax.ShapeDtypeStruct((sh.devices, 1, w...  10 us
    pallas_call x1, Pallas kernels, local_fast(): call(part(second_kernel), 'second', (line, tile, field, field, field), [v...  4.61 us
    pallas_call x2, Pallas kernels, build(): call(part(build_kernel, spans), name, (kern, kern, near), [vmem] * (1 + l...  3.93 us
  transfers between devices with their start and end apart: 4, of which 1 were waited for; matrix products, arithmetic and copies ran while one was open for 0% of the time, Pallas kernels for 6%

profile of v8, /device:TPU:0, one launch (start us, length us, event | category | flops | bytes accessed | tf_op | source)
XLA Modules:
  0.0 71.1 jit_solution(14975528080911774127)
XLA Ops:
  0.6 1.1 %prepare.1 = (f32[8,1024]{1,0:T(8,128)S(1)}, f32[8,128]{1,0:T(8,128)S(1)}, f32[8,128]{1,0:T(8,128)S(1)}) custom-call(f32[3,1,1,4,256]{4,3,2,1,0:T(4,128)} %pos_hbm.1, s32[1,1,4]{2,1,0:T(1,128)} %counts_hbm.1, f32[3,1,1,4,256]{4,3,2,1,0:T(4,128)} %tgt_hbm.1, s32[4,4,8]{2,1,0:T(4,128)} %bitcast.9, f32[16,32]{1,0:T(8,128)} %bitcast.10), custom_call_target="tpu_custom_call" | custom-call | flops 1000000 | bytes 100000 | tf_op jit(solution)/shard_map/prepare/pallas_call | solution.py:698
  1.8 0.7 collective-permute-start.1
  2.4 5.8 %collective-permute-start = (f32[8,1024]{1,0:T(8,128)S(1)}, f32[8,1024]{1,0:T(8,128)S(1)}, u32[]{:S(2)}, u32[]{:S(2)}) collective-permute-start(f32[8,1024]{1,0:T(8,128)S(1)} %get-tuple-element.29.own_ref), channel_id=1, source_target_pairs={{0,4},{4,0},{8,12},{12,8},{16,20},{20,16},{24,28},{28,24},{1,5},{5... | collective-permute-start | bytes 98312 | tf_op jit(solution)/shard_map/ppermute | solution.py:213
  8.3 1.3 %build_own.1 = (bf16[1,256,2560]{2,1,0:T(8,128)(2,1)S(1)}, bf16[1,256,2560]{2,1,0:T(8,128)(2,1)S(1)}, bf16[1,48,1024]{2,1,0:T(8,128)(2,1)S(1)}) custom-call(f32[8,1024]{1,0:T(8,128)S(1)} %get-tuple-element.29.own_ref, f32[1,8,1024]{2,1,0:T(8,128)S(1)} %bitcast.5), custom_call_target="tpu_custom_call" | custom-call | flops 3000000000 | bytes 100000 | tf_op jit(solution)/shard_map/build_own/pallas_call | solution.py:720
  9.6 0.0 collective-permute-done.1
  9.6 0.5 collective-permute-done
  10.2 0.7 collective-permute-start.3
  10.9 2.9 %collective-permute-start.2 = (f32[3,8,1024]{2,1,0:T(8,128)S(1)}, f32[3,8,1024]{2,1,0:T(8,128)S(1)}, u32[]{:S(2)}, u32[]{:S(2)}) collective-permute-start(f32[3,8,1024]{2,1,0:T(8,128)S(1)} %pad_maximum_fusion.refs_0_.row_ref), channel_id=1, source_target_pairs={{0,1},{1,0},{2,3},{3,2},{4,5},{5,4},{6,7},{7,6},{8,9},{9,8},{10,11... | collective-permute-start | bytes 294920 | tf_op jit(solution)/shard_map/ppermute | solution.py:213
  13.8 2.6 %build_pair.1 = (bf16[2,256,2560]{2,1,0:T(8,128)(2,1)S(1)}, bf16[2,256,2560]{2,1,0:T(8,128)(2,1)S(1)}, bf16[2,48,1024]{2,1,0:T(8,128)(2,1)S(1)}) custom-call(f32[8,1024]{1,0:T(8,128)S(1)} %get-tuple-element.29.own_ref, f32[3,8,1024]{2,1,0:T(8,128)S(1)} %pad_maximum_fusion.refs_0_.row_ref), custom_call_target="tpu_custom_call" | custom-call | flops 6000000000 | bytes 100000 | tf_op jit(solution)/shard_map/build_pair/pallas_call | solution.py:720
  16.3 0.0 collective-permute-done.3.odd_ref
  16.4 0.0 collective-permute-done.2.even_ref
  16.4 0.7 terms.1
  17.1 13.1 %all_to_all.15.recv_ref = f32[32,8,128]{2,1,0:T(8,128)S(1)} all-to-all(f32[32,8,128]{2,1,0:T(8,128)S(1)} %terms.1), channel_id=1, replica_groups=mesh['gx'=8,'gy'=4] {'gx','gy'}, dimensions={0} | all-to-all | bytes 262144 | tf_op jit(solution)/shard_map/all_to_all | solution.py:693
  30.2 10.0 %first.1 = (f32[32,1,3328]{2,1,0:T(1,128)S(1)}, f32[9,8,1024]{2,1,0:T(8,128)S(1)}, bf16[9,48,1024]{2,1,0:T(8,128)(2,1)S(1)}, bf16[9,48,1024]{2,1,0:T(8,128)(2,1)...) custom-call(f32[3,8,1024]{2,1,0:T(8,128)S(1)} %pad_maximum_fusion.re, ...), custom_call_target="tpu_custom_call" | custom-call | flops 1000000 | bytes 100000 | tf_op jit(solution)/shard_map/first/pallas_call | solution.py:742
  40.2 15.6 %all_to_all.16.recv_ref = f32[32,1,3328]{2,1,0:T(1,128)S(1)} all-to-all(f32[32,1,3328]{2,1,0:T(1,128)S(1)} %get-tuple-element.43), channel_id=1, replica_groups=mesh['gx'=8,'gy'=4] {'gx','gy'}, dimensions={0} | all-to-all | bytes 851968 | tf_op jit(solution)/shard_map/all_to_all | solution.py:693
  55.8 4.6 %second.1 = (f32[32,1,128]{2,1,0:T(1,128)S(1)}, f32[8,128]{1,0:T(8,128)S(1)}, f32[8,1024]{1,0:T(8,128)S(1)}, f32[8,1024]{1,0:T(8,128)S(1)}, f32[8,1024]{1,0:T(8,128)S(1)}) custom-call(f32[32,1,3328]{2,1,0:T(1,128)S(1)} %all_to_all.16.recv_ref, f32[3,8,1024]{2,1,0:T(8,128)S(1)} %pad_maximum_fusion.refs_0_.row_ref, ...), custom_call_target="tpu_custom_call" | custom-call | flops 1000000 | bytes 100000 | tf_op jit(solution)/shard_map/second/pallas_call | solution.py:761
  60.4 9.6 %all_to_all.17.recv_ref = f32[32,1,128]{2,1,0:T(1,128)S(1)} all-to-all(f32[32,1,128]{2,1,0:T(1,128)S(1)} %get-tuple-element.51), channel_id=1, replica_groups=mesh['gx'=8,'gy'=4] {'gx','gy'}, dimensions={0} | all-to-all | bytes 32768 | tf_op jit(solution)/shard_map/all_to_all | solution.py:693
  70.0 1.1 %last.1 = (f32[3,1,1,4,256]{4,3,2,1,0:T(4,128)}, f32[3,1,1,4,256]{4,3,2,1,0:T(4,128)}) custom-call(f32[32,1,128]{2,1,0:T(1,128)S(1)} %all_to_all.17.recv_ref, f32[8,128]{1,0:T(8,128)S(1)} %get-tuple-element.52.sums_ref, f32[9,8,1024]{2,1,0:T(8,128)S(1)} %get-tuple-element.44.search_ref, f32[8,1024]{1,0:T(8,128)S(1)} %get-tuple-element.48.image_ref, ...), custom_call_target="tpu_custom_call" | custom-call | flops 1000000 | bytes 100000 | tf_op jit(solution)/shard_map/last/pallas_call | solution.py:767
  (1 shorter events, 0.0 us)
Async XLA Ops:
  1.8 7.9 %collective-permute-start.1 = (f32[8,1024]{1,0:T(8,128)S(1)}, f32[8,1024]{1,0:T(8,128)S(1)}, u32[]{:S(2)}, u32[]{:S(2)}) collective-permute-start(f32[8,1024]{1,0:T(8,128)S(1)} %get-tuple-element.29.own_ref), channel_id=1, source_target_pairs={{4,8},{8,4},{12,16},{16,12},{20,24},{24,20},{5,9},{9,5},{13,17},{1... | collective-permute-start | bytes 98312 | tf_op jit(solution)/shard_map/ppermute | solution.py:213
  2.4 7.7 %collective-permute-start = (f32[8,1024]{1,0:T(8,128)S(1)}, f32[8,1024]{1,0:T(8,128)S(1)}, u32[]{:S(2)}, u32[]{:S(2)}) collective-permute-start(f32[8,1024]{1,0:T(8,128)S(1)} %get-tuple-element.29.own_ref), channel_id=1, source_target_pairs={{0,4},{4,0},{8,12},{12,8},{16,20},{20,16},{24,28},{28,24},{1,5},{5... | collective-permute-start | bytes 98312 | tf_op jit(solution)/shard_map/ppermute | solution.py:213
  10.2 6.2 %collective-permute-start.3 = (f32[3,8,1024]{2,1,0:T(8,128)S(1)}, f32[3,8,1024]{2,1,0:T(8,128)S(1)}, u32[]{:S(2)}, u32[]{:S(2)}) collective-permute-start(f32[3,8,1024]{2,1,0:T(8,128)S(1)} %pad_maximum_fusion.refs_0_.row_ref), channel_id=1, source_target_pairs={{1,2},{2,1},{5,6},{6,5},{9,10},{10,9},{13,14},{14,13},{17,18},{18,... | collective-permute-start | bytes 294920 | tf_op jit(solution)/shard_map/ppermute | solution.py:213
  10.9 5.5 %collective-permute-start.2 = (f32[3,8,1024]{2,1,0:T(8,128)S(1)}, f32[3,8,1024]{2,1,0:T(8,128)S(1)}, u32[]{:S(2)}, u32[]{:S(2)}) collective-permute-start(f32[3,8,1024]{2,1,0:T(8,128)S(1)} %pad_maximum_fusion.refs_0_.row_ref), channel_id=1, source_target_pairs={{0,1},{1,0},{2,3},{3,2},{4,5},{5,4},{6,7},{7,6},{8,9},{9,8},{10,11... | collective-permute-start | bytes 294920 | tf_op jit(solution)/shard_map/ppermute | solution.py:213

commit v9 on v7

--- a/solution.py
+++ b/solution.py
@@ -589,6 +589,7 @@
     product_ref[...] = jnp.zeros_like(product_ref)
     rows, cols = sh.near_ids(i, j)
     zeros5 = jnp.zeros((5, sh.points), F32)
+    pending = []
     parts = [sh.window_of(coarse, sh.window_start(near_row)) for near_row in rows]
     for group in range(3):
         for c in range(3):
@@ -605,7 +606,10 @@
             search = search_ref[at] - alpha * step
             if at == 0:
                 next_ref[...] = search
-            apply_column(sh, high_ref, low_ref, kern_at, search, product_ref)
+            if pending:
+                apply_column(sh, *pending.pop(), product_ref)
+            pending.append((high_ref, low_ref, kern_at, search))
+    apply_column(sh, *pending.pop(), product_ref)
     residual = rhs_rows(row_ref[0], sh.points)
     image = image_ref[...]
     residual = residual - alpha * image

time: 71.5 us -> 70.8 us (level)
  no operation moved by 1% of the time
where the time goes in v9:
time: 70.8 us; the launch traced here: 70.6 us
  blocking collectives  38.3 us (54%)
  Pallas kernels  20.9 us (30%)
  starting transfers between devices  10.1 us (14%)
  between operations  0.72 us (1%)
    all_to_all x3, blocking collectives, exchange(): return lax.all_to_all(payload, both, 0, 0)  38.3 us
    pallas_call x1, Pallas kernels, local_fast(): call(part(first_kernel), 'first', (jax.ShapeDtypeStruct((sh.devices, 1, w...  10.2 us
    ppermute x4, starting transfers between devices, swap(): return lax.ppermute(x, axis, pairs)  10.1 us
    pallas_call x1, Pallas kernels, local_fast(): call(part(second_kernel), 'second', (line, tile, field, field, field), [v...  3.94 us
    pallas_call x2, Pallas kernels, build(): call(part(build_kernel, spans), name, (kern, kern, near), [vmem] * (1 + l...  3.93 us
  transfers between devices with their start and end apart: 4, of which 1 were waited for; matrix products, arithmetic and copies ran while one was open for 0% of the time, Pallas kernels for 6%

profile of v9, /device:TPU:0, one launch (start us, length us, event | category | flops | bytes accessed | tf_op | source)
XLA Modules:
  0.0 70.6 jit_solution(7875374988329291188)
XLA Ops:
  0.6 1.1 %prepare.1 = (f32[8,1024]{1,0:T(8,128)S(1)}, f32[8,128]{1,0:T(8,128)S(1)}, f32[8,128]{1,0:T(8,128)S(1)}) custom-call(f32[3,1,1,4,256]{4,3,2,1,0:T(4,128)} %pos_hbm.1, s32[1,1,4]{2,1,0:T(1,128)} %counts_hbm.1, f32[3,1,1,4,256]{4,3,2,1,0:T(4,128)} %tgt_hbm.1, s32[4,4,8]{2,1,0:T(4,128)} %bitcast.9, f32[16,32]{1,0:T(8,128)} %bitcast.10), custom_call_target="tpu_custom_call" | custom-call | flops 1000000 | bytes 100000 | tf_op jit(solution)/shard_map/prepare/pallas_call | solution.py:699
  1.8 0.7 collective-permute-start.1
  2.4 5.8 %collective-permute-start = (f32[8,1024]{1,0:T(8,128)S(1)}, f32[8,1024]{1,0:T(8,128)S(1)}, u32[]{:S(2)}, u32[]{:S(2)}) collective-permute-start(f32[8,1024]{1,0:T(8,128)S(1)} %get-tuple-element.29.own_ref), channel_id=1, source_target_pairs={{0,4},{4,0},{8,12},{12,8},{16,20},{20,16},{24,28},{28,24},{1,5},{5... | collective-permute-start | bytes 98312 | tf_op jit(solution)/shard_map/ppermute | solution.py:213
  8.3 1.3 %build_own.1 = (bf16[1,256,2560]{2,1,0:T(8,128)(2,1)S(1)}, bf16[1,256,2560]{2,1,0:T(8,128)(2,1)S(1)}, bf16[1,48,1024]{2,1,0:T(8,128)(2,1)S(1)}) custom-call(f32[8,1024]{1,0:T(8,128)S(1)} %get-tuple-element.29.own_ref, f32[1,8,1024]{2,1,0:T(8,128)S(1)} %bitcast.5), custom_call_target="tpu_custom_call" | custom-call | flops 3000000000 | bytes 100000 | tf_op jit(solution)/shard_map/build_own/pallas_call | solution.py:721
  9.6 0.0 collective-permute-done.1
  9.6 0.5 collective-permute-done
  10.2 0.7 collective-permute-start.3
  10.9 2.9 %collective-permute-start.2 = (f32[3,8,1024]{2,1,0:T(8,128)S(1)}, f32[3,8,1024]{2,1,0:T(8,128)S(1)}, u32[]{:S(2)}, u32[]{:S(2)}) collective-permute-start(f32[3,8,1024]{2,1,0:T(8,128)S(1)} %pad_maximum_fusion.refs_0_.row_ref), channel_id=1, source_target_pairs={{0,1},{1,0},{2,3},{3,2},{4,5},{5,4},{6,7},{7,6},{8,9},{9,8},{10,11... | collective-permute-start | bytes 294920 | tf_op jit(solution)/shard_map/ppermute | solution.py:213
  13.8 2.6 %build_pair.1 = (bf16[2,256,2560]{2,1,0:T(8,128)(2,1)S(1)}, bf16[2,256,2560]{2,1,0:T(8,128)(2,1)S(1)}, bf16[2,48,1024]{2,1,0:T(8,128)(2,1)S(1)}) custom-call(f32[8,1024]{1,0:T(8,128)S(1)} %get-tuple-element.29.own_ref, f32[3,8,1024]{2,1,0:T(8,128)S(1)} %pad_maximum_fusion.refs_0_.row_ref), custom_call_target="tpu_custom_call" | custom-call | flops 6000000000 | bytes 100000 | tf_op jit(solution)/shard_map/build_pair/pallas_call | solution.py:721
  16.3 0.0 collective-permute-done.3.odd_ref
  16.4 0.0 collective-permute-done.2.even_ref
  16.4 0.7 terms.1
  17.1 13.1 %all_to_all.15.recv_ref = f32[32,8,128]{2,1,0:T(8,128)S(1)} all-to-all(f32[32,8,128]{2,1,0:T(8,128)S(1)} %terms.1), channel_id=1, replica_groups=mesh['gx'=8,'gy'=4] {'gx','gy'}, dimensions={0} | all-to-all | bytes 262144 | tf_op jit(solution)/shard_map/all_to_all | solution.py:694
  30.2 10.2 %first.1 = (f32[32,1,3328]{2,1,0:T(1,128)S(1)}, f32[9,8,1024]{2,1,0:T(8,128)S(1)}, bf16[9,48,1024]{2,1,0:T(8,128)(2,1)S(1)}, bf16[9,48,1024]{2,1,0:T(8,128)(2,1)...) custom-call(f32[3,8,1024]{2,1,0:T(8,128)S(1)} %pad_maximum_fusion.re, ...), custom_call_target="tpu_custom_call" | custom-call | flops 1000000 | bytes 100000 | tf_op jit(solution)/shard_map/first/pallas_call | solution.py:743
  40.3 15.6 %all_to_all.16.recv_ref = f32[32,1,3328]{2,1,0:T(1,128)S(1)} all-to-all(f32[32,1,3328]{2,1,0:T(1,128)S(1)} %get-tuple-element.43), channel_id=1, replica_groups=mesh['gx'=8,'gy'=4] {'gx','gy'}, dimensions={0} | all-to-all | bytes 851968 | tf_op jit(solution)/shard_map/all_to_all | solution.py:694
  55.9 3.9 %second.1 = (f32[32,1,128]{2,1,0:T(1,128)S(1)}, f32[8,128]{1,0:T(8,128)S(1)}, f32[8,1024]{1,0:T(8,128)S(1)}, f32[8,1024]{1,0:T(8,128)S(1)}, f32[8,1024]{1,0:T(8,128)S(1)}) custom-call(f32[32,1,3328]{2,1,0:T(1,128)S(1)} %all_to_all.16.recv_ref, f32[3,8,1024]{2,1,0:T(8,128)S(1)} %pad_maximum_fusion.refs_0_.row_ref, ...), custom_call_target="tpu_custom_call" | custom-call | flops 1000000 | bytes 100000 | tf_op jit(solution)/shard_map/second/pallas_call | solution.py:762
  59.9 9.6 %all_to_all.17.recv_ref = f32[32,1,128]{2,1,0:T(1,128)S(1)} all-to-all(f32[32,1,128]{2,1,0:T(1,128)S(1)} %get-tuple-element.51), channel_id=1, replica_groups=mesh['gx'=8,'gy'=4] {'gx','gy'}, dimensions={0} | all-to-all | bytes 32768 | tf_op jit(solution)/shard_map/all_to_all | solution.py:694
  69.5 1.1 %last.1 = (f32[3,1,1,4,256]{4,3,2,1,0:T(4,128)}, f32[3,1,1,4,256]{4,3,2,1,0:T(4,128)}) custom-call(f32[32,1,128]{2,1,0:T(1,128)S(1)} %all_to_all.17.recv_ref, f32[8,128]{1,0:T(8,128)S(1)} %get-tuple-element.52.sums_ref, f32[9,8,1024]{2,1,0:T(8,128)S(1)} %get-tuple-element.44.search_ref, f32[8,1024]{1,0:T(8,128)S(1)} %get-tuple-element.48.image_ref, ...), custom_call_target="tpu_custom_call" | custom-call | flops 1000000 | bytes 100000 | tf_op jit(solution)/shard_map/last/pallas_call | solution.py:768
  (1 shorter events, 0.0 us)
Async XLA Ops:
  1.8 7.9 %collective-permute-start.1 = (f32[8,1024]{1,0:T(8,128)S(1)}, f32[8,1024]{1,0:T(8,128)S(1)}, u32[]{:S(2)}, u32[]{:S(2)}) collective-permute-start(f32[8,1024]{1,0:T(8,128)S(1)} %get-tuple-element.29.own_ref), channel_id=1, source_target_pairs={{4,8},{8,4},{12,16},{16,12},{20,24},{24,20},{5,9},{9,5},{13,17},{1... | collective-permute-start | bytes 98312 | tf_op jit(solution)/shard_map/ppermute | solution.py:213
  2.4 7.7 %collective-permute-start = (f32[8,1024]{1,0:T(8,128)S(1)}, f32[8,1024]{1,0:T(8,128)S(1)}, u32[]{:S(2)}, u32[]{:S(2)}) collective-permute-start(f32[8,1024]{1,0:T(8,128)S(1)} %get-tuple-element.29.own_ref), channel_id=1, source_target_pairs={{0,4},{4,0},{8,12},{12,8},{16,20},{20,16},{24,28},{28,24},{1,5},{5... | collective-permute-start | bytes 98312 | tf_op jit(solution)/shard_map/ppermute | solution.py:213
  10.2 6.2 %collective-permute-start.3 = (f32[3,8,1024]{2,1,0:T(8,128)S(1)}, f32[3,8,1024]{2,1,0:T(8,128)S(1)}, u32[]{:S(2)}, u32[]{:S(2)}) collective-permute-start(f32[3,8,1024]{2,1,0:T(8,128)S(1)} %pad_maximum_fusion.refs_0_.row_ref), channel_id=1, source_target_pairs={{1,2},{2,1},{5,6},{6,5},{9,10},{10,9},{13,14},{14,13},{17,18},{18,... | collective-permute-start | bytes 294920 | tf_op jit(solution)/shard_map/ppermute | solution.py:213
  10.9 5.5 %collective-permute-start.2 = (f32[3,8,1024]{2,1,0:T(8,128)S(1)}, f32[3,8,1024]{2,1,0:T(8,128)S(1)}, u32[]{:S(2)}, u32[]{:S(2)}) collective-permute-start(f32[3,8,1024]{2,1,0:T(8,128)S(1)} %pad_maximum_fusion.refs_0_.row_ref), channel_id=1, source_target_pairs={{0,1},{1,0},{2,3},{3,2},{4,5},{5,4},{6,7},{7,6},{8,9},{9,8},{10,11... | collective-permute-start | bytes 294920 | tf_op jit(solution)/shard_map/ppermute | solution.py:213
